TPU v7x, 32 devices: a whole 2x2x4 slice. The times are simulated.
32 devices in a mesh: req: 4 (over z), head: 2 (over core), exp: 4 (over y, x).
Axes of the slice: x: 2, y: 2, z: 4, core: 2. Of those that a mesh axis runs over, the one named last changes fastest.
Arguments:
- queries: bfloat16 [16, 64, 32, 128], P('req', 'exp', 'head'), may hold values from -8 to 8
- new_keys: bfloat16 [16, 64, 4, 128], P('req', 'exp', 'head'), may hold values from -8 to 8
- new_values: bfloat16 [16, 64, 4, 128], P('req', 'exp', 'head'), may hold values from -6 to 6
- key_cache: bfloat16 [16, 24576, 4, 128], P('req', 'exp', 'head'), may hold values from -6 to 6
- value_cache: bfloat16 [16, 24576, 4, 128], P('req', 'exp', 'head'), may hold values from -6 to 6
- lengths: int32 [16], P('req'), may hold values from 1 to 24576, 131072 in all
- residual: bfloat16 [1024, 2048], P(('req', 'exp')), may hold values from -24 to 24
- out_weight: bfloat16 [4096, 2048], P('head', 'exp'), may hold values from -1.796875 to 1.796875
- norm_gain: float32 [2048], replicated, may hold values from 0.1 to 1.9
- route_ids: int32 [1024, 8], P(('req', 'exp')), may hold values from 0 to 15, all different within a row; in each aligned block of 64 rows (0 to 63, 64 to 127, ...) at most 64 rows name the same one
- route_weights: float32 [1024, 8], P(('req', 'exp')), may hold values from 0.05 to 0.3
- expert_in: bfloat16 [16, 2048, 2, 768], P(('req', 'exp'), None, None, 'head'), may hold values from -0.125 to 0.125
- expert_out: bfloat16 [16, 768, 2048], P(('req', 'exp'), 'head'), may hold values from -0.21875 to 0.21875
Outputs:
- output: bfloat16 [1024, 2048], P(('req', 'exp'), 'head')
Inputs may be any that keep to these rules, and one draw needn't show every extreme that they name: `route_ids`: each row names 8 different experts. Among the 64 rows of one device (aligned blocks of rows 0 to 63, 64 to 127 and so on) no expert is named by more than 64 rows.
All inputs are finite; a program needn't handle non-finite values. No bound on the sum of `lengths` on one device may be relied on, other than what follows from the above.
Results may differ from a plain program's by a relative error of at most 0.0051.
Values may be sent and summed in bfloat16 or wider, within the bound.
No kernel may reach another device: no remote copies, remote signals or barrier semaphores. Data moves between devices by JAX's collectives and lax.ppermute only.
A program may use at most 192 MiB of HBM per device.

v0:
```python
import functools
import math
import jax
import jax.numpy as jnp
from jax import lax
from jax.experimental import pallas as pl
from jax.experimental.pallas import tpu as pltpu
from jax.sharding import PartitionSpec as P

masked_score = -1e30
norm_epsilon = 1e-06


def attend_kernel(pieces, sub, tail, factor, exp_count, info_ref, *refs):
    q_refs = refs[:pieces]
    nk_ref, nv_ref, k_ref, v_ref, o_ref = refs[pieces : pieces + 5]
    q_all, q_cat, pattern, m_scr, l_scr, acc, p_even, p_odd, stats, turned = refs[pieces + 5 :]
    requests = pl.num_programs(0)
    request = pl.program_id(0)
    head_size = k_ref.shape[2]
    kv = 2
    piece_rows, heads = q_refs[0].shape[1], q_refs[0].shape[2]
    group = heads // kv
    rows = piece_rows * pieces
    lanes = rows * group
    length = info_ref[request]
    even_lane = lax.broadcasted_iota(jnp.int32, (lanes, 128), 1) % 2 == 0

    @pl.when(request == 0)
    def _():
        stats[...] = jnp.zeros_like(stats)
        parity = lax.broadcasted_iota(jnp.int32, (16, head_size), 0) % 2
        pattern[0] = (1 - parity).astype(jnp.float32).astype(jnp.bfloat16)
        pattern[1] = parity.astype(jnp.float32).astype(jnp.bfloat16)

    for piece in range(pieces):
        where_to = info_ref[requests + piece] * piece_rows
        q_all[pl.ds(where_to, piece_rows)] = q_refs[piece][0].astype(jnp.float32)
    for head in range(kv):
        chosen = q_all[:, head * group : (head + 1) * group, :].reshape(lanes, head_size)
        q_cat[:, head * head_size : (head + 1) * head_size] = chosen.astype(jnp.bfloat16)

    def spread(block):
        if block.shape[0] < 16:
            left = block * pattern[0, : block.shape[0]]
            right = block * pattern[1, : block.shape[0]]
        else:
            tiles = block.reshape(block.shape[0] // 16, 16, head_size)
            left = (tiles * pattern[0][None]).reshape(block.shape)
            right = (tiles * pattern[1][None]).reshape(block.shape)
        return jnp.concatenate([left, right], axis=1)

    def score(block):
        return lax.dot_general(
            q_cat[...],
            spread(block),
            (((1,), (1,)), ((), ())),
            preferred_element_type=jnp.float32,
        )

    def both_columns(even, odd):
        shape = (lanes, 128)
        return jnp.where(even_lane, jnp.broadcast_to(even, shape), jnp.broadcast_to(odd, shape))

    def reduce_parity(wide, op, neutral):
        even = op(jnp.where(even_lane, wide, neutral), axis=1, keepdims=True)
        odd = op(jnp.where(even_lane, neutral, wide), axis=1, keepdims=True)
        return even, odd

    def init():
        scores = score(nk_ref[0]) * factor
        fresh = scores.shape[1]
        even = lax.broadcasted_iota(jnp.int32, scores.shape, 1) % 2 == 0
        top_even = jnp.max(jnp.where(even, scores, -jnp.inf), axis=1, keepdims=True)
        top_odd = jnp.max(jnp.where(even, -jnp.inf, scores), axis=1, keepdims=True)
        top_even = top_even.astype(jnp.bfloat16).astype(jnp.float32)
        top_odd = top_odd.astype(jnp.bfloat16).astype(jnp.float32)
        m_scr[...] = both_columns(top_even, top_odd)
        probs = jnp.exp2(
            scores
            - jnp.where(
                even,
                jnp.broadcast_to(top_even, scores.shape),
                jnp.broadcast_to(top_odd, scores.shape),
            )
        )
        l_even = jnp.sum(jnp.where(even, probs, 0.0), axis=1, keepdims=True)
        l_odd = jnp.sum(jnp.where(even, 0.0, probs), axis=1, keepdims=True)
        lane = lax.broadcasted_iota(jnp.int32, (lanes, 128), 1)
        l_scr[...] = jnp.where(lane < 2, both_columns(l_even, l_odd), 0.0)
        acc[...] = jnp.dot(
            probs.astype(jnp.bfloat16), spread(nv_ref[0]), preferred_element_type=jnp.float32
        )

    def piece_of(ref, start, size):
        return ref[0, pl.ds(pl.multiple_of(start * kv, kv * tail), size * kv), :]

    step = 256

    def soften(start, size, target, masked):
        top = m_scr[...]
        total = l_scr[...]
        for tile in range(size * kv // step):
            scores = score(piece_of_tile(k_ref, start, tile))
            for part in range(step // 128):
                piece = scores[:, part * 128 : (part + 1) * 128]
                probs = jnp.exp2(piece * factor - top)
                if masked:
                    lane = lax.broadcasted_iota(jnp.int32, (1, 128), 1)
                    position = start + (tile * step + part * 128 + lane) // kv
                    probs = jnp.where(position < length, probs, 0.0)
                total = total + probs
                at = tile * step + part * 128
                target[:, at : at + 128] = probs.astype(jnp.bfloat16)
        l_scr[...] = total

    def piece_of_tile(ref, start, tile):
        first = pl.multiple_of(start * kv, kv * tail) + tile * step
        return ref[0, pl.ds(first, step), :]

    def weigh(start, size, source):
        values = spread(piece_of(v_ref, start, size))
        acc[...] += jnp.dot(source[:, : size * kv], values, preferred_element_type=jnp.float32)

    init()
    here = length
    pairs = here // (2 * sub)

    def loop(i, carry):
        start = pl.multiple_of(i * 2 * sub, 2 * sub)
        before = jnp.maximum(start - sub, 0)
        soften(start, sub, p_even, False)
        weigh(before, sub, p_odd)
        soften(start + sub, sub, p_odd, False)
        weigh(start, sub, p_even)
        return carry

    p_odd[...] = jnp.zeros_like(p_odd)
    lax.fori_loop(0, pairs, loop, 0)
    weigh(pl.multiple_of(jnp.maximum(pairs * 2 * sub - sub, 0), sub), sub, p_odd)

    def tail_loop(i, carry):
        start = pl.multiple_of(pairs * 2 * sub + i * tail, tail)
        soften(start, tail, p_even, True)
        weigh(start, tail, p_even)
        return carry

    lax.fori_loop(0, (here - pairs * 2 * sub + tail - 1) // tail, tail_loop, 0)
    largest = jnp.max(l_scr[...])

    @pl.when(jnp.logical_not(largest < 1e30))
    def _():
        init()

        def slow_loop(i, carry):
            start = pl.multiple_of(i * tail, tail)
            scores = score(piece_of(k_ref, start, tail)) * factor
            lane = lax.broadcasted_iota(jnp.int32, (1, tail * kv), 1)
            inside = start + lane // kv < length
            scores = jnp.where(inside, scores, masked_score)
            wide = m_scr[...]
            for part in range(tail * kv // 128):
                wide = jnp.maximum(wide, scores[:, part * 128 : (part + 1) * 128])
            even, odd = reduce_parity(wide, jnp.max, -jnp.inf)
            even = even.astype(jnp.bfloat16).astype(jnp.float32)
            odd = odd.astype(jnp.bfloat16).astype(jnp.float32)
            top = both_columns(even, odd)
            fade = jnp.exp2(m_scr[...] - top)
            total = l_scr[...] * fade
            for part in range(tail * kv // 128):
                at = part * 128
                probs = jnp.where(
                    inside[:, at : at + 128], jnp.exp2(scores[:, at : at + 128] - top), 0.0
                )
                total = total + probs
                p_even[:, at : at + 128] = probs.astype(jnp.bfloat16)
            l_scr[...] = total
            m_scr[...] = top
            for head in range(kv):
                columns = slice(head * head_size, (head + 1) * head_size)
                acc[:, columns] = acc[:, columns] * jnp.broadcast_to(
                    fade[:, head : head + 1], (lanes, head_size)
                )
            weigh(start, tail, p_even)
            return carry

        lax.fori_loop(0, (here + tail - 1) // tail, slow_loop, 0)

    share = heads // exp_count
    totals = reduce_parity(l_scr[...], jnp.sum, 0.0)
    lane = lax.broadcasted_iota(jnp.int32, (lanes, head_size), 1)
    member_of_row = lax.broadcasted_iota(jnp.int32, (lanes, head_size), 0) % group
    for head in range(kv):
        total = totals[head]
        inverse = jnp.broadcast_to(1.0 / total, (lanes, head_size))
        columns = slice(head * head_size, (head + 1) * head_size)
        turned[...] = acc[:, columns] * inverse
        upper = total.astype(jnp.bfloat16).astype(jnp.float32)
        kinds = [upper, m_scr[:, head : head + 1], total - upper]
        placed = jnp.zeros((lanes, head_size), jnp.float32)
        for kind, column in enumerate(kinds):
            placed = jnp.where(
                lane == member_of_row + 8 * kind,
                jnp.broadcast_to(column, placed.shape),
                placed,
            )
        gathered = jnp.sum(placed.reshape(rows, group, head_size), axis=1)
        stats[head] = stats[head] + pltpu.roll(gathered, 24 * request, 1)
        for member in range(group):
            index = head * group + member
            target, inside = index // share, index % share
            offset = pl.multiple_of(
                request * (share * head_size) + inside * head_size, head_size
            )
            o_ref[target, :, pl.ds(offset, head_size)] = turned[
                pl.ds(member, rows, stride=group), :
            ].astype(jnp.bfloat16)

    @pl.when(request == requests - 1)
    def _():
        for target in range(exp_count):
            head = target * share // group
            o_ref[target, :, requests * share * head_size :] = stats[head].astype(jnp.bfloat16)


def attend(queries, order, new_keys, new_values, keys, values, local_lengths, sub, tail, exp_count):
    requests, span, kv, head_size = keys.shape
    piece_rows, heads = queries[0].shape[1:3]
    pieces = len(queries)
    rows = piece_rows * pieces
    share = heads // exp_count
    fresh = new_keys.shape[1]
    width = requests * share * head_size + 128
    info = jnp.concatenate([local_lengths, order])
    factor = head_size ** (-0.5) * math.log2(math.e)
    lanes = rows * heads // kv
    flat = lambda x: x.reshape(requests, x.shape[1] * kv, head_size)
    block = lambda n: pl.BlockSpec((1, n, head_size), lambda r, info: (r, 0, 0))
    return pl.pallas_call(
        functools.partial(attend_kernel, pieces, sub, tail, factor, exp_count),
        grid_spec=pltpu.PrefetchScalarGridSpec(
            num_scalar_prefetch=1,
            grid=(requests,),
            in_specs=[
                pl.BlockSpec((1, piece_rows, heads, head_size), lambda r, info: (r, 0, 0, 0))
            ]
            * pieces
            + [block(fresh * kv), block(fresh * kv), block(span * kv), block(span * kv)],
            out_specs=pl.BlockSpec((exp_count, rows, width), lambda r, info: (0, 0, 0)),
            scratch_shapes=[
                pltpu.VMEM((rows, heads, head_size), jnp.float32),
                pltpu.VMEM((lanes, kv * head_size), jnp.bfloat16),
                pltpu.VMEM((2, 16, head_size), jnp.bfloat16),
                pltpu.VMEM((lanes, 128), jnp.float32),
                pltpu.VMEM((lanes, 128), jnp.float32),
                pltpu.VMEM((lanes, kv * head_size), jnp.float32),
                pltpu.VMEM((lanes, 2 * sub * kv), jnp.bfloat16),
                pltpu.VMEM((lanes, sub * kv), jnp.bfloat16),
                pltpu.VMEM((kv, rows, head_size), jnp.float32),
                pltpu.VMEM((lanes, head_size), jnp.float32),
            ],
        ),
        out_shape=jax.ShapeDtypeStruct((exp_count, rows, width), jnp.bfloat16),
        compiler_params=pltpu.CompilerParams(dimension_semantics=("arbitrary",)),
        name="attend",
    )(info, *queries, flat(new_keys), flat(new_values), flat(keys), flat(values))


def merge_kernel(parts, share, info_ref, *refs):
    x_refs = refs[:parts]
    w_refs = refs[parts : 2 * parts]
    keep_ref, send_ref, attn = refs[2 * parts :]
    rows, width = x_refs[0].shape
    head_size = 128
    requests = (width - head_size) // (share * head_size)
    group_shift = info_ref[0]
    half = info_ref[1]
    tables = []
    for x_ref in x_refs:
        table = x_ref[:, width - head_size :].astype(jnp.float32)
        tables.append(pltpu.roll(table, group_shift, 1))
    for request in range(requests):
        for member in range(share):
            at = 24 * request + member
            tops = [t[:, at + 8 : at + 9] for t in tables]
            sums = [t[:, at : at + 1] + t[:, at + 16 : at + 17] for t in tables]
            top = functools.reduce(jnp.maximum, tops)
            weights = [s * jnp.exp2(m - top) for s, m in zip(sums, tops)]
            inverse = 1.0 / functools.reduce(jnp.add, weights)
            start = (request * share + member) * head_size
            mixed = jnp.zeros((rows, head_size), jnp.float32)
            for weight, x_ref in zip(weights, x_refs):
                part = x_ref[:, start : start + head_size].astype(jnp.float32)
                mixed = mixed + jnp.broadcast_to(weight * inverse, part.shape) * part
            attn[
                request * rows : (request + 1) * rows, member * head_size : (member + 1) * head_size
            ] = mixed.astype(jnp.bfloat16)
    columns = w_refs[0].shape[1]
    per_half = keep_ref.shape[1] // columns
    for part in range(parts):
        made = jnp.dot(attn[...], w_refs[part][...], preferred_element_type=jnp.float32)
        chunk = info_ref[2 + part]
        inside = pl.multiple_of((chunk % per_half) * columns, columns)

        @pl.when(chunk // per_half == half)
        def _():
            keep_ref[:, pl.ds(inside, columns)] = made

        @pl.when(chunk // per_half != half)
        def _():
            send_ref[:, pl.ds(inside, columns)] = made.astype(jnp.bfloat16)


def merge_project(messages, weights, info, share, requests):
    rows, width = messages[0].shape
    columns = weights[0].shape[1]
    parts = len(messages)
    half_width = parts * columns // 2
    shape = (requests * rows, half_width)
    return pl.pallas_call(
        functools.partial(merge_kernel, parts, share),
        in_specs=[pl.BlockSpec(memory_space=pltpu.SMEM)]
        + [pl.BlockSpec(memory_space=pltpu.VMEM)] * (2 * parts),
        out_specs=[pl.BlockSpec(memory_space=pltpu.VMEM)] * 2,
        out_shape=[
            jax.ShapeDtypeStruct(shape, jnp.float32),
            jax.ShapeDtypeStruct(shape, jnp.bfloat16),
        ],
        scratch_shapes=[pltpu.VMEM((requests * rows, share * head_size_of(weights, share)), jnp.bfloat16)],
        name="merge_project",
    )(info, *messages, *weights)


def head_size_of(weights, share):
    return weights[0].shape[0] // share


def shift(value, axis, step):
    size = lax.axis_size(axis)
    return lax.ppermute(value, axis, [(i, (i + step) % size) for i in range(size)])


def take_block(value, index):
    return lax.dynamic_index_in_dim(value, index, 0, keepdims=False)


def gather_blocks(block, axis):
    return [block] + [shift(block, axis, s) for s in range(1, lax.axis_size(axis))]


def route_table(route_ids, route_weights):
    req_size, exp_size = lax.axis_size("req"), lax.axis_size("exp")
    req_at, exp_at = lax.axis_index("req"), lax.axis_index("exp")
    groups = req_size * exp_size
    table = jnp.sum(
        jnp.where(
            route_ids[None, :, :] == lax.iota(jnp.int32, groups)[:, None, None],
            route_weights[None, :, :],
            0.0,
        ),
        axis=2,
    )
    mine = lax.all_to_all(table, ("req", "exp"), split_axis=0, concat_axis=0, tiled=True)
    by_req = (req_at - lax.iota(jnp.int32, req_size)) % req_size
    by_exp = (exp_at - lax.iota(jnp.int32, exp_size)) % exp_size
    order = by_req[None, :] * exp_size + by_exp[:, None]
    return jnp.take(mine, order.reshape(-1), axis=0).reshape(exp_size, -1)


def halves(value, width, axis):
    head_at = lax.axis_index("head")
    own = lax.dynamic_slice_in_dim(value, head_at * width, width, axis)
    other = lax.dynamic_slice_in_dim(value, (1 - head_at) * width, width, axis)
    return own, other


def dense_experts(half_hidden, row_weights, gains, maps_in, maps_out):
    row_count, half_width = half_hidden.shape
    req_size, exp_size = lax.axis_size("req"), lax.axis_size("exp")
    sent = half_hidden.astype(jnp.bfloat16)
    column = jnp.concatenate(gather_blocks(sent, "req"), axis=0)
    blocks = gather_blocks(column, "exp")
    back = []
    for s, own in enumerate(blocks):
        other = shift(own, "head", 1)
        wide = [own.astype(jnp.float32), other.astype(jnp.float32)]
        squares = sum(jnp.sum(x * x, axis=-1, keepdims=True) for x in wide)
        factor = lax.rsqrt(squares / (2 * half_width) + norm_epsilon)
        gate_up = sum(
            jnp.dot(
                (x * factor * gain).astype(jnp.bfloat16), maps, preferred_element_type=jnp.float32
            )
            for x, gain, maps in zip(wide, gains, maps_in)
        )
        half_units = gate_up.shape[-1] // 2
        activated = (
            jax.nn.silu(gate_up[:, :half_units])
            * gate_up[:, half_units:]
        ).astype(jnp.bfloat16)
        weight = row_weights[s][:, None]
        kept, passed = [
            jnp.dot(activated, maps, preferred_element_type=jnp.float32) * weight
            for maps in maps_out
        ]
        swapped = shift(passed.astype(jnp.bfloat16), "head", 1).astype(jnp.float32)
        back.append(kept + swapped)
    plane_sum = back[0]
    for s in range(1, exp_size):
        plane_sum = plane_sum + shift(back[s].astype(jnp.bfloat16), "exp", -s).astype(jnp.float32)
    plane_sum = plane_sum.reshape(req_size, row_count, half_width)
    mixture = plane_sum[0]
    outgoing = plane_sum.astype(jnp.bfloat16)
    for s in range(1, req_size):
        mixture = mixture + shift(outgoing[s], "req", -s).astype(jnp.float32)
    return mixture


def sparse_experts(half_hidden, route_ids, route_weights, norm_gain, expert_in, expert_out, capacity):
    row_count, half_width = half_hidden.shape
    head_at = lax.axis_index("head")
    other = shift(half_hidden, "head", 1)
    first = jnp.where(head_at == 0, half_hidden, other)
    second = jnp.where(head_at == 0, other, half_hidden)
    hidden = jnp.concatenate([first, second], axis=1)
    normed = (
        hidden
        * lax.rsqrt(jnp.mean(hidden * hidden, axis=-1, keepdims=True) + norm_epsilon)
        * norm_gain
    ).astype(jnp.bfloat16)
    model_width = 2 * half_width
    local_experts = expert_in.shape[0]
    groups = lax.axis_size("req") * lax.axis_size("exp")
    experts_all = local_experts * groups
    expert_iota = lax.iota(jnp.int32, experts_all)
    named_count = jnp.sum((route_ids[:, :, None] == expert_iota).astype(jnp.int32), axis=1)
    earlier = jnp.cumsum(named_count, axis=0) - named_count
    slot_rank = jnp.take_along_axis(earlier, route_ids, axis=1)
    slot_index = route_ids * capacity + slot_rank
    slot_iota = lax.iota(jnp.int32, experts_all * capacity)
    placing = jnp.any(slot_index[None, :, :] == slot_iota[:, None, None], axis=2).astype(
        jnp.bfloat16
    )
    outgoing = jnp.dot(placing, normed, preferred_element_type=jnp.float32).astype(jnp.bfloat16)
    outgoing = outgoing.reshape(groups, local_experts, capacity, model_width)
    input_maps = expert_in.reshape(local_experts, model_width, -1)
    gate_up = jnp.einsum(
        "geci,eif->gecf",
        lax.all_to_all(outgoing, ("req", "exp"), split_axis=0, concat_axis=0, tiled=True),
        input_maps,
        preferred_element_type=jnp.float32,
    )
    half_units = gate_up.shape[-1] // 2
    activated = (jax.nn.silu(gate_up[..., :half_units]) * gate_up[..., half_units:]).astype(
        jnp.bfloat16
    )
    partial_value = jnp.einsum(
        "gecf,efi->geci", activated, expert_out, preferred_element_type=jnp.float32
    )
    summed = lax.psum_scatter(partial_value, "head", scatter_dimension=3, tiled=True).astype(
        jnp.bfloat16
    )
    returned = lax.all_to_all(summed, ("req", "exp"), split_axis=0, concat_axis=0, tiled=True)
    flat_results = returned.reshape(experts_all * capacity, half_width)
    picked = jnp.take(flat_results, slot_index, axis=0).astype(jnp.float32)
    return jnp.sum(picked * route_weights[:, :, None], axis=1)


def local(
    queries,
    new_keys,
    new_values,
    key_cache,
    value_cache,
    lengths,
    residual,
    out_weight,
    norm_gain,
    route_ids,
    route_weights,
    expert_in,
    expert_out,
):
    requests, span, kv, head_size = key_cache.shape
    heads = queries.shape[2]
    exp_size = lax.axis_size("exp")
    exp_at, head_at = lax.axis_index("exp"), lax.axis_index("head")
    share = heads // exp_size
    group = heads // kv
    sources = (exp_at - lax.iota(jnp.int32, exp_size)) % exp_size
    targets = [(exp_at + s) % exp_size for s in range(exp_size)]

    row_count, model_width = residual.shape
    half_width = model_width // 2
    groups = lax.axis_size("req") * exp_size
    experts_all = expert_in.shape[0] * groups
    capacity = max(2, 2 * row_count * route_ids.shape[1] // experts_all)
    dense = capacity >= row_count and experts_all == groups

    pieces = gather_blocks(queries, "exp")
    local_lengths = jnp.clip(lengths - exp_at * span, 0, span)
    split_weight = out_weight.reshape(exp_size, share * head_size, -1)
    weight_parts = [take_block(split_weight, targets[0])] + [
        shift(take_block(split_weight, targets[s]), "exp", s) for s in range(1, exp_size)
    ]
    if dense:
        row_weights = route_table(route_ids, route_weights)
        maps_in = halves(expert_in[0].reshape(model_width, -1), half_width, 0)
        maps_out = halves(expert_out[0], half_width, 1)
        gains = halves(norm_gain, half_width, 0)
        pieces, row_weights, maps_in, maps_out = lax.optimization_barrier(
            (pieces, row_weights, maps_in, maps_out)
        )
    messages = attend(
        pieces, sources, new_keys, new_values, key_cache, value_cache, local_lengths,
        512, 256, exp_size,
    )
    received = [take_block(messages, targets[0])] + [
        shift(take_block(messages, targets[s]), "exp", s) for s in range(1, exp_size)
    ]
    group_shift = (head_size - (exp_at * share) % group) % head_size
    info = jnp.concatenate([jnp.stack([group_shift, head_at]).astype(jnp.int32), sources])
    kept, sent = merge_project(received, weight_parts, info, share, requests)
    both = kept + shift(sent, "head", 1).astype(jnp.float32)
    both = both.reshape(exp_size, row_count, half_width)
    outgoing = both.astype(jnp.bfloat16)
    hidden = lax.dynamic_slice_in_dim(residual, head_at * half_width, half_width, 1).astype(
        jnp.float32
    ) + take_block(both, targets[0])
    for s in range(1, exp_size):
        hidden = hidden + shift(take_block(outgoing, targets[s]), "exp", s).astype(jnp.float32)

    if dense:
        mixture = dense_experts(hidden, row_weights, gains, maps_in, maps_out)
    else:
        mixture = sparse_experts(
            hidden, route_ids, route_weights, norm_gain, expert_in, expert_out, capacity
        )
    return (hidden + mixture).astype(jnp.bfloat16)


def solution(mesh):
    return jax.shard_map(
        local,
        mesh=mesh,
        in_specs=(
            P("req", "exp", "head", None),
            P("req", "exp", "head", None),
            P("req", "exp", "head", None),
            P("req", "exp", "head", None),
            P("req", "exp", "head", None),
            P("req"),
            P(("req", "exp"), None),
            P("head", "exp"),
            P(),
            P(("req", "exp"), None),
            P(("req", "exp"), None),
            P(("req", "exp"), None, None, "head"),
            P(("req", "exp"), "head", None),
        ),
        out_specs=P(("req", "exp"), "head"),
        check_vma=False,
    )
```

profile of v0, /device:TPU:0, one launch (start us, length us, event | category | flops | bytes accessed | tf_op | source)
XLA Modules:
  0.0 197.4 jit_solution(5585213559552634088)
XLA Ops:
  0.0 3.0 %collective-permute-start = (bf16[4,16,16,128]{3,2,1,0:T(8,128)(2,1)}, bf16[4,16,16,128]{3,2,1,0:T(8,128)(2,1)S(1)}, u32[]{:S(2)}, u32[]{:S(2)}) collective-permute-start(bf16[4,16,16,128]{3,2,1,0:T(8,128)(2,1)} %refs_0_), channel_id=1, source_target_pairs={{0,1},{1,2},{2,3},{3,0},{4,5},{5,6},{6,7},{7,4},{8,9},{9,10},{10,1... | collective-permute-start | bytes 786440 | tf_op jit(solution)/shard_map/ppermute | solution.py:340
  3.0 1.5 collective-permute-start.1
  4.5 1.4 collective-permute-start.2
  5.9 1.3 select_reduce_fusion
  7.2 5.0 %all-to-all-start = ((f32[16,1,64]{2,1,0:T(1,128)}), f32[16,1,64]{2,1,0:T(1,128)S(1)}, u32[]{:S(2)}, u32[]{:S(2)}) async-start(f32[16,1,64]{2,1,0:T(1,128)} %bitcast.3), calls=%async_computation | async-start | bytes 16384 | tf_op jit(solution)/shard_map/all_to_all | solution.py:363
  12.3 2.9 %dynamic-slice_bitcast_fusion.2 = (bf16[512,512]{1,0:T(8,128)(2,1)}, bf16[512,512]{1,0:T(8,128)(2,1)}, bf16[512,512]{1,0:T(8,128)(2,1)}, bf16[512,512]{1,0:T(8,128)(2,1)}) fusion(bf16[4,512,512]{2,1,0:T(8,128)(2,1)} %bitcast.86, s32[]{:T(128)S(6)} %select_n.125, s32[]{:T(128)S(6)} %select_n.123, s32[]{:T(128)S(6)} %select_n.121, s32[]{:T(128)S(6)} %select_n.119), kind=kLoop, calls=%fused_computation.94 | loop fusion | bytes 4194320 | tf_op jit(solution)/shard_map/jit(dynamic_index_in_dim)/squeeze | solution.py:344
  15.2 1.9 collective-permute-start.6
  17.1 1.5 collective-permute-start.7
  18.7 4.2 %copy.19 = bf16[256,8,2,384]{3,1,2,0:T(8,128)(2,1)} copy(bf16[256,8,2,384]{3,2,1,0:T(2,128)(2,1)} %bitcast.85) | data formatting | bytes 6291456
  22.9 3.4 %constant_dynamic-slice_fusion = (bf16[1024,768]{1,0:T(8,128)(2,1)S(1)}, bf16[1024,768]{1,0:T(8,128)(2,1)}) fusion(bf16[2048,768]{1,0:T(8,128)(2,1)} %bitcast.82, s32[]{:T(128)S(6)} %select_n.117, s32[]{:T(128)S(6)} %select_n.108), kind=kLoop, calls=%fused_computation.125 | loop fusion | bytes 6291464 | tf_op jit(solution)/shard_map/dynamic_slice | solution.py:373
  26.5 0.4 copy-done.5
  26.9 0.6 pad_add_fusion.1.info_ref
  27.7 0.6 gather_fusion
  28.3 1.5 collective-permute-start.8
  29.9 36.0 %attend.1 = bf16[4,64,2176]{2,1,0:T(8,128)(2,1)} custom-call(s32[8]{0:T(128)} %pad_add_fusion.1.info_ref, bf16[4,16,16,128]{3,2,1,0:T(8,128)(2,1)} %refs_0_, bf16[4,16,16,128]{3,2,1,0:T(8,128)(2,1)} %copy-done.2, bf16[4,16,16,128]{3,2,1,0:T(8,128)(2,1)} %collective-permute-done.1.refs_2_, bf16[4,16,16,128]{3,2,1,0:T(8,128)(2,1)} %collective-permute-done.2.refs_3_, ...), custom_call_target="tpu_custom_call" | custom-call | tf_op jit(solution)/shard_map/attend/pallas_call | solution.py:239
  65.9 2.2 %dynamic-slice_bitcast_fusion.6 = (bf16[64,2176]{1,0:T(8,128)(2,1)S(1)}, bf16[64,2176]{1,0:T(8,128)(2,1)}, bf16[64,2176]{1,0:T(8,128)(2,1)}, bf16[64,2176]{1,0:T(8,128)(2,1)}) fusion(bf16[4,64,2176]{2,1,0:T(8,128)(2,1)} %attend.1, s32[]{:T(128)S(6)} %select_n.125, s32[]{:T(128)S(6)} %select_n.123, s32[]{:T(128)S(6)} %select_n.121, s32[]{:T(128)S(6)} %select_n.119), kind=kLoop, calls=%fused_computation.106 | loop fusion | bytes 2228240 | tf_op jit(solution)/shard_map/jit(dynamic_index_in_dim)/squeeze | solution.py:344
  68.0 2.9 %collective-permute-start.5 = (bf16[64,2176]{1,0:T(8,128)(2,1)S(1)}, bf16[64,2176]{1,0:T(8,128)(2,1)}, u32[]{:S(2)}, u32[]{:S(2)}) collective-permute-start(bf16[64,2176]{1,0:T(8,128)(2,1)S(1)} %get-tuple-element.39), channel_id=1, source_target_pairs={{0,3},{1,0},{2,1},{3,2},{4,7},{5,4},{6,5},{7,6},{8,11},{9,8},{10,9... | collective-permute-start | bytes 835592 | tf_op jit(solution)/shard_map/ppermute | solution.py:340
  71.0 0.6 pad_add_fusion.info_ref
  71.6 6.8 %collective-permute-done.3.refs_1_ = bf16[64,2176]{1,0:T(8,128)(2,1)} collective-permute-done((bf16[64,2176]{1,0:T(8,128)(2,1)}, bf16[64,2176]{1,0:T(8,128)(2,1)}, u32[]{:S(2)}, u32[]{:S(2)}) %collective-permute-start.3) | collective-permute-done | bytes 278560 | tf_op jit(solution)/shard_map/ppermute | solution.py:340
  78.5 2.0 %collective-permute-done.4.refs_2_ = bf16[64,2176]{1,0:T(8,128)(2,1)} collective-permute-done((bf16[64,2176]{1,0:T(8,128)(2,1)}, bf16[64,2176]{1,0:T(8,128)(2,1)}, u32[]{:S(2)}, u32[]{:S(2)}) %collective-permute-start.4) | collective-permute-done | bytes 278560 | tf_op jit(solution)/shard_map/ppermute | solution.py:340
  80.5 5.1 %merge_project.1 = (f32[256,1024]{1,0:T(8,128)}, bf16[256,1024]{1,0:T(8,128)(2,1)}) custom-call(s32[6]{0:T(128)} %pad_add_fusion.info_ref, bf16[64,2176]{1,0:T(8,128)(2,1)} %get-tuple-element.42.refs_0_, bf16[64,2176]{1,0:T(8,128)(2,1)} %collective-permute-done.3.refs_1_, bf16[64,2176]{1,0:T(8,128)(2,1)} %collective-permute-done.4.refs_2_, ...), custom_call_target="tpu_custom_call" | custom-call | tf_op jit(solution)/shard_map/merge_project/pallas_call | solution.py:320
  85.6 2.1 %collective-permute-done.9 = bf16[256,1024]{1,0:T(8,128)(2,1)S(1)} collective-permute-done((bf16[256,1024]{1,0:T(8,128)(2,1)}, bf16[256,1024]{1,0:T(8,128)(2,1)S(1)}, u32[]{:S(2)}, u32[]{:S(2)}) %collective-permute-start.9) | collective-permute-done | bytes 524320 | tf_op jit(solution)/shard_map/ppermute | solution.py:340
  87.7 1.4 convert_add_fusion
  89.2 1.5 collective-permute-start.10
  90.7 1.8 collective-permute-start.11
  92.5 1.2 collective-permute-start.12
  93.7 2.9 %collective-permute-done.10 = bf16[64,1024]{1,0:T(8,128)(2,1)S(1)} collective-permute-done((bf16[64,1024]{1,0:T(8,128)(2,1)S(1)}, bf16[64,1024]{1,0:T(8,128)(2,1)S(1)}, u32[]{:S(2)}, u32[]{:S(2)}) %collective-permute-start.10) | collective-permute-done | bytes 131104 | tf_op jit(solution)/shard_map/ppermute | solution.py:340
  96.5 2.0 collective-permute-done.11
  98.6 6.1 %collective-permute-start.13 = (bf16[64,1024]{1,0:T(8,128)(2,1)S(1)}, bf16[64,1024]{1,0:T(8,128)(2,1)S(1)}, u32[]{:S(2)}, u32[]{:S(2)}) collective-permute-start(bf16[64,1024]{1,0:T(8,128)(2,1)S(1)} %get-tuple-element.29), channel_id=1, source_target_pairs={{0,8},{8,16},{16,24},{24,0},{1,9},{9,17},{17,25},{25,1},{2,10},{10... | collective-permute-start | bytes 393224 | tf_op jit(solution)/shard_map/ppermute | solution.py:340
  104.8 3.8 %collective-permute-start.14 = (bf16[64,1024]{1,0:T(8,128)(2,1)S(1)}, bf16[64,1024]{1,0:T(8,128)(2,1)S(1)}, u32[]{:S(2)}, u32[]{:S(2)}) collective-permute-start(bf16[64,1024]{1,0:T(8,128)(2,1)S(1)} %get-tuple-element.29), channel_id=1, source_target_pairs={{0,16},{8,24},{16,0},{24,8},{1,17},{9,25},{17,1},{25,9},{2,18},{10... | collective-permute-start | bytes 393224 | tf_op jit(solution)/shard_map/ppermute | solution.py:340
  108.5 3.9 %collective-permute-done.13 = bf16[64,1024]{1,0:T(8,128)(2,1)S(1)} collective-permute-done((bf16[64,1024]{1,0:T(8,128)(2,1)S(1)}, bf16[64,1024]{1,0:T(8,128)(2,1)S(1)}, u32[]{:S(2)}, u32[]{:S(2)}) %collective-permute-start.13) | collective-permute-done | bytes 131104 | tf_op jit(solution)/shard_map/ppermute | solution.py:340
  112.4 4.9 %collective-permute-done.14 = bf16[64,1024]{1,0:T(8,128)(2,1)S(1)} collective-permute-done((bf16[64,1024]{1,0:T(8,128)(2,1)S(1)}, bf16[64,1024]{1,0:T(8,128)(2,1)S(1)}, u32[]{:S(2)}, u32[]{:S(2)}) %collective-permute-start.14) | collective-permute-done | bytes 131104 | tf_op jit(solution)/shard_map/ppermute | solution.py:340
  117.6 1.1 collective-permute-start.18
  118.7 0.5 collective-permute-start.22
  119.2 2.8 %collective-permute-start.26 = (bf16[256,1024]{1,0:T(8,128)(2,1)S(1)}, bf16[256,1024]{1,0:T(8,128)(2,1)S(1)}, u32[]{:S(2)}, u32[]{:S(2)}) collective-permute-start(bf16[256,1024]{1,0:T(8,128)(2,1)S(1)} %get-tuple-element.28), channel_id=1, source_target_pairs={{0,3},{1,0},{2,1},{3,2},{4,7},{5,4},{6,5},{7,6},{8,11},{9,8},{10,9... | collective-permute-start | bytes 1572872 | tf_op jit(solution)/shard_map/ppermute | solution.py:340
  122.3 0.6 fusion.59
  122.9 0.8 copy-done
  123.7 0.6 convolution_add_fusion
  124.3 9.1 %collective-permute-done.18 = bf16[256,1024]{1,0:T(8,128)(2,1)S(1)} collective-permute-done((bf16[256,1024]{1,0:T(8,128)(2,1)S(1)}, bf16[256,1024]{1,0:T(8,128)(2,1)S(1)}, u32[]{:S(2)}, u32[]{:S(2)}) %collective-permute-start.18) | collective-permute-done | bytes 524320 | tf_op jit(solution)/shard_map/ppermute | solution.py:340
  133.5 0.4 fusion.10
  134.0 0.6 collective-permute-start.17
  134.6 9.4 %collective-permute-done.22 = bf16[256,1024]{1,0:T(8,128)(2,1)S(1)} collective-permute-done((bf16[256,1024]{1,0:T(8,128)(2,1)S(1)}, bf16[256,1024]{1,0:T(8,128)(2,1)S(1)}, u32[]{:S(2)}, u32[]{:S(2)}) %collective-permute-start.22) | collective-permute-done | bytes 524320 | tf_op jit(solution)/shard_map/ppermute | solution.py:340
  145.2 0.6 fusion.57
  145.9 0.6 fusion.54
  146.6 0.4 fusion.11
  147.6 0.6 fusion.50
  148.2 0.6 fusion.47
  148.9 0.4 fusion.12
  150.0 0.6 fusion.43
  150.6 0.6 fusion.40
  151.4 0.4 fusion.13
  152.1 0.4 fusion.7
  152.5 1.7 collective-permute-start.21
  154.3 0.4 fusion.8
  154.7 1.6 collective-permute-start.25
  156.3 0.4 fusion.9
  156.8 10.6 %collective-permute-done.21 = bf16[256,1024]{1,0:T(8,128)(2,1)S(1)} collective-permute-done((bf16[256,1024]{1,0:T(8,128)(2,1)S(1)}, bf16[256,1024]{1,0:T(8,128)(2,1)S(1)}, u32[]{:S(2)}, u32[]{:S(2)}) %collective-permute-start.21) | collective-permute-done | bytes 524320 | tf_op jit(solution)/shard_map/ppermute | solution.py:340
  167.4 12.7 %collective-permute-done.25 = bf16[256,1024]{1,0:T(8,128)(2,1)S(1)} collective-permute-done((bf16[256,1024]{1,0:T(8,128)(2,1)S(1)}, bf16[256,1024]{1,0:T(8,128)(2,1)S(1)}, u32[]{:S(2)}, u32[]{:S(2)}) %collective-permute-start.25) | collective-permute-done | bytes 524320 | tf_op jit(solution)/shard_map/ppermute | solution.py:340
  180.1 0.6 fusion.98
  180.7 2.7 %collective-permute-start.30 = (bf16[64,1024]{1,0:T(8,128)(2,1)S(1)}, bf16[64,1024]{1,0:T(8,128)(2,1)S(1)}, u32[]{:S(2)}, u32[]{:S(2)}) collective-permute-start(bf16[64,1024]{1,0:T(8,128)(2,1)S(1)} %get-tuple-element.43), channel_id=1, source_target_pairs={{0,24},{8,0},{16,8},{24,16},{1,25},{9,1},{17,9},{25,17},{2,26},{10... | collective-permute-start | bytes 393224 | tf_op jit(solution)/shard_map/ppermute | solution.py:340
  183.4 2.1 %collective-permute-start.31 = (bf16[64,1024]{1,0:T(8,128)(2,1)S(1)}, bf16[64,1024]{1,0:T(8,128)(2,1)S(1)}, u32[]{:S(2)}, u32[]{:S(2)}) collective-permute-start(bf16[64,1024]{1,0:T(8,128)(2,1)S(1)} %get-tuple-element.45), channel_id=1, source_target_pairs={{0,16},{8,24},{16,0},{24,8},{1,17},{9,25},{17,1},{25,9},{2,18},{10... | collective-permute-start | bytes 393224 | tf_op jit(solution)/shard_map/ppermute | solution.py:340
  185.5 1.6 collective-permute-done.30
  187.2 9.5 %collective-permute-done.31 = bf16[64,1024]{1,0:T(8,128)(2,1)S(1)} collective-permute-done((bf16[64,1024]{1,0:T(8,128)(2,1)S(1)}, bf16[64,1024]{1,0:T(8,128)(2,1)S(1)}, u32[]{:S(2)}, u32[]{:S(2)}) %collective-permute-start.31) | collective-permute-done | bytes 131104 | tf_op jit(solution)/shard_map/ppermute | solution.py:340
  196.7 0.7 fusion.85
  (79 shorter events, 4.5 us)
Async XLA Ops:
  0.0 28.3 %collective-permute-start = (bf16[4,16,16,128]{3,2,1,0:T(8,128)(2,1)}, bf16[4,16,16,128]{3,2,1,0:T(8,128)(2,1)S(1)}, u32[]{:S(2)}, u32[]{:S(2)}) collective-permute-start(bf16[4,16,16,128]{3,2,1,0:T(8,128)(2,1)} %refs_0_), channel_id=1, source_target_pairs={{0,1},{1,2},{2,3},{3,0},{4,5},{5,6},{6,7},{7,4},{8,9},{9,10},{10,1... | collective-permute-start | bytes 786440 | tf_op jit(solution)/shard_map/ppermute | solution.py:340
  3.0 26.9 %collective-permute-start.1 = (bf16[4,16,16,128]{3,2,1,0:T(8,128)(2,1)}, bf16[4,16,16,128]{3,2,1,0:T(8,128)(2,1)}, u32[]{:S(2)}, u32[]{:S(2)}) collective-permute-start(bf16[4,16,16,128]{3,2,1,0:T(8,128)(2,1)} %refs_0_), channel_id=1, source_target_pairs={{0,2},{1,3},{2,0},{3,1},{4,6},{5,7},{6,4},{7,5},{8,10},{9,11},{10,... | collective-permute-start | bytes 786440 | tf_op jit(solution)/shard_map/ppermute | solution.py:340
  4.5 25.4 %collective-permute-start.2 = (bf16[4,16,16,128]{3,2,1,0:T(8,128)(2,1)}, bf16[4,16,16,128]{3,2,1,0:T(8,128)(2,1)}, u32[]{:S(2)}, u32[]{:S(2)}) collective-permute-start(bf16[4,16,16,128]{3,2,1,0:T(8,128)(2,1)} %refs_0_), channel_id=1, source_target_pairs={{0,3},{1,0},{2,1},{3,2},{4,7},{5,4},{6,5},{7,6},{8,11},{9,8},{10,9... | collective-permute-start | bytes 786440 | tf_op jit(solution)/shard_map/ppermute | solution.py:340
  7.2 20.4 %all-to-all-start = ((f32[16,1,64]{2,1,0:T(1,128)}), f32[16,1,64]{2,1,0:T(1,128)S(1)}, u32[]{:S(2)}, u32[]{:S(2)}) async-start(f32[16,1,64]{2,1,0:T(1,128)} %bitcast.3), calls=%async_computation | async-start | bytes 16384 | tf_op jit(solution)/shard_map/all_to_all | solution.py:363
  15.2 52.8 %collective-permute-start.6 = (bf16[512,512]{1,0:T(8,128)(2,1)}, bf16[512,512]{1,0:T(8,128)(2,1)}, u32[]{:S(2)}, u32[]{:S(2)}) collective-permute-start(bf16[512,512]{1,0:T(8,128)(2,1)} %get-tuple-element.35), channel_id=1, source_target_pairs={{0,1},{1,2},{2,3},{3,0},{4,5},{5,6},{6,7},{7,4},{8,9},{9,10},{10,1... | collective-permute-start | bytes 1572872 | tf_op jit(solution)/shard_map/ppermute | solution.py:340
  17.1 54.5 %collective-permute-start.7 = (bf16[512,512]{1,0:T(8,128)(2,1)}, bf16[512,512]{1,0:T(8,128)(2,1)}, u32[]{:S(2)}, u32[]{:S(2)}) collective-permute-start(bf16[512,512]{1,0:T(8,128)(2,1)} %get-tuple-element.34), channel_id=1, source_target_pairs={{0,2},{1,3},{2,0},{3,1},{4,6},{5,7},{6,4},{7,5},{8,10},{9,11},{10,... | collective-permute-start | bytes 1572872 | tf_op jit(solution)/shard_map/ppermute | solution.py:340
  22.9 3.4 %copy-start.1 = (bf16[1,384,2048]{2,1,0:T(8,128)(2,1)S(1)}, bf16[1,384,2048]{2,1,0:T(8,128)(2,1)}, u32[]{:S(2)}) copy-start(bf16[1,384,2048]{2,1,0:T(8,128)(2,1)} %param.25) | copy-start | bytes 4718596
  26.2 0.7 copy-start.5
  28.3 1.5 copy-start.2
  28.3 43.3 %collective-permute-start.8 = (bf16[512,512]{1,0:T(8,128)(2,1)}, bf16[512,512]{1,0:T(8,128)(2,1)}, u32[]{:S(2)}, u32[]{:S(2)}) collective-permute-start(bf16[512,512]{1,0:T(8,128)(2,1)} %get-tuple-element.33), channel_id=1, source_target_pairs={{0,3},{1,0},{2,1},{3,2},{4,7},{5,4},{6,5},{7,6},{8,11},{9,8},{10,9... | collective-permute-start | bytes 1572872 | tf_op jit(solution)/shard_map/ppermute | solution.py:340
  68.0 10.4 %collective-permute-start.3 = (bf16[64,2176]{1,0:T(8,128)(2,1)}, bf16[64,2176]{1,0:T(8,128)(2,1)}, u32[]{:S(2)}, u32[]{:S(2)}) collective-permute-start(bf16[64,2176]{1,0:T(8,128)(2,1)} %get-tuple-element.41), channel_id=1, source_target_pairs={{0,1},{1,2},{2,3},{3,0},{4,5},{5,6},{6,7},{7,4},{8,9},{9,10},{10,1... | collective-permute-start | bytes 835592 | tf_op jit(solution)/shard_map/ppermute | solution.py:340
  68.0 12.5 %collective-permute-start.4 = (bf16[64,2176]{1,0:T(8,128)(2,1)}, bf16[64,2176]{1,0:T(8,128)(2,1)}, u32[]{:S(2)}, u32[]{:S(2)}) collective-permute-start(bf16[64,2176]{1,0:T(8,128)(2,1)} %get-tuple-element.40), channel_id=1, source_target_pairs={{0,2},{1,3},{2,0},{3,1},{4,6},{5,7},{6,4},{7,5},{8,10},{9,11},{10,... | collective-permute-start | bytes 835592 | tf_op jit(solution)/shard_map/ppermute | solution.py:340
  68.0 12.5 %collective-permute-start.5 = (bf16[64,2176]{1,0:T(8,128)(2,1)S(1)}, bf16[64,2176]{1,0:T(8,128)(2,1)}, u32[]{:S(2)}, u32[]{:S(2)}) collective-permute-start(bf16[64,2176]{1,0:T(8,128)(2,1)S(1)} %get-tuple-element.39), channel_id=1, source_target_pairs={{0,3},{1,0},{2,1},{3,2},{4,7},{5,4},{6,5},{7,6},{8,11},{9,8},{10,9... | collective-permute-start | bytes 835592 | tf_op jit(solution)/shard_map/ppermute | solution.py:340
  85.6 2.1 %collective-permute-start.9 = (bf16[256,1024]{1,0:T(8,128)(2,1)}, bf16[256,1024]{1,0:T(8,128)(2,1)S(1)}, u32[]{:S(2)}, u32[]{:S(2)}) collective-permute-start(bf16[256,1024]{1,0:T(8,128)(2,1)} %get-tuple-element.21), channel_id=1, source_target_pairs={{0,4},{4,0},{1,5},{5,1},{2,6},{6,2},{3,7},{7,3},{8,12},{12,8},{9,1... | collective-permute-start | bytes 1572872 | tf_op jit(solution)/shard_map/ppermute | solution.py:340
  89.0 9.5 %copy-start.3 = (bf16[64,2048]{1,0:T(8,128)(2,1)S(1)}, bf16[64,2048]{1,0:T(8,128)(2,1)}, u32[]{:S(2)}) copy-start(bf16[64,2048]{1,0:T(8,128)(2,1)} %param.19) | copy-start | bytes 786436
  89.1 28.4 %copy-start.4 = (f32[2048]{0:T(1024)S(1)}, f32[2048]{0:T(1024)}, u32[]{:S(2)}) copy-start(f32[2048]{0:T(1024)} %param.21) | copy-start | bytes 24580
  89.2 7.3 %collective-permute-start.10 = (bf16[64,1024]{1,0:T(8,128)(2,1)S(1)}, bf16[64,1024]{1,0:T(8,128)(2,1)S(1)}, u32[]{:S(2)}, u32[]{:S(2)}) collective-permute-start(bf16[64,1024]{1,0:T(8,128)(2,1)S(1)} %get-tuple-element.46), channel_id=1, source_target_pairs={{0,1},{1,2},{2,3},{3,0},{4,5},{5,6},{6,7},{7,4},{8,9},{9,10},{10,1... | collective-permute-start | bytes 393224 | tf_op jit(solution)/shard_map/ppermute | solution.py:340
  90.7 7.8 %collective-permute-start.11 = (bf16[64,1024]{1,0:T(8,128)(2,1)S(1)}, bf16[64,1024]{1,0:T(8,128)(2,1)S(1)}, u32[]{:S(2)}, u32[]{:S(2)}) collective-permute-start(bf16[64,1024]{1,0:T(8,128)(2,1)S(1)} %get-tuple-element.48), channel_id=1, source_target_pairs={{0,2},{1,3},{2,0},{3,1},{4,6},{5,7},{6,4},{7,5},{8,10},{9,11},{10,... | collective-permute-start | bytes 393224 | tf_op jit(solution)/shard_map/ppermute | solution.py:340
  92.5 6.1 %collective-permute-start.12 = (bf16[64,1024]{1,0:T(8,128)(2,1)S(1)}, bf16[64,1024]{1,0:T(8,128)(2,1)S(1)}, u32[]{:S(2)}, u32[]{:S(2)}) collective-permute-start(bf16[64,1024]{1,0:T(8,128)(2,1)S(1)} %get-tuple-element.47), channel_id=1, source_target_pairs={{0,3},{1,0},{2,1},{3,2},{4,7},{5,4},{6,5},{7,6},{8,11},{9,8},{10,9... | collective-permute-start | bytes 393224 | tf_op jit(solution)/shard_map/ppermute | solution.py:340
  98.6 13.8 %collective-permute-start.13 = (bf16[64,1024]{1,0:T(8,128)(2,1)S(1)}, bf16[64,1024]{1,0:T(8,128)(2,1)S(1)}, u32[]{:S(2)}, u32[]{:S(2)}) collective-permute-start(bf16[64,1024]{1,0:T(8,128)(2,1)S(1)} %get-tuple-element.29), channel_id=1, source_target_pairs={{0,8},{8,16},{16,24},{24,0},{1,9},{9,17},{17,25},{25,1},{2,10},{10... | collective-permute-start | bytes 393224 | tf_op jit(solution)/shard_map/ppermute | solution.py:340
  104.8 12.5 %collective-permute-start.14 = (bf16[64,1024]{1,0:T(8,128)(2,1)S(1)}, bf16[64,1024]{1,0:T(8,128)(2,1)S(1)}, u32[]{:S(2)}, u32[]{:S(2)}) collective-permute-start(bf16[64,1024]{1,0:T(8,128)(2,1)S(1)} %get-tuple-element.29), channel_id=1, source_target_pairs={{0,16},{8,24},{16,0},{24,8},{1,17},{9,25},{17,1},{25,9},{2,18},{10... | collective-permute-start | bytes 393224 | tf_op jit(solution)/shard_map/ppermute | solution.py:340
  108.5 8.8 %collective-permute-start.15 = (bf16[64,1024]{1,0:T(8,128)(2,1)S(1)}, bf16[64,1024]{1,0:T(8,128)(2,1)S(1)}, u32[]{:S(2)}, u32[]{:S(2)}) collective-permute-start(bf16[64,1024]{1,0:T(8,128)(2,1)S(1)} %get-tuple-element.29), channel_id=1, source_target_pairs={{0,24},{8,0},{16,8},{24,16},{1,25},{9,1},{17,9},{25,17},{2,26},{10... | collective-permute-start | bytes 393224 | tf_op jit(solution)/shard_map/ppermute | solution.py:340
  117.5 4.6 %collective-permute-start.16 = (bf16[256,1024]{1,0:T(8,128)(2,1)S(1)}, bf16[256,1024]{1,0:T(8,128)(2,1)S(1)}, u32[]{:S(2)}, u32[]{:S(2)}) collective-permute-start(bf16[256,1024]{1,0:T(8,128)(2,1)S(1)} %get-tuple-element.28), channel_id=1, source_target_pairs={{0,4},{4,0},{1,5},{5,1},{2,6},{6,2},{3,7},{7,3},{8,12},{12,8},{9,1... | collective-permute-start | bytes 1572872 | tf_op jit(solution)/shard_map/ppermute | solution.py:340
  117.6 15.8 %collective-permute-start.18 = (bf16[256,1024]{1,0:T(8,128)(2,1)S(1)}, bf16[256,1024]{1,0:T(8,128)(2,1)S(1)}, u32[]{:S(2)}, u32[]{:S(2)}) collective-permute-start(bf16[256,1024]{1,0:T(8,128)(2,1)S(1)} %get-tuple-element.28), channel_id=1, source_target_pairs={{0,1},{1,2},{2,3},{3,0},{4,5},{5,6},{6,7},{7,4},{8,9},{9,10},{10,1... | collective-permute-start | bytes 1572872 | tf_op jit(solution)/shard_map/ppermute | solution.py:340
  118.7 25.3 %collective-permute-start.22 = (bf16[256,1024]{1,0:T(8,128)(2,1)S(1)}, bf16[256,1024]{1,0:T(8,128)(2,1)S(1)}, u32[]{:S(2)}, u32[]{:S(2)}) collective-permute-start(bf16[256,1024]{1,0:T(8,128)(2,1)S(1)} %get-tuple-element.28), channel_id=1, source_target_pairs={{0,2},{1,3},{2,0},{3,1},{4,6},{5,7},{6,4},{7,5},{8,10},{9,11},{10,... | collective-permute-start | bytes 1572872 | tf_op jit(solution)/shard_map/ppermute | solution.py:340
  119.2 24.9 %collective-permute-start.26 = (bf16[256,1024]{1,0:T(8,128)(2,1)S(1)}, bf16[256,1024]{1,0:T(8,128)(2,1)S(1)}, u32[]{:S(2)}, u32[]{:S(2)}) collective-permute-start(bf16[256,1024]{1,0:T(8,128)(2,1)S(1)} %get-tuple-element.28), channel_id=1, source_target_pairs={{0,3},{1,0},{2,1},{3,2},{4,7},{5,4},{6,5},{7,6},{8,11},{9,8},{10,9... | collective-permute-start | bytes 1572872 | tf_op jit(solution)/shard_map/ppermute | solution.py:340
  122.3 1.4 copy-start
  133.4 11.6 %collective-permute-start.19 = (bf16[256,1024]{1,0:T(8,128)(2,1)S(1)}, bf16[256,1024]{1,0:T(8,128)(2,1)S(1)}, u32[]{:S(2)}, u32[]{:S(2)}) collective-permute-start(bf16[256,1024]{1,0:T(8,128)(2,1)S(1)} %collective-permute-done.18), channel_id=1, source_target_pairs={{0,4},{4,0},{1,5},{5,1},{2,6},{6,2},{3,7},{7,3},{8,12},{12,8},{9,1... | collective-permute-start | bytes 1572872 | tf_op jit(solution)/shard_map/ppermute | solution.py:340
  134.0 22.8 %collective-permute-start.17 = (bf16[256,1024]{1,0:T(8,128)(2,1)S(1)}, bf16[256,1024]{1,0:T(8,128)(2,1)S(1)}, u32[]{:S(2)}, u32[]{:S(2)}) collective-permute-start(bf16[256,1024]{1,0:T(8,128)(2,1)S(1)} %fusion.10), channel_id=1, source_target_pairs={{0,4},{4,0},{1,5},{5,1},{2,6},{6,2},{3,7},{7,3},{8,12},{12,8},{9,1... | collective-permute-start | bytes 1572872 | tf_op jit(solution)/shard_map/ppermute | solution.py:340
  144.0 3.4 %collective-permute-start.23 = (bf16[256,1024]{1,0:T(8,128)(2,1)S(1)}, bf16[256,1024]{1,0:T(8,128)(2,1)S(1)}, u32[]{:S(2)}, u32[]{:S(2)}) collective-permute-start(bf16[256,1024]{1,0:T(8,128)(2,1)S(1)} %collective-permute-done.22), channel_id=1, source_target_pairs={{0,4},{4,0},{1,5},{5,1},{2,6},{6,2},{3,7},{7,3},{8,12},{12,8},{9,1... | collective-permute-start | bytes 1572872 | tf_op jit(solution)/shard_map/ppermute | solution.py:340
  144.2 5.6 %collective-permute-start.27 = (bf16[256,1024]{1,0:T(8,128)(2,1)S(1)}, bf16[256,1024]{1,0:T(8,128)(2,1)S(1)}, u32[]{:S(2)}, u32[]{:S(2)}) collective-permute-start(bf16[256,1024]{1,0:T(8,128)(2,1)S(1)} %collective-permute-done.26), channel_id=1, source_target_pairs={{0,4},{4,0},{1,5},{5,1},{2,6},{6,2},{3,7},{7,3},{8,12},{12,8},{9,1... | collective-permute-start | bytes 1572872 | tf_op jit(solution)/shard_map/ppermute | solution.py:340
  147.1 5.0 %collective-permute-start.20 = (bf16[256,1024]{1,0:T(8,128)(2,1)S(1)}, bf16[256,1024]{1,0:T(8,128)(2,1)S(1)}, u32[]{:S(2)}, u32[]{:S(2)}) collective-permute-start(bf16[256,1024]{1,0:T(8,128)(2,1)S(1)} %fusion.11), channel_id=1, source_target_pairs={{0,4},{4,0},{1,5},{5,1},{2,6},{6,2},{3,7},{7,3},{8,12},{12,8},{9,1... | collective-permute-start | bytes 1572872 | tf_op jit(solution)/shard_map/ppermute | solution.py:340
  149.4 4.9 %collective-permute-start.24 = (bf16[256,1024]{1,0:T(8,128)(2,1)S(1)}, bf16[256,1024]{1,0:T(8,128)(2,1)S(1)}, u32[]{:S(2)}, u32[]{:S(2)}) collective-permute-start(bf16[256,1024]{1,0:T(8,128)(2,1)S(1)} %fusion.12), channel_id=1, source_target_pairs={{0,4},{4,0},{1,5},{5,1},{2,6},{6,2},{3,7},{7,3},{8,12},{12,8},{9,1... | collective-permute-start | bytes 1572872 | tf_op jit(solution)/shard_map/ppermute | solution.py:340
  151.8 4.5 %collective-permute-start.28 = (bf16[256,1024]{1,0:T(8,128)(2,1)S(1)}, bf16[256,1024]{1,0:T(8,128)(2,1)S(1)}, u32[]{:S(2)}, u32[]{:S(2)}) collective-permute-start(bf16[256,1024]{1,0:T(8,128)(2,1)S(1)} %fusion.13), channel_id=1, source_target_pairs={{0,4},{4,0},{1,5},{5,1},{2,6},{6,2},{3,7},{7,3},{8,12},{12,8},{9,1... | collective-permute-start | bytes 1572872 | tf_op jit(solution)/shard_map/ppermute | solution.py:340
  152.5 14.8 %collective-permute-start.21 = (bf16[256,1024]{1,0:T(8,128)(2,1)S(1)}, bf16[256,1024]{1,0:T(8,128)(2,1)S(1)}, u32[]{:S(2)}, u32[]{:S(2)}) collective-permute-start(bf16[256,1024]{1,0:T(8,128)(2,1)S(1)} %fusion.7), channel_id=1, source_target_pairs={{0,3},{1,0},{2,1},{3,2},{4,7},{5,4},{6,5},{7,6},{8,11},{9,8},{10,9... | collective-permute-start | bytes 1572872 | tf_op jit(solution)/shard_map/ppermute | solution.py:340
  154.7 25.3 %collective-permute-start.25 = (bf16[256,1024]{1,0:T(8,128)(2,1)S(1)}, bf16[256,1024]{1,0:T(8,128)(2,1)S(1)}, u32[]{:S(2)}, u32[]{:S(2)}) collective-permute-start(bf16[256,1024]{1,0:T(8,128)(2,1)S(1)} %fusion.8), channel_id=1, source_target_pairs={{0,2},{1,3},{2,0},{3,1},{4,6},{5,7},{6,4},{7,5},{8,10},{9,11},{10,... | collective-permute-start | bytes 1572872 | tf_op jit(solution)/shard_map/ppermute | solution.py:340
  156.8 23.3 %collective-permute-start.29 = (bf16[256,1024]{1,0:T(8,128)(2,1)S(1)}, bf16[256,1024]{1,0:T(8,128)(2,1)S(1)}, u32[]{:S(2)}, u32[]{:S(2)}) collective-permute-start(bf16[256,1024]{1,0:T(8,128)(2,1)S(1)} %fusion.9), channel_id=1, source_target_pairs={{0,1},{1,2},{2,3},{3,0},{4,5},{5,6},{6,7},{7,4},{8,9},{9,10},{10,1... | collective-permute-start | bytes 1572872 | tf_op jit(solution)/shard_map/ppermute | solution.py:340
  180.7 6.4 %collective-permute-start.30 = (bf16[64,1024]{1,0:T(8,128)(2,1)S(1)}, bf16[64,1024]{1,0:T(8,128)(2,1)S(1)}, u32[]{:S(2)}, u32[]{:S(2)}) collective-permute-start(bf16[64,1024]{1,0:T(8,128)(2,1)S(1)} %get-tuple-element.43), channel_id=1, source_target_pairs={{0,24},{8,0},{16,8},{24,16},{1,25},{9,1},{17,9},{25,17},{2,26},{10... | collective-permute-start | bytes 393224 | tf_op jit(solution)/shard_map/ppermute | solution.py:340
  183.4 13.2 %collective-permute-start.31 = (bf16[64,1024]{1,0:T(8,128)(2,1)S(1)}, bf16[64,1024]{1,0:T(8,128)(2,1)S(1)}, u32[]{:S(2)}, u32[]{:S(2)}) collective-permute-start(bf16[64,1024]{1,0:T(8,128)(2,1)S(1)} %get-tuple-element.45), channel_id=1, source_target_pairs={{0,16},{8,24},{16,0},{24,8},{1,17},{9,25},{17,1},{25,9},{2,18},{10... | collective-permute-start | bytes 393224 | tf_op jit(solution)/shard_map/ppermute | solution.py:340
  185.5 11.2 %collective-permute-start.32 = (bf16[64,1024]{1,0:T(8,128)(2,1)S(1)}, bf16[64,1024]{1,0:T(8,128)(2,1)S(1)}, u32[]{:S(2)}, u32[]{:S(2)}) collective-permute-start(bf16[64,1024]{1,0:T(8,128)(2,1)S(1)} %get-tuple-element.44), channel_id=1, source_target_pairs={{0,8},{8,16},{16,24},{24,0},{1,9},{9,17},{17,25},{25,1},{2,10},{10... | collective-permute-start | bytes 393224 | tf_op jit(solution)/shard_map/ppermute | solution.py:340
where the time goes:
time: 197 us
  waiting for transfers between devices  77.8 us (39%)
  starting transfers between devices  47.6 us (24%)
  Pallas kernels  41.1 us (21%)
  local copies, waits for them, and re-layouts  14.9 us (8%)
  matrix products  8.7 us (4%)
  other arithmetic  6.99 us (4%)
    ppermute x33, waiting for transfers between devices, shift(): lax.ppermute(value, axis, [(i, (i + step) % size) for i in range(size)])  77.8 us
    ppermute x33, starting transfers between devices, shift(): lax.ppermute(value, axis, [(i, (i + step) % size) for i in range(size)])  42.6 us
    pallas_call x1, Pallas kernels, attend(): pl.pallas_call(functools.partial(attend_kernel, pieces, sub, tail, factor...  36 us
    unnamed x13, local copies, waits for them, and re-layouts  5.35 us
    squeeze x3, local copies, waits for them, and re-layouts, take_block(): return lax.dynamic_index_in_dim(value, index, 0, keepdims=False)  5.09 us
    pallas_call x1, Pallas kernels, merge_project(): pl.pallas_call(functools.partial(merge_kernel, parts, share), in_specs=[p...  5.07 us
    dot_general x8, matrix products, dense_experts(): jnp.dot((x * factor * gain).astype(jnp.bfloat16), maps, preferred_element...  5.02 us
    all_to_all x1, starting transfers between devices, route_table(): lax.all_to_all(table, ('req', 'exp'), split_axis=0, concat_axis=0, tiled=...  5.01 us
  transfers between devices with their start and end apart: 34, of which 14 were waited for; matrix products, arithmetic and copies ran while one was open for 13% of the time, Pallas kernels for 18%

commit v1 on v0

--- a/solution.py
+++ b/solution.py
@@ -348,11 +348,14 @@
     return [block] + [shift(block, axis, s) for s in range(1, lax.axis_size(axis))]
 
 
+def swap(value, axis, bits):
+    size = lax.axis_size(axis)
+    return lax.ppermute(value, axis, [(i, i ^ bits) for i in range(size)])
+
+
 def route_table(route_ids, route_weights):
-    req_size, exp_size = lax.axis_size("req"), lax.axis_size("exp")
-    req_at, exp_at = lax.axis_index("req"), lax.axis_index("exp")
-    groups = req_size * exp_size
-    table = jnp.sum(
+    groups = lax.axis_size("req") * lax.axis_size("exp")
+    return jnp.sum(
         jnp.where(
             route_ids[None, :, :] == lax.iota(jnp.int32, groups)[:, None, None],
             route_weights[None, :, :],
@@ -360,9 +363,13 @@
         ),
         axis=2,
     )
+
+
+def exchange_table(table):
+    req_size, exp_size = lax.axis_size("req"), lax.axis_size("exp")
     mine = lax.all_to_all(table, ("req", "exp"), split_axis=0, concat_axis=0, tiled=True)
-    by_req = (req_at - lax.iota(jnp.int32, req_size)) % req_size
-    by_exp = (exp_at - lax.iota(jnp.int32, exp_size)) % exp_size
+    by_req = (lax.axis_index("req") - lax.iota(jnp.int32, req_size)) % req_size
+    by_exp = lax.axis_index("exp") ^ lax.iota(jnp.int32, exp_size)
     order = by_req[None, :] * exp_size + by_exp[:, None]
     return jnp.take(mine, order.reshape(-1), axis=0).reshape(exp_size, -1)
 
@@ -374,40 +381,54 @@
     return own, other
 
 
-def dense_experts(half_hidden, row_weights, gains, maps_in, maps_out):
+def expert_block(own, weights, gains, maps_in, maps_out):
+    other = swap(own, "head", 1)
+    wide = [own.astype(jnp.float32), other.astype(jnp.float32)]
+    squares = sum(jnp.sum(x * x, axis=-1, keepdims=True) for x in wide)
+    factor = lax.rsqrt(squares / (2 * own.shape[1]) + norm_epsilon)
+    gate_up = sum(
+        jnp.dot((x * factor * gain).astype(jnp.bfloat16), maps, preferred_element_type=jnp.float32)
+        for x, gain, maps in zip(wide, gains, maps_in)
+    )
+    half_units = gate_up.shape[-1] // 2
+    activated = (jax.nn.silu(gate_up[:, :half_units]) * gate_up[:, half_units:]).astype(
+        jnp.bfloat16
+    )
+    kept, passed = [
+        jnp.dot(activated, maps, preferred_element_type=jnp.float32) * weights[:, None]
+        for maps in maps_out
+    ]
+    return kept + swap(passed.astype(jnp.bfloat16), "head", 1).astype(jnp.float32)
+
+
+def dense_experts(half_hidden, table, gains, maps_in, maps_out):
     row_count, half_width = half_hidden.shape
-    req_size, exp_size = lax.axis_size("req"), lax.axis_size("exp")
+    req_size = lax.axis_size("req")
     sent = half_hidden.astype(jnp.bfloat16)
     column = jnp.concatenate(gather_blocks(sent, "req"), axis=0)
-    blocks = gather_blocks(column, "exp")
-    back = []
-    for s, own in enumerate(blocks):
-        other = shift(own, "head", 1)
-        wide = [own.astype(jnp.float32), other.astype(jnp.float32)]
-        squares = sum(jnp.sum(x * x, axis=-1, keepdims=True) for x in wide)
-        factor = lax.rsqrt(squares / (2 * half_width) + norm_epsilon)
-        gate_up = sum(
-            jnp.dot(
-                (x * factor * gain).astype(jnp.bfloat16), maps, preferred_element_type=jnp.float32
-            )
-            for x, gain, maps in zip(wide, gains, maps_in)
-        )
-        half_units = gate_up.shape[-1] // 2
-        activated = (
-            jax.nn.silu(gate_up[:, :half_units])
-            * gate_up[:, half_units:]
-        ).astype(jnp.bfloat16)
-        weight = row_weights[s][:, None]
-        kept, passed = [
-            jnp.dot(activated, maps, preferred_element_type=jnp.float32) * weight
-            for maps in maps_out
-        ]
-        swapped = shift(passed.astype(jnp.bfloat16), "head", 1).astype(jnp.float32)
-        back.append(kept + swapped)
-    plane_sum = back[0]
-    for s in range(1, exp_size):
-        plane_sum = plane_sum + shift(back[s].astype(jnp.bfloat16), "exp", -s).astype(jnp.float32)
-    plane_sum = plane_sum.reshape(req_size, row_count, half_width)
+    column, table = lax.optimization_barrier((column, table))
+    row_weights = exchange_table(table)
+    middle = column.shape[0] // 2
+
+    def run(block, weights):
+        return expert_block(block, weights, gains, maps_in, maps_out)
+
+    def over(value, bits):
+        return swap(value.astype(jnp.bfloat16), "exp", bits).astype(jnp.float32)
+
+    near_x = swap(column, "exp", 1)
+    near_y = swap(column, "exp", 2)
+    far_top = swap(near_x[:middle], "exp", 2)
+    far_low = swap(near_y[middle:], "exp", 1)
+    own = run(column, row_weights[0])
+    for_x = run(near_x, row_weights[1])
+    for_y = run(near_y, row_weights[2])
+    top = own[:middle] + over(for_x[:middle], 1)
+    low = own[middle:] + over(for_y[middle:], 2)
+    far = run(jnp.concatenate([far_top, far_low], axis=0), row_weights[3])
+    top = top + over(for_y[:middle] + over(far[:middle], 1), 2)
+    low = low + over(for_x[middle:] + over(far[middle:], 2), 1)
+    plane_sum = jnp.concatenate([top, low], axis=0).reshape(req_size, row_count, half_width)
     mixture = plane_sum[0]
     outgoing = plane_sum.astype(jnp.bfloat16)
     for s in range(1, req_size):
@@ -494,7 +515,7 @@
     groups = lax.axis_size("req") * exp_size
     experts_all = expert_in.shape[0] * groups
     capacity = max(2, 2 * row_count * route_ids.shape[1] // experts_all)
-    dense = capacity >= row_count and experts_all == groups
+    dense = capacity >= row_count and experts_all == groups and exp_size == 4
 
     pieces = gather_blocks(queries, "exp")
     local_lengths = jnp.clip(lengths - exp_at * span, 0, span)
@@ -502,21 +523,23 @@
     weight_parts = [take_block(split_weight, targets[0])] + [
         shift(take_block(split_weight, targets[s]), "exp", s) for s in range(1, exp_size)
     ]
+    messages = attend(
+        pieces, sources, new_keys, new_values, key_cache, value_cache, local_lengths,
+        512, 256, exp_size,
+    )
+    received = [take_block(messages, targets[0])] + [
+        shift(take_block(messages, targets[s]), "exp", s) for s in range(1, exp_size)
+    ]
     if dense:
-        row_weights = route_table(route_ids, route_weights)
+        table = route_table(route_ids, route_weights)
         maps_in = halves(expert_in[0].reshape(model_width, -1), half_width, 0)
         maps_out = halves(expert_out[0], half_width, 1)
         gains = halves(norm_gain, half_width, 0)
-        pieces, row_weights, maps_in, maps_out = lax.optimization_barrier(
-            (pieces, row_weights, maps_in, maps_out)
+        own_message = received[0]
+        own_message, maps_in, maps_out = lax.optimization_barrier(
+            (own_message, maps_in, maps_out)
         )
-    messages = attend(
-        pieces, sources, new_keys, new_values, key_cache, value_cache, local_lengths,
-        512, 256, exp_size,
-    )
-    received = [take_block(messages, targets[0])] + [
-        shift(take_block(messages, targets[s]), "exp", s) for s in range(1, exp_size)
-    ]
+        received = [own_message] + received[1:]
     group_shift = (head_size - (exp_at * share) % group) % head_size
     info = jnp.concatenate([jnp.stack([group_shift, head_at]).astype(jnp.int32), sources])
     kept, sent = merge_project(received, weight_parts, info, share, requests)
@@ -530,7 +553,7 @@
         hidden = hidden + shift(take_block(outgoing, targets[s]), "exp", s).astype(jnp.float32)
 
     if dense:
-        mixture = dense_experts(hidden, row_weights, gains, maps_in, maps_out)
+        mixture = dense_experts(hidden, table, gains, maps_in, maps_out)
     else:
         mixture = sparse_experts(
             hidden, route_ids, route_weights, norm_gain, expert_in, expert_out, capacity

time: 197 us -> 186 us (0.944)
  waiting for transfers between devices: 77.8 us -> 50.8 us
  starting transfers between devices: 47.6 us -> 52.8 us
  other arithmetic: 6.99 us -> 11.8 us
  matrix products: 8.7 us -> 12.7 us
  local copies, waits for them, and re-layouts: 14.9 us -> 17.4 us
    ppermute x33 -> x19, waiting for transfers between devices: 77.8 us -> 29.8 us  [shift(): lax.ppermute(value, axis, [(i, (i + step) % size) for i in range(size)])]
    ppermute x0 -> x18, waiting for transfers between devices: none -> 14.5 us  [swap(): return lax.ppermute(value, axis, [(i, i ^ bits) for i in range(size)])]
    ppermute x0 -> x18, starting transfers between devices: none -> 11.4 us  [swap(): return lax.ppermute(value, axis, [(i, i ^ bits) for i in range(size)])]
    ppermute x33 -> x19, starting transfers between devices: 42.6 us -> 35.3 us  [shift(): lax.ppermute(value, axis, [(i, (i + step) % size) for i in range(size)])]
    all_to_all x1, waiting for transfers between devices: 0.01 us -> 6.41 us  [exchange_table(): lax.all_to_all(table, ('req', 'exp'), split_axis=0, concat_axis=0, tiled=...]
    reduce_sum x8, other arithmetic: 1.46 us -> 5.62 us  [expert_block(): squares = sum((jnp.sum(x * x, axis=-1, keepdims=True) for x in wide))]
    dot_general x16, matrix products: 8.7 us -> 12.7 us  [the longest x8 9.16 us: expert_block(): jnp.dot((x * factor * gain).astype(jnp.bfloat16), maps, preferred_element...]
    slice x1 -> x6, local copies, waits for them, and re-layouts: 0.01 us -> 2.16 us  [the longest x1 1.09 us: dense_experts(): far_top = swap(near_x[:middle], 'exp', 2)]
  transfers between devices with their start and end apart: 34 -> 38, of which waited for: 14 -> 15; matrix products, arithmetic and copies ran while one was open for 13% -> 20% of each run, Pallas kernels for 18% -> 19%
where the time goes in v1:
time: 186 us; the launch traced here: 187 us
  starting transfers between devices  52.8 us (28%)
  waiting for transfers between devices  50.8 us (27%)
  Pallas kernels  40.9 us (22%)
  local copies, waits for them, and re-layouts  17.4 us (9%)
  matrix products  12.7 us (7%)
  other arithmetic  11.8 us (6%)
    pallas_call x1, Pallas kernels, attend(): pl.pallas_call(functools.partial(attend_kernel, pieces, sub, tail, factor...  35.9 us
    ppermute x19, starting transfers between devices, shift(): lax.ppermute(value, axis, [(i, (i + step) % size) for i in range(size)])  35.3 us
    ppermute x19, waiting for transfers between devices, shift(): lax.ppermute(value, axis, [(i, (i + step) % size) for i in range(size)])  29.8 us
    ppermute x18, waiting for transfers between devices, swap(): return lax.ppermute(value, axis, [(i, i ^ bits) for i in range(size)])  14.5 us
    ppermute x18, starting transfers between devices, swap(): return lax.ppermute(value, axis, [(i, i ^ bits) for i in range(size)])  11.4 us
    dot_general x8, matrix products, expert_block(): jnp.dot((x * factor * gain).astype(jnp.bfloat16), maps, preferred_element...  9.16 us
    all_to_all x1, waiting for transfers between devices, exchange_table(): lax.all_to_all(table, ('req', 'exp'), split_axis=0, concat_axis=0, tiled=...  6.41 us
    all_to_all x1, starting transfers between devices, exchange_table(): lax.all_to_all(table, ('req', 'exp'), split_axis=0, concat_axis=0, tiled=...  6.13 us
  transfers between devices with their start and end apart: 38, of which 15 were waited for; matrix products, arithmetic and copies ran while one was open for 20% of the time, Pallas kernels for 19%

profile of v1, /device:TPU:0, one launch (start us, length us, event | category | flops | bytes accessed | tf_op | source)
XLA Modules:
  0.0 186.9 jit_solution(18100408455732343901)
XLA Ops:
  0.0 3.0 %collective-permute-start = (bf16[4,16,16,128]{3,2,1,0:T(8,128)(2,1)}, bf16[4,16,16,128]{3,2,1,0:T(8,128)(2,1)S(1)}, u32[]{:S(2)}, u32[]{:S(2)}) collective-permute-start(bf16[4,16,16,128]{3,2,1,0:T(8,128)(2,1)} %refs_0_.1), channel_id=1, source_target_pairs={{0,1},{1,2},{2,3},{3,0},{4,5},{5,6},{6,7},{7,4},{8,9},{9,10},{10,1... | collective-permute-start | bytes 786440 | tf_op jit(solution)/shard_map/ppermute | solution.py:340
  3.0 1.5 collective-permute-start.1
  4.5 1.4 collective-permute-start.2
  5.9 2.9 %dynamic-slice_bitcast_fusion.2 = (bf16[512,512]{1,0:T(8,128)(2,1)}, bf16[512,512]{1,0:T(8,128)(2,1)}, bf16[512,512]{1,0:T(8,128)(2,1)}, bf16[512,512]{1,0:T(8,128)(2,1)}) fusion(bf16[4,512,512]{2,1,0:T(8,128)(2,1)} %bitcast.82, s32[]{:T(128)S(6)} %select_n.112, s32[]{:T(128)S(6)} %select_n.110, s32[]{:T(128)S(6)} %select_n.108, s32[]{:T(128)S(6)} %select_n.105), kind=kLoop, calls=%fused_computation.97 | loop fusion | bytes 4194320 | tf_op jit(solution)/shard_map/jit(dynamic_index_in_dim)/squeeze | solution.py:344
  8.9 0.6 collective-permute-start.6
  10.0 4.3 %copy.19 = bf16[256,8,2,384]{3,1,2,0:T(8,128)(2,1)} copy(bf16[256,8,2,384]{3,2,1,0:T(2,128)(2,1)} %bitcast.81) | data formatting | bytes 6291456
  14.3 0.7 pad_add_fusion.1.info_ref
  15.1 1.9 %collective-permute-start.8 = (bf16[512,512]{1,0:T(8,128)(2,1)}, bf16[512,512]{1,0:T(8,128)(2,1)}, u32[]{:S(2)}, u32[]{:S(2)}) collective-permute-start(bf16[512,512]{1,0:T(8,128)(2,1)} %get-tuple-element.27), channel_id=1, source_target_pairs={{0,3},{1,0},{2,1},{3,2},{4,7},{5,4},{6,5},{7,6},{8,11},{9,8},{10,9... | collective-permute-start | bytes 1572872 | tf_op jit(solution)/shard_map/ppermute | solution.py:340
  17.6 35.9 %attend.1 = bf16[4,64,2176]{2,1,0:T(8,128)(2,1)} custom-call(s32[8]{0:T(128)} %pad_add_fusion.1.info_ref, bf16[4,16,16,128]{3,2,1,0:T(8,128)(2,1)} %refs_0_.1, bf16[4,16,16,128]{3,2,1,0:T(8,128)(2,1)} %copy-done.5, bf16[4,16,16,128]{3,2,1,0:T(8,128)(2,1)} %collective-permute-done.1.refs_2_, bf16[4,16,16,128]{3,2,1,0:T(8,128)(2,1)} %collective-permute-done.2.refs_3_, ...), custom_call_target="tpu_custom_call" | custom-call | tf_op jit(solution)/shard_map/attend/pallas_call | solution.py:239
  53.5 2.0 %dynamic-slice_bitcast_fusion.6 = (bf16[64,2176]{1,0:T(8,128)(2,1)S(1)}, bf16[64,2176]{1,0:T(8,128)(2,1)S(1)}, bf16[64,2176]{1,0:T(8,128)(2,1)S(1)}, bf16[64,2176]{1,0:T(8,128)(2,1)}) fusion(bf16[4,64,2176]{2,1,0:T(8,128)(2,1)} %attend.1, s32[]{:T(128)S(6)} %select_n.112, s32[]{:T(128)S(6)} %select_n.110, s32[]{:T(128)S(6)} %select_n.108, s32[]{:T(128)S(6)} %select_n.105), kind=kLoop, calls=%fused_computation.109 | loop fusion | bytes 2228240 | tf_op jit(solution)/shard_map/jit(dynamic_index_in_dim)/squeeze | solution.py:344
  55.5 2.9 %collective-permute-start.5 = (bf16[64,2176]{1,0:T(8,128)(2,1)S(1)}, bf16[64,2176]{1,0:T(8,128)(2,1)S(1)}, u32[]{:S(2)}, u32[]{:S(2)}) collective-permute-start(bf16[64,2176]{1,0:T(8,128)(2,1)S(1)} %get-tuple-element.33), channel_id=1, source_target_pairs={{0,3},{1,0},{2,1},{3,2},{4,7},{5,4},{6,5},{7,6},{8,11},{9,8},{10,9... | collective-permute-start | bytes 835592 | tf_op jit(solution)/shard_map/ppermute | solution.py:340
  58.4 0.7 pad_add_fusion.info_ref
  59.1 3.2 %constant_dynamic-slice_fusion = (bf16[1024,768]{1,0:T(8,128)(2,1)S(1)}, bf16[1024,768]{1,0:T(8,128)(2,1)}) fusion(bf16[2048,768]{1,0:T(8,128)(2,1)} %bitcast.78, s32[]{:T(128)S(6)} %select_n.106, s32[]{:T(128)S(6)} %select_n.100), kind=kLoop, calls=%fused_computation.128 | loop fusion | bytes 6291464 | tf_op jit(solution)/shard_map/dynamic_slice | solution.py:380
  62.3 3.6 %collective-permute-done.3.refs_1_ = bf16[64,2176]{1,0:T(8,128)(2,1)S(1)} collective-permute-done((bf16[64,2176]{1,0:T(8,128)(2,1)S(1)}, bf16[64,2176]{1,0:T(8,128)(2,1)S(1)}, u32[]{:S(2)}, u32[]{:S(2)}) %collective-permute-start.3) | collective-permute-done | bytes 278560 | tf_op jit(solution)/shard_map/ppermute | solution.py:340
  65.9 3.4 %collective-permute-done.4.refs_2_ = bf16[64,2176]{1,0:T(8,128)(2,1)S(1)} collective-permute-done((bf16[64,2176]{1,0:T(8,128)(2,1)S(1)}, bf16[64,2176]{1,0:T(8,128)(2,1)S(1)}, u32[]{:S(2)}, u32[]{:S(2)}) %collective-permute-start.4) | collective-permute-done | bytes 278560 | tf_op jit(solution)/shard_map/ppermute | solution.py:340
  69.3 0.7 copy-done.3
  70.0 0.7 copy-done.4
  70.8 5.1 %merge_project.1 = (f32[256,1024]{1,0:T(8,128)}, bf16[256,1024]{1,0:T(8,128)(2,1)}) custom-call(s32[6]{0:T(128)} %pad_add_fusion.info_ref, bf16[64,2176]{1,0:T(8,128)(2,1)} %get-tuple-element.14.refs_0_, bf16[64,2176]{1,0:T(8,128)(2,1)} %copy-done.2, bf16[64,2176]{1,0:T(8,128)(2,1)} %copy-done.3, bf16[64,2176]{1,0:T(8,128)(2,1)} %copy-done.4, ...), custom_call_target="tpu_custom_call" | custom-call | tf_op jit(solution)/shard_map/merge_project/pallas_call | solution.py:320
  76.1 2.0 %collective-permute-done.9 = bf16[256,1024]{1,0:T(8,128)(2,1)} collective-permute-done((bf16[256,1024]{1,0:T(8,128)(2,1)}, bf16[256,1024]{1,0:T(8,128)(2,1)}, u32[]{:S(2)}, u32[]{:S(2)}) %collective-permute-start.9) | collective-permute-done | bytes 524320 | tf_op jit(solution)/shard_map/ppermute | solution.py:340
  78.1 1.5 convert_add_fusion.3
  79.7 1.5 collective-permute-start.10
  81.3 1.8 collective-permute-start.11
  83.6 3.5 %collective-permute-done.10 = bf16[64,1024]{1,0:T(8,128)(2,1)S(1)} collective-permute-done((bf16[64,1024]{1,0:T(8,128)(2,1)S(1)}, bf16[64,1024]{1,0:T(8,128)(2,1)S(1)}, u32[]{:S(2)}, u32[]{:S(2)}) %collective-permute-start.10) | collective-permute-done | bytes 131104 | tf_op jit(solution)/shard_map/ppermute | solution.py:340
  87.1 2.0 %collective-permute-done.11 = bf16[64,1024]{1,0:T(8,128)(2,1)S(1)} collective-permute-done((bf16[64,1024]{1,0:T(8,128)(2,1)S(1)}, bf16[64,1024]{1,0:T(8,128)(2,1)S(1)}, u32[]{:S(2)}, u32[]{:S(2)}) %collective-permute-start.11) | collective-permute-done | bytes 131104 | tf_op jit(solution)/shard_map/ppermute | solution.py:340
  89.5 13.1 %collective-permute-start.14 = (bf16[64,1024]{1,0:T(8,128)(2,1)S(1)}, bf16[64,1024]{1,0:T(8,128)(2,1)S(1)}, u32[]{:S(2)}, u32[]{:S(2)}) collective-permute-start(bf16[64,1024]{1,0:T(8,128)(2,1)S(1)} %get-tuple-element.23), channel_id=1, source_target_pairs={{0,16},{8,24},{16,0},{24,8},{1,17},{9,25},{17,1},{25,9},{2,18},{10... | collective-permute-start | bytes 393224 | tf_op jit(solution)/shard_map/ppermute | solution.py:340
  102.6 0.6 select_reduce_fusion
  103.2 3.2 %collective-permute-done.13 = bf16[64,1024]{1,0:T(8,128)(2,1)S(1)} collective-permute-done((bf16[64,1024]{1,0:T(8,128)(2,1)S(1)}, bf16[64,1024]{1,0:T(8,128)(2,1)S(1)}, u32[]{:S(2)}, u32[]{:S(2)}) %collective-permute-start.13) | collective-permute-done | bytes 131104 | tf_op jit(solution)/shard_map/ppermute | solution.py:340
  106.4 4.9 %collective-permute-done.14 = bf16[64,1024]{1,0:T(8,128)(2,1)S(1)} collective-permute-done((bf16[64,1024]{1,0:T(8,128)(2,1)S(1)}, bf16[64,1024]{1,0:T(8,128)(2,1)S(1)}, u32[]{:S(2)}, u32[]{:S(2)}) %collective-permute-start.14) | collective-permute-done | bytes 131104 | tf_op jit(solution)/shard_map/ppermute | solution.py:340
  111.4 0.8 pad_maximum_fusion
  112.2 0.8 collective-permute-start.22
  113.0 0.7 collective-permute-start.18
  113.7 6.1 %all-to-all-start = ((f32[16,1,64]{2,1,0:T(1,128)}), f32[16,1,64]{2,1,0:T(1,128)S(1)}, u32[]{:S(2)}, u32[]{:S(2)}) async-start(f32[16,1,64]{2,1,0:T(1,128)} %bitcast.23), calls=%async_computation | async-start | bytes 16384 | tf_op jit(solution)/shard_map/all_to_all | solution.py:370
  119.8 1.2 fusion.4
  121.0 6.4 %all-to-all-done = f32[16,1,64]{2,1,0:T(1,128)S(1)} async-done(((f32[16,1,64]{2,1,0:T(1,128)}), f32[16,1,64]{2,1,0:T(1,128)S(1)}, u32[]{:S(2)}, u32[]{:S(2)}) %all-to-all-start) | async-done | bytes 4128 | tf_op jit(solution)/shard_map/all_to_all | solution.py:370
  128.4 1.1 slice.134
  129.5 0.9 collective-permute-start.25
  130.4 1.0 slice.135
  131.3 1.0 collective-permute-start.26
  132.3 1.2 fusion.7
  133.6 1.7 fusion.42
  135.2 1.7 convolution_add_fusion.2
  138.1 1.2 fusion.16
  139.4 1.2 fusion.10
  141.5 1.7 fusion.36
  143.2 0.6 convolution_add_fusion
  144.8 1.7 fusion.39
  146.4 0.6 convolution_add_fusion.1
  147.4 0.6 fusion.28
  148.0 0.6 fusion.32
  150.8 1.4 collective-permute-start.32
  152.8 1.0 collective-permute-start.29
  153.8 0.8 collective-permute-start.33
  155.1 1.0 collective-permute-start.21
  156.1 5.9 %collective-permute-done.29 = bf16[128,1024]{1,0:T(8,128)(2,1)S(1)} collective-permute-done((bf16[128,1024]{1,0:T(8,128)(2,1)S(1)}, bf16[128,1024]{1,0:T(8,128)(2,1)S(1)}, u32[]{:S(2)}, u32[]{:S(2)}) %collective-permute-start.29) | collective-permute-done | bytes 262176 | tf_op jit(solution)/shard_map/ppermute | solution.py:353
  162.1 0.7 collective-permute-start.30
  162.8 2.9 %collective-permute-done.33 = bf16[128,1024]{1,0:T(8,128)(2,1)S(1)} collective-permute-done((bf16[128,1024]{1,0:T(8,128)(2,1)S(1)}, bf16[128,1024]{1,0:T(8,128)(2,1)S(1)}, u32[]{:S(2)}, u32[]{:S(2)}) %collective-permute-start.33) | collective-permute-done | bytes 262176 | tf_op jit(solution)/shard_map/ppermute | solution.py:353
  165.7 1.2 collective-permute-start.34
  167.4 3.4 %collective-permute-done.30 = bf16[128,1024]{1,0:T(8,128)(2,1)S(1)} collective-permute-done((bf16[128,1024]{1,0:T(8,128)(2,1)S(1)}, bf16[128,1024]{1,0:T(8,128)(2,1)S(1)}, u32[]{:S(2)}, u32[]{:S(2)}) %collective-permute-start.30) | collective-permute-done | bytes 262176 | tf_op jit(solution)/shard_map/ppermute | solution.py:353
  170.8 2.3 %collective-permute-done.34 = bf16[128,1024]{1,0:T(8,128)(2,1)S(1)} collective-permute-done((bf16[128,1024]{1,0:T(8,128)(2,1)S(1)}, bf16[128,1024]{1,0:T(8,128)(2,1)S(1)}, u32[]{:S(2)}, u32[]{:S(2)}) %collective-permute-start.34) | collective-permute-done | bytes 262176 | tf_op jit(solution)/shard_map/ppermute | solution.py:353
  173.3 2.4 %collective-permute-start.35 = (bf16[64,1024]{1,0:T(8,128)(2,1)S(1)}, bf16[64,1024]{1,0:T(8,128)(2,1)S(1)}, u32[]{:S(2)}, u32[]{:S(2)}) collective-permute-start(bf16[64,1024]{1,0:T(8,128)(2,1)S(1)} %get-tuple-element.44), channel_id=1, source_target_pairs={{0,16},{8,24},{16,0},{24,8},{1,17},{9,25},{17,1},{25,9},{2,18},{10... | collective-permute-start | bytes 393224 | tf_op jit(solution)/shard_map/ppermute | solution.py:340
  175.7 1.1 collective-permute-start.36
  176.8 2.8 %collective-permute-start.31 = (bf16[64,1024]{1,0:T(8,128)(2,1)S(1)}, bf16[64,1024]{1,0:T(8,128)(2,1)S(1)}, u32[]{:S(2)}, u32[]{:S(2)}) collective-permute-start(bf16[64,1024]{1,0:T(8,128)(2,1)S(1)} %slice.192), channel_id=1, source_target_pairs={{0,24},{8,0},{16,8},{24,16},{1,25},{9,1},{17,9},{25,17},{2,26},{10... | collective-permute-start | bytes 393224 | tf_op jit(solution)/shard_map/ppermute | solution.py:340
  179.6 6.6 %collective-permute-done.35 = bf16[64,1024]{1,0:T(8,128)(2,1)S(1)} collective-permute-done((bf16[64,1024]{1,0:T(8,128)(2,1)S(1)}, bf16[64,1024]{1,0:T(8,128)(2,1)S(1)}, u32[]{:S(2)}, u32[]{:S(2)}) %collective-permute-start.35) | collective-permute-done | bytes 131104 | tf_op jit(solution)/shard_map/ppermute | solution.py:340
  186.2 0.7 fusion.72
  (111 shorter events, 10.8 us)
Async XLA Ops:
  0.0 15.1 %collective-permute-start = (bf16[4,16,16,128]{3,2,1,0:T(8,128)(2,1)}, bf16[4,16,16,128]{3,2,1,0:T(8,128)(2,1)S(1)}, u32[]{:S(2)}, u32[]{:S(2)}) collective-permute-start(bf16[4,16,16,128]{3,2,1,0:T(8,128)(2,1)} %refs_0_.1), channel_id=1, source_target_pairs={{0,1},{1,2},{2,3},{3,0},{4,5},{5,6},{6,7},{7,4},{8,9},{9,10},{10,1... | collective-permute-start | bytes 786440 | tf_op jit(solution)/shard_map/ppermute | solution.py:340
  3.0 14.1 %collective-permute-start.1 = (bf16[4,16,16,128]{3,2,1,0:T(8,128)(2,1)}, bf16[4,16,16,128]{3,2,1,0:T(8,128)(2,1)}, u32[]{:S(2)}, u32[]{:S(2)}) collective-permute-start(bf16[4,16,16,128]{3,2,1,0:T(8,128)(2,1)} %refs_0_.1), channel_id=1, source_target_pairs={{0,2},{1,3},{2,0},{3,1},{4,6},{5,7},{6,4},{7,5},{8,10},{9,11},{10,... | collective-permute-start | bytes 786440 | tf_op jit(solution)/shard_map/ppermute | solution.py:340
  4.5 13.1 %collective-permute-start.2 = (bf16[4,16,16,128]{3,2,1,0:T(8,128)(2,1)}, bf16[4,16,16,128]{3,2,1,0:T(8,128)(2,1)}, u32[]{:S(2)}, u32[]{:S(2)}) collective-permute-start(bf16[4,16,16,128]{3,2,1,0:T(8,128)(2,1)} %refs_0_.1), channel_id=1, source_target_pairs={{0,3},{1,0},{2,1},{3,2},{4,7},{5,4},{6,5},{7,6},{8,11},{9,8},{10,9... | collective-permute-start | bytes 786440 | tf_op jit(solution)/shard_map/ppermute | solution.py:340
  8.9 46.6 %collective-permute-start.6 = (bf16[512,512]{1,0:T(8,128)(2,1)}, bf16[512,512]{1,0:T(8,128)(2,1)}, u32[]{:S(2)}, u32[]{:S(2)}) collective-permute-start(bf16[512,512]{1,0:T(8,128)(2,1)} %get-tuple-element.29), channel_id=1, source_target_pairs={{0,1},{1,2},{2,3},{3,0},{4,5},{5,6},{6,7},{7,4},{8,9},{9,10},{10,1... | collective-permute-start | bytes 1572872 | tf_op jit(solution)/shard_map/ppermute | solution.py:340
  9.4 52.9 %collective-permute-start.7 = (bf16[512,512]{1,0:T(8,128)(2,1)}, bf16[512,512]{1,0:T(8,128)(2,1)}, u32[]{:S(2)}, u32[]{:S(2)}) collective-permute-start(bf16[512,512]{1,0:T(8,128)(2,1)} %get-tuple-element.28), channel_id=1, source_target_pairs={{0,2},{1,3},{2,0},{3,1},{4,6},{5,7},{6,4},{7,5},{8,10},{9,11},{10,... | collective-permute-start | bytes 1572872 | tf_op jit(solution)/shard_map/ppermute | solution.py:340
  10.0 4.3 %copy-start.10 = (s32[4]{0:T(128)S(1)}, s32[4]{0:T(128)}, u32[]{:S(2)}) copy-start(s32[4]{0:T(128)} %param.18) | copy-start | bytes 52
  10.0 5.0 %copy-start.1 = (bf16[1,384,2048]{2,1,0:T(8,128)(2,1)S(1)}, bf16[1,384,2048]{2,1,0:T(8,128)(2,1)}, u32[]{:S(2)}) copy-start(bf16[1,384,2048]{2,1,0:T(8,128)(2,1)} %param.25) | copy-start | bytes 4718596
  15.1 2.5 %copy-start.5 = (bf16[4,16,16,128]{3,2,1,0:T(8,128)(2,1)}, bf16[4,16,16,128]{3,2,1,0:T(8,128)(2,1)S(1)}, u32[]{:S(2)}) copy-start(bf16[4,16,16,128]{3,2,1,0:T(8,128)(2,1)S(1)} %collective-permute-done.refs_1_) | copy-start | bytes 786436
  15.1 47.2 %collective-permute-start.8 = (bf16[512,512]{1,0:T(8,128)(2,1)}, bf16[512,512]{1,0:T(8,128)(2,1)}, u32[]{:S(2)}, u32[]{:S(2)}) collective-permute-start(bf16[512,512]{1,0:T(8,128)(2,1)} %get-tuple-element.27), channel_id=1, source_target_pairs={{0,3},{1,0},{2,1},{3,2},{4,7},{5,4},{6,5},{7,6},{8,11},{9,8},{10,9... | collective-permute-start | bytes 1572872 | tf_op jit(solution)/shard_map/ppermute | solution.py:340
  55.5 10.4 %collective-permute-start.3 = (bf16[64,2176]{1,0:T(8,128)(2,1)S(1)}, bf16[64,2176]{1,0:T(8,128)(2,1)S(1)}, u32[]{:S(2)}, u32[]{:S(2)}) collective-permute-start(bf16[64,2176]{1,0:T(8,128)(2,1)S(1)} %get-tuple-element.35), channel_id=1, source_target_pairs={{0,1},{1,2},{2,3},{3,0},{4,5},{5,6},{6,7},{7,4},{8,9},{9,10},{10,1... | collective-permute-start | bytes 835592 | tf_op jit(solution)/shard_map/ppermute | solution.py:340
  55.5 13.8 %collective-permute-start.4 = (bf16[64,2176]{1,0:T(8,128)(2,1)S(1)}, bf16[64,2176]{1,0:T(8,128)(2,1)S(1)}, u32[]{:S(2)}, u32[]{:S(2)}) collective-permute-start(bf16[64,2176]{1,0:T(8,128)(2,1)S(1)} %get-tuple-element.34), channel_id=1, source_target_pairs={{0,2},{1,3},{2,0},{3,1},{4,6},{5,7},{6,4},{7,5},{8,10},{9,11},{10,... | collective-permute-start | bytes 835592 | tf_op jit(solution)/shard_map/ppermute | solution.py:340
  55.5 13.8 %collective-permute-start.5 = (bf16[64,2176]{1,0:T(8,128)(2,1)S(1)}, bf16[64,2176]{1,0:T(8,128)(2,1)S(1)}, u32[]{:S(2)}, u32[]{:S(2)}) collective-permute-start(bf16[64,2176]{1,0:T(8,128)(2,1)S(1)} %get-tuple-element.33), channel_id=1, source_target_pairs={{0,3},{1,0},{2,1},{3,2},{4,7},{5,4},{6,5},{7,6},{8,11},{9,8},{10,9... | collective-permute-start | bytes 835592 | tf_op jit(solution)/shard_map/ppermute | solution.py:340
  65.9 4.8 %copy-start.2 = (bf16[64,2176]{1,0:T(8,128)(2,1)}, bf16[64,2176]{1,0:T(8,128)(2,1)S(1)}, u32[]{:S(2)}) copy-start(bf16[64,2176]{1,0:T(8,128)(2,1)S(1)} %collective-permute-done.3.refs_1_) | copy-start | bytes 835588
  69.3 0.7 copy-start.3
  70.0 0.7 copy-start.4
  75.8 2.3 %collective-permute-start.9 = (bf16[256,1024]{1,0:T(8,128)(2,1)}, bf16[256,1024]{1,0:T(8,128)(2,1)}, u32[]{:S(2)}, u32[]{:S(2)}) collective-permute-start(bf16[256,1024]{1,0:T(8,128)(2,1)} %get-tuple-element.16), channel_id=1, source_target_pairs={{0,4},{4,0},{1,5},{5,1},{2,6},{6,2},{3,7},{7,3},{8,12},{12,8},{9,1... | collective-permute-start | bytes 1572872 | tf_op jit(solution)/shard_map/ppermute | solution.py:340
  79.6 4.0 %copy-start.7 = (f32[2048]{0:T(1024)S(1)}, f32[2048]{0:T(1024)}, u32[]{:S(2)}) copy-start(f32[2048]{0:T(1024)} %param.21) | copy-start | bytes 24580
  79.6 9.5 %copy-start.6 = (bf16[64,2048]{1,0:T(8,128)(2,1)S(1)}, bf16[64,2048]{1,0:T(8,128)(2,1)}, u32[]{:S(2)}) copy-start(bf16[64,2048]{1,0:T(8,128)(2,1)} %param.19) | copy-start | bytes 786436
  79.6 23.0 %copy-start.8 = (f32[64,8]{0,1:T(8,128)S(1)}, f32[64,8]{0,1:T(8,128)}, u32[]{:S(2)}) copy-start(f32[64,8]{0,1:T(8,128)} %param.23) | copy-start | bytes 6148
  79.6 23.0 %copy-start.9 = (s32[64,8]{0,1:T(8,128)S(1)}, s32[64,8]{0,1:T(8,128)}, u32[]{:S(2)}) copy-start(s32[64,8]{0,1:T(8,128)} %param.22) | copy-start | bytes 6148
  79.7 7.4 %collective-permute-start.10 = (bf16[64,1024]{1,0:T(8,128)(2,1)S(1)}, bf16[64,1024]{1,0:T(8,128)(2,1)S(1)}, u32[]{:S(2)}, u32[]{:S(2)}) collective-permute-start(bf16[64,1024]{1,0:T(8,128)(2,1)S(1)} %get-tuple-element.41), channel_id=1, source_target_pairs={{0,1},{1,2},{2,3},{3,0},{4,5},{5,6},{6,7},{7,4},{8,9},{9,10},{10,1... | collective-permute-start | bytes 393224 | tf_op jit(solution)/shard_map/ppermute | solution.py:340
  81.3 7.8 %collective-permute-start.11 = (bf16[64,1024]{1,0:T(8,128)(2,1)S(1)}, bf16[64,1024]{1,0:T(8,128)(2,1)S(1)}, u32[]{:S(2)}, u32[]{:S(2)}) collective-permute-start(bf16[64,1024]{1,0:T(8,128)(2,1)S(1)} %get-tuple-element.43), channel_id=1, source_target_pairs={{0,2},{1,3},{2,0},{3,1},{4,6},{5,7},{6,4},{7,5},{8,10},{9,11},{10,... | collective-permute-start | bytes 393224 | tf_op jit(solution)/shard_map/ppermute | solution.py:340
  83.0 6.0 %collective-permute-start.12 = (bf16[64,1024]{1,0:T(8,128)(2,1)S(1)}, bf16[64,1024]{1,0:T(8,128)(2,1)S(1)}, u32[]{:S(2)}, u32[]{:S(2)}) collective-permute-start(bf16[64,1024]{1,0:T(8,128)(2,1)S(1)} %get-tuple-element.42), channel_id=1, source_target_pairs={{0,3},{1,0},{2,1},{3,2},{4,7},{5,4},{6,5},{7,6},{8,11},{9,8},{10,9... | collective-permute-start | bytes 393224 | tf_op jit(solution)/shard_map/ppermute | solution.py:340
  89.2 17.3 %collective-permute-start.13 = (bf16[64,1024]{1,0:T(8,128)(2,1)S(1)}, bf16[64,1024]{1,0:T(8,128)(2,1)S(1)}, u32[]{:S(2)}, u32[]{:S(2)}) collective-permute-start(bf16[64,1024]{1,0:T(8,128)(2,1)S(1)} %get-tuple-element.23), channel_id=1, source_target_pairs={{0,8},{8,16},{16,24},{24,0},{1,9},{9,17},{17,25},{25,1},{2,10},{10... | collective-permute-start | bytes 393224 | tf_op jit(solution)/shard_map/ppermute | solution.py:340
  89.5 21.9 %collective-permute-start.14 = (bf16[64,1024]{1,0:T(8,128)(2,1)S(1)}, bf16[64,1024]{1,0:T(8,128)(2,1)S(1)}, u32[]{:S(2)}, u32[]{:S(2)}) collective-permute-start(bf16[64,1024]{1,0:T(8,128)(2,1)S(1)} %get-tuple-element.23), channel_id=1, source_target_pairs={{0,16},{8,24},{16,0},{24,8},{1,17},{9,25},{17,1},{25,9},{2,18},{10... | collective-permute-start | bytes 393224 | tf_op jit(solution)/shard_map/ppermute | solution.py:340
  102.6 8.8 %collective-permute-start.15 = (bf16[64,1024]{1,0:T(8,128)(2,1)S(1)}, bf16[64,1024]{1,0:T(8,128)(2,1)S(1)}, u32[]{:S(2)}, u32[]{:S(2)}) collective-permute-start(bf16[64,1024]{1,0:T(8,128)(2,1)S(1)} %get-tuple-element.23), channel_id=1, source_target_pairs={{0,24},{8,0},{16,8},{24,16},{1,25},{9,1},{17,9},{25,17},{2,26},{10... | collective-permute-start | bytes 393224 | tf_op jit(solution)/shard_map/ppermute | solution.py:340
  112.2 18.2 %collective-permute-start.22 = (bf16[256,1024]{1,0:T(8,128)(2,1)}, bf16[256,1024]{1,0:T(8,128)(2,1)}, u32[]{:S(2)}, u32[]{:S(2)}) collective-permute-start(bf16[256,1024]{1,0:T(8,128)(2,1)} %pad_maximum_fusion), channel_id=1, source_target_pairs={{0,2},{1,3},{2,0},{3,1},{4,6},{5,7},{6,4},{7,5},{8,10},{9,11},{10,... | collective-permute-start | bytes 1572872 | tf_op jit(solution)/shard_map/ppermute | solution.py:353
  113.0 15.4 %collective-permute-start.18 = (bf16[256,1024]{1,0:T(8,128)(2,1)}, bf16[256,1024]{1,0:T(8,128)(2,1)}, u32[]{:S(2)}, u32[]{:S(2)}) collective-permute-start(bf16[256,1024]{1,0:T(8,128)(2,1)} %pad_maximum_fusion), channel_id=1, source_target_pairs={{0,1},{1,0},{2,3},{3,2},{4,5},{5,4},{6,7},{7,6},{8,9},{9,8},{10,11... | collective-permute-start | bytes 1572872 | tf_op jit(solution)/shard_map/ppermute | solution.py:353
  113.7 18.7 %collective-permute-start.16 = (bf16[256,1024]{1,0:T(8,128)(2,1)}, bf16[256,1024]{1,0:T(8,128)(2,1)}, u32[]{:S(2)}, u32[]{:S(2)}) collective-permute-start(bf16[256,1024]{1,0:T(8,128)(2,1)} %pad_maximum_fusion), channel_id=1, source_target_pairs={{0,4},{4,0},{1,5},{5,1},{2,6},{6,2},{3,7},{7,3},{8,12},{12,8},{9,1... | collective-permute-start | bytes 1572872 | tf_op jit(solution)/shard_map/ppermute | solution.py:353
  113.7 13.8 %all-to-all-start = ((f32[16,1,64]{2,1,0:T(1,128)}), f32[16,1,64]{2,1,0:T(1,128)S(1)}, u32[]{:S(2)}, u32[]{:S(2)}) async-start(f32[16,1,64]{2,1,0:T(1,128)} %bitcast.23), calls=%async_computation | async-start | bytes 16384 | tf_op jit(solution)/shard_map/all_to_all | solution.py:370
  128.4 5.1 %copy-start = (bf16[1024,768]{1,0:T(8,128)(2,1)S(1)}, bf16[1024,768]{1,0:T(8,128)(2,1)}, u32[]{:S(2)}) copy-start(bf16[1024,768]{1,0:T(8,128)(2,1)} %get-tuple-element.18) | copy-start | bytes 4718596
  129.5 11.1 %collective-permute-start.25 = (bf16[128,1024]{1,0:T(8,128)(2,1)S(1)}, bf16[128,1024]{1,0:T(8,128)(2,1)S(1)}, u32[]{:S(2)}, u32[]{:S(2)}) collective-permute-start(bf16[128,1024]{1,0:T(8,128)(2,1)S(1)} %slice.134), channel_id=1, source_target_pairs={{0,2},{1,3},{2,0},{3,1},{4,6},{5,7},{6,4},{7,5},{8,10},{9,11},{10,... | collective-permute-start | bytes 786440 | tf_op jit(solution)/shard_map/ppermute | solution.py:353
  131.3 9.3 %collective-permute-start.26 = (bf16[128,1024]{1,0:T(8,128)(2,1)S(1)}, bf16[128,1024]{1,0:T(8,128)(2,1)S(1)}, u32[]{:S(2)}, u32[]{:S(2)}) collective-permute-start(bf16[128,1024]{1,0:T(8,128)(2,1)S(1)} %slice.135), channel_id=1, source_target_pairs={{0,1},{1,0},{2,3},{3,2},{4,5},{5,4},{6,7},{7,6},{8,9},{9,8},{10,11... | collective-permute-start | bytes 786440 | tf_op jit(solution)/shard_map/ppermute | solution.py:353
  137.5 29.5 %collective-permute-start.17 = (bf16[256,1024]{1,0:T(8,128)(2,1)S(1)}, bf16[256,1024]{1,0:T(8,128)(2,1)S(1)}, u32[]{:S(2)}, u32[]{:S(2)}) collective-permute-start(bf16[256,1024]{1,0:T(8,128)(2,1)S(1)} %fusion), channel_id=1, source_target_pairs={{0,4},{4,0},{1,5},{5,1},{2,6},{6,2},{3,7},{7,3},{8,12},{12,8},{9,1... | collective-permute-start | bytes 1572872 | tf_op jit(solution)/shard_map/ppermute | solution.py:353
  137.6 3.8 %collective-permute-start.23 = (bf16[256,1024]{1,0:T(8,128)(2,1)}, bf16[256,1024]{1,0:T(8,128)(2,1)S(1)}, u32[]{:S(2)}, u32[]{:S(2)}) collective-permute-start(bf16[256,1024]{1,0:T(8,128)(2,1)} %collective-permute-done.22), channel_id=1, source_target_pairs={{0,4},{4,0},{1,5},{5,1},{2,6},{6,2},{3,7},{7,3},{8,12},{12,8},{9,1... | collective-permute-start | bytes 1572872 | tf_op jit(solution)/shard_map/ppermute | solution.py:353
  138.1 6.5 %collective-permute-start.19 = (bf16[256,1024]{1,0:T(8,128)(2,1)}, bf16[256,1024]{1,0:T(8,128)(2,1)S(1)}, u32[]{:S(2)}, u32[]{:S(2)}) collective-permute-start(bf16[256,1024]{1,0:T(8,128)(2,1)} %collective-permute-done.18), channel_id=1, source_target_pairs={{0,4},{4,0},{1,5},{5,1},{2,6},{6,2},{3,7},{7,3},{8,12},{12,8},{9,1... | collective-permute-start | bytes 1572872 | tf_op jit(solution)/shard_map/ppermute | solution.py:353
  140.7 6.5 %collective-permute-start.27 = (bf16[256,1024]{1,0:T(8,128)(2,1)S(1)}, bf16[256,1024]{1,0:T(8,128)(2,1)S(1)}, u32[]{:S(2)}, u32[]{:S(2)}) collective-permute-start(bf16[256,1024]{1,0:T(8,128)(2,1)S(1)} %constant_dynamic-update-slice_fusion), channel_id=1, source_target_pairs={{0,4},{4,0},{1,5},{5,1},{2,6},{6,2},{3,7},{7,3},{8,12},{12,8},{9,1... | collective-permute-start | bytes 1572872 | tf_op jit(solution)/shard_map/ppermute | solution.py:353
  144.4 5.9 %collective-permute-start.24 = (bf16[256,1024]{1,0:T(8,128)(2,1)S(1)}, bf16[256,1024]{1,0:T(8,128)(2,1)S(1)}, u32[]{:S(2)}, u32[]{:S(2)}) collective-permute-start(bf16[256,1024]{1,0:T(8,128)(2,1)S(1)} %fusion.2), channel_id=1, source_target_pairs={{0,4},{4,0},{1,5},{5,1},{2,6},{6,2},{3,7},{7,3},{8,12},{12,8},{9,1... | collective-permute-start | bytes 1572872 | tf_op jit(solution)/shard_map/ppermute | solution.py:353
  149.2 3.0 %collective-permute-start.28 = (bf16[256,1024]{1,0:T(8,128)(2,1)S(1)}, bf16[256,1024]{1,0:T(8,128)(2,1)S(1)}, u32[]{:S(2)}, u32[]{:S(2)}) collective-permute-start(bf16[256,1024]{1,0:T(8,128)(2,1)S(1)} %fusion.3), channel_id=1, source_target_pairs={{0,4},{4,0},{1,5},{5,1},{2,6},{6,2},{3,7},{7,3},{8,12},{12,8},{9,1... | collective-permute-start | bytes 1572872 | tf_op jit(solution)/shard_map/ppermute | solution.py:353
  150.2 4.4 %collective-permute-start.20 = (bf16[256,1024]{1,0:T(8,128)(2,1)S(1)}, bf16[256,1024]{1,0:T(8,128)(2,1)S(1)}, u32[]{:S(2)}, u32[]{:S(2)}) collective-permute-start(bf16[256,1024]{1,0:T(8,128)(2,1)S(1)} %fusion.1), channel_id=1, source_target_pairs={{0,4},{4,0},{1,5},{5,1},{2,6},{6,2},{3,7},{7,3},{8,12},{12,8},{9,1... | collective-permute-start | bytes 1572872 | tf_op jit(solution)/shard_map/ppermute | solution.py:353
  150.8 16.6 %collective-permute-start.32 = (bf16[128,1024]{1,0:T(8,128)(2,1)S(1)}, bf16[128,1024]{1,0:T(8,128)(2,1)S(1)}, u32[]{:S(2)}, u32[]{:S(2)}) collective-permute-start(bf16[128,1024]{1,0:T(8,128)(2,1)S(1)} %slice.190), channel_id=1, source_target_pairs={{0,2},{1,3},{2,0},{3,1},{4,6},{5,7},{6,4},{7,5},{8,10},{9,11},{10,... | collective-permute-start | bytes 786440 | tf_op jit(solution)/shard_map/ppermute | solution.py:353
  152.8 9.2 %collective-permute-start.29 = (bf16[128,1024]{1,0:T(8,128)(2,1)S(1)}, bf16[128,1024]{1,0:T(8,128)(2,1)S(1)}, u32[]{:S(2)}, u32[]{:S(2)}) collective-permute-start(bf16[128,1024]{1,0:T(8,128)(2,1)S(1)} %get-tuple-element.40), channel_id=1, source_target_pairs={{0,1},{1,0},{2,3},{3,2},{4,5},{5,4},{6,7},{7,6},{8,9},{9,8},{10,11... | collective-permute-start | bytes 786440 | tf_op jit(solution)/shard_map/ppermute | solution.py:353
  153.8 11.9 %collective-permute-start.33 = (bf16[128,1024]{1,0:T(8,128)(2,1)S(1)}, bf16[128,1024]{1,0:T(8,128)(2,1)S(1)}, u32[]{:S(2)}, u32[]{:S(2)}) collective-permute-start(bf16[128,1024]{1,0:T(8,128)(2,1)S(1)} %get-tuple-element.39), channel_id=1, source_target_pairs={{0,2},{1,3},{2,0},{3,1},{4,6},{5,7},{6,4},{7,5},{8,10},{9,11},{10,... | collective-permute-start | bytes 786440 | tf_op jit(solution)/shard_map/ppermute | solution.py:353
  155.1 12.3 %collective-permute-start.21 = (bf16[128,1024]{1,0:T(8,128)(2,1)S(1)}, bf16[128,1024]{1,0:T(8,128)(2,1)S(1)}, u32[]{:S(2)}, u32[]{:S(2)}) collective-permute-start(bf16[128,1024]{1,0:T(8,128)(2,1)S(1)} %slice.191), channel_id=1, source_target_pairs={{0,1},{1,0},{2,3},{3,2},{4,5},{5,4},{6,7},{7,6},{8,9},{9,8},{10,11... | collective-permute-start | bytes 786440 | tf_op jit(solution)/shard_map/ppermute | solution.py:353
  162.1 8.7 %collective-permute-start.30 = (bf16[128,1024]{1,0:T(8,128)(2,1)S(1)}, bf16[128,1024]{1,0:T(8,128)(2,1)S(1)}, u32[]{:S(2)}, u32[]{:S(2)}) collective-permute-start(bf16[128,1024]{1,0:T(8,128)(2,1)S(1)} %fusion.47), channel_id=1, source_target_pairs={{0,2},{1,3},{2,0},{3,1},{4,6},{5,7},{6,4},{7,5},{8,10},{9,11},{10,... | collective-permute-start | bytes 786440 | tf_op jit(solution)/shard_map/ppermute | solution.py:353
  165.7 7.3 %collective-permute-start.34 = (bf16[128,1024]{1,0:T(8,128)(2,1)S(1)}, bf16[128,1024]{1,0:T(8,128)(2,1)S(1)}, u32[]{:S(2)}, u32[]{:S(2)}) collective-permute-start(bf16[128,1024]{1,0:T(8,128)(2,1)S(1)} %fusion.44), channel_id=1, source_target_pairs={{0,1},{1,0},{2,3},{3,2},{4,5},{5,4},{6,7},{7,6},{8,9},{9,8},{10,11... | collective-permute-start | bytes 786440 | tf_op jit(solution)/shard_map/ppermute | solution.py:353
  173.3 12.8 %collective-permute-start.35 = (bf16[64,1024]{1,0:T(8,128)(2,1)S(1)}, bf16[64,1024]{1,0:T(8,128)(2,1)S(1)}, u32[]{:S(2)}, u32[]{:S(2)}) collective-permute-start(bf16[64,1024]{1,0:T(8,128)(2,1)S(1)} %get-tuple-element.44), channel_id=1, source_target_pairs={{0,16},{8,24},{16,0},{24,8},{1,17},{9,25},{17,1},{25,9},{2,18},{10... | collective-permute-start | bytes 393224 | tf_op jit(solution)/shard_map/ppermute | solution.py:340
  175.7 10.5 %collective-permute-start.36 = (bf16[64,1024]{1,0:T(8,128)(2,1)S(1)}, bf16[64,1024]{1,0:T(8,128)(2,1)S(1)}, u32[]{:S(2)}, u32[]{:S(2)}) collective-permute-start(bf16[64,1024]{1,0:T(8,128)(2,1)S(1)} %get-tuple-element.45), channel_id=1, source_target_pairs={{0,8},{8,16},{16,24},{24,0},{1,9},{9,17},{17,25},{25,1},{2,10},{10... | collective-permute-start | bytes 393224 | tf_op jit(solution)/shard_map/ppermute | solution.py:340
  176.8 9.3 %collective-permute-start.31 = (bf16[64,1024]{1,0:T(8,128)(2,1)S(1)}, bf16[64,1024]{1,0:T(8,128)(2,1)S(1)}, u32[]{:S(2)}, u32[]{:S(2)}) collective-permute-start(bf16[64,1024]{1,0:T(8,128)(2,1)S(1)} %slice.192), channel_id=1, source_target_pairs={{0,24},{8,0},{16,8},{24,16},{1,25},{9,1},{17,9},{25,17},{2,26},{10... | collective-permute-start | bytes 393224 | tf_op jit(solution)/shard_map/ppermute | solution.py:340

commit v2 on v1

--- a/solution.py
+++ b/solution.py
@@ -11,10 +11,12 @@
 norm_epsilon = 1e-06
 
 
-def attend_kernel(pieces, sub, tail, factor, exp_count, info_ref, *refs):
+def attend_kernel(pieces, base, listed, sub, tail, factor, exp_count, info_ref, *refs):
     q_refs = refs[:pieces]
-    nk_ref, nv_ref, k_ref, v_ref, o_ref = refs[pieces : pieces + 5]
-    q_all, q_cat, pattern, m_scr, l_scr, acc, p_even, p_odd, stats, turned = refs[pieces + 5 :]
+    nk_ref, nv_ref, k_ref, v_ref = refs[pieces : pieces + 4]
+    out_refs = refs[pieces + 4 : pieces + 4 + exp_count]
+    scratch = refs[pieces + 4 + exp_count :]
+    q_all, q_cat, pattern, m_scr, l_scr, acc, p_even, p_odd, stats, turned, staged = scratch
     requests = pl.num_programs(0)
     request = pl.program_id(0)
     head_size = k_ref.shape[2]
@@ -23,7 +25,7 @@
     group = heads // kv
     rows = piece_rows * pieces
     lanes = rows * group
-    length = info_ref[request]
+    length = info_ref[request + base]
     even_lane = lax.broadcasted_iota(jnp.int32, (lanes, 128), 1) % 2 == 0
 
     @pl.when(request == 0)
@@ -34,7 +36,7 @@
         pattern[1] = parity.astype(jnp.float32).astype(jnp.bfloat16)
 
     for piece in range(pieces):
-        where_to = info_ref[requests + piece] * piece_rows
+        where_to = info_ref[listed + piece] * piece_rows
         q_all[pl.ds(where_to, piece_rows)] = q_refs[piece][0].astype(jnp.float32)
     for head in range(kv):
         chosen = q_all[:, head * group : (head + 1) * group, :].reshape(lanes, head_size)
@@ -212,7 +214,7 @@
             offset = pl.multiple_of(
                 request * (share * head_size) + inside * head_size, head_size
             )
-            o_ref[target, :, pl.ds(offset, head_size)] = turned[
+            staged[target, :, pl.ds(offset, head_size)] = turned[
                 pl.ds(member, rows, stride=group), :
             ].astype(jnp.bfloat16)
 
@@ -220,13 +222,15 @@
     def _():
         for target in range(exp_count):
             head = target * share // group
-            o_ref[target, :, requests * share * head_size :] = stats[head].astype(jnp.bfloat16)
-
-
-def attend(queries, order, new_keys, new_values, keys, values, local_lengths, sub, tail, exp_count):
-    requests, span, kv, head_size = keys.shape
-    piece_rows, heads = queries[0].shape[1:3]
-    pieces = len(queries)
+            staged[target, :, requests * share * head_size :] = stats[head].astype(jnp.bfloat16)
+        for step_away in range(exp_count):
+            out_refs[step_away][...] = staged[info_ref[listed + (-step_away) % exp_count]]
+
+
+def attend(queries, order, new_keys, new_values, keys, values, local_lengths, base, sub, tail):
+    listed, span, kv, head_size = keys.shape
+    requests, piece_rows, heads = queries[0].shape[:3]
+    pieces = exp_count = len(queries)
     rows = piece_rows * pieces
     share = heads // exp_count
     fresh = new_keys.shape[1]
@@ -234,10 +238,10 @@
     info = jnp.concatenate([local_lengths, order])
     factor = head_size ** (-0.5) * math.log2(math.e)
     lanes = rows * heads // kv
-    flat = lambda x: x.reshape(requests, x.shape[1] * kv, head_size)
-    block = lambda n: pl.BlockSpec((1, n, head_size), lambda r, info: (r, 0, 0))
+    flat = lambda x: x.reshape(listed, x.shape[1] * kv, head_size)
+    block = lambda n: pl.BlockSpec((1, n, head_size), lambda r, info: (r + base, 0, 0))
     return pl.pallas_call(
-        functools.partial(attend_kernel, pieces, sub, tail, factor, exp_count),
+        functools.partial(attend_kernel, pieces, base, listed, sub, tail, factor, exp_count),
         grid_spec=pltpu.PrefetchScalarGridSpec(
             num_scalar_prefetch=1,
             grid=(requests,),
@@ -246,7 +250,7 @@
             ]
             * pieces
             + [block(fresh * kv), block(fresh * kv), block(span * kv), block(span * kv)],
-            out_specs=pl.BlockSpec((exp_count, rows, width), lambda r, info: (0, 0, 0)),
+            out_specs=[pl.BlockSpec((rows, width), lambda r, info: (0, 0))] * exp_count,
             scratch_shapes=[
                 pltpu.VMEM((rows, heads, head_size), jnp.float32),
                 pltpu.VMEM((lanes, kv * head_size), jnp.bfloat16),
@@ -254,47 +258,50 @@
                 pltpu.VMEM((lanes, 128), jnp.float32),
                 pltpu.VMEM((lanes, 128), jnp.float32),
                 pltpu.VMEM((lanes, kv * head_size), jnp.float32),
-                pltpu.VMEM((lanes, 2 * sub * kv), jnp.bfloat16),
+                pltpu.VMEM((lanes, sub * kv), jnp.bfloat16),
                 pltpu.VMEM((lanes, sub * kv), jnp.bfloat16),
                 pltpu.VMEM((kv, rows, head_size), jnp.float32),
                 pltpu.VMEM((lanes, head_size), jnp.float32),
+                pltpu.VMEM((exp_count, rows, width), jnp.bfloat16),
             ],
         ),
-        out_shape=jax.ShapeDtypeStruct((exp_count, rows, width), jnp.bfloat16),
+        out_shape=[jax.ShapeDtypeStruct((rows, width), jnp.bfloat16)] * exp_count,
         compiler_params=pltpu.CompilerParams(dimension_semantics=("arbitrary",)),
         name="attend",
     )(info, *queries, flat(new_keys), flat(new_values), flat(keys), flat(values))
 
 
-def merge_kernel(parts, share, info_ref, *refs):
-    x_refs = refs[:parts]
-    w_refs = refs[parts : 2 * parts]
-    keep_ref, send_ref, attn = refs[2 * parts :]
-    rows, width = x_refs[0].shape
+def merge_kernel(parts, batches, share, info_ref, *refs):
+    w_refs = refs[batches * parts : (batches + 1) * parts]
+    keep_ref, send_ref, attn = refs[(batches + 1) * parts :]
+    rows, width = refs[0].shape
     head_size = 128
     requests = (width - head_size) // (share * head_size)
     group_shift = info_ref[0]
     half = info_ref[1]
-    tables = []
-    for x_ref in x_refs:
-        table = x_ref[:, width - head_size :].astype(jnp.float32)
-        tables.append(pltpu.roll(table, group_shift, 1))
-    for request in range(requests):
-        for member in range(share):
-            at = 24 * request + member
-            tops = [t[:, at + 8 : at + 9] for t in tables]
-            sums = [t[:, at : at + 1] + t[:, at + 16 : at + 17] for t in tables]
-            top = functools.reduce(jnp.maximum, tops)
-            weights = [s * jnp.exp2(m - top) for s, m in zip(sums, tops)]
-            inverse = 1.0 / functools.reduce(jnp.add, weights)
-            start = (request * share + member) * head_size
-            mixed = jnp.zeros((rows, head_size), jnp.float32)
-            for weight, x_ref in zip(weights, x_refs):
-                part = x_ref[:, start : start + head_size].astype(jnp.float32)
-                mixed = mixed + jnp.broadcast_to(weight * inverse, part.shape) * part
-            attn[
-                request * rows : (request + 1) * rows, member * head_size : (member + 1) * head_size
-            ] = mixed.astype(jnp.bfloat16)
+    for batch in range(batches):
+        x_refs = refs[batch * parts : (batch + 1) * parts]
+        tables = []
+        for x_ref in x_refs:
+            table = x_ref[:, width - head_size :].astype(jnp.float32)
+            tables.append(pltpu.roll(table, group_shift, 1))
+        for request in range(requests):
+            first = (batch * requests + request) * rows
+            for member in range(share):
+                at = 24 * request + member
+                tops = [t[:, at + 8 : at + 9] for t in tables]
+                sums = [t[:, at : at + 1] + t[:, at + 16 : at + 17] for t in tables]
+                top = functools.reduce(jnp.maximum, tops)
+                weights = [s * jnp.exp2(m - top) for s, m in zip(sums, tops)]
+                inverse = 1.0 / functools.reduce(jnp.add, weights)
+                start = (request * share + member) * head_size
+                mixed = jnp.zeros((rows, head_size), jnp.float32)
+                for weight, x_ref in zip(weights, x_refs):
+                    part = x_ref[:, start : start + head_size].astype(jnp.float32)
+                    mixed = mixed + jnp.broadcast_to(weight * inverse, part.shape) * part
+                attn[
+                    first : first + rows, member * head_size : (member + 1) * head_size
+                ] = mixed.astype(jnp.bfloat16)
     columns = w_refs[0].shape[1]
     per_half = keep_ref.shape[1] // columns
     for part in range(parts):
@@ -311,16 +318,16 @@
             send_ref[:, pl.ds(inside, columns)] = made.astype(jnp.bfloat16)
 
 
-def merge_project(messages, weights, info, share, requests):
-    rows, width = messages[0].shape
+def merge_project(batches, weights, info, share, requests):
+    rows = batches[0][0].shape[0]
     columns = weights[0].shape[1]
-    parts = len(messages)
+    parts = len(weights)
     half_width = parts * columns // 2
     shape = (requests * rows, half_width)
     return pl.pallas_call(
-        functools.partial(merge_kernel, parts, share),
+        functools.partial(merge_kernel, parts, len(batches), share),
         in_specs=[pl.BlockSpec(memory_space=pltpu.SMEM)]
-        + [pl.BlockSpec(memory_space=pltpu.VMEM)] * (2 * parts),
+        + [pl.BlockSpec(memory_space=pltpu.VMEM)] * ((len(batches) + 1) * parts),
         out_specs=[pl.BlockSpec(memory_space=pltpu.VMEM)] * 2,
         out_shape=[
             jax.ShapeDtypeStruct(shape, jnp.float32),
@@ -328,7 +335,7 @@
         ],
         scratch_shapes=[pltpu.VMEM((requests * rows, share * head_size_of(weights, share)), jnp.bfloat16)],
         name="merge_project",
-    )(info, *messages, *weights)
+    )(info, *[message for batch in batches for message in batch], *weights)
 
 
 def head_size_of(weights, share):
@@ -405,8 +412,8 @@
     row_count, half_width = half_hidden.shape
     req_size = lax.axis_size("req")
     sent = half_hidden.astype(jnp.bfloat16)
+    sent, table = lax.optimization_barrier((sent, table))
     column = jnp.concatenate(gather_blocks(sent, "req"), axis=0)
-    column, table = lax.optimization_barrier((column, table))
     row_weights = exchange_table(table)
     middle = column.shape[0] // 2
 
@@ -517,29 +524,34 @@
     capacity = max(2, 2 * row_count * route_ids.shape[1] // experts_all)
     dense = capacity >= row_count and experts_all == groups and exp_size == 4
 
-    pieces = gather_blocks(queries, "exp")
+    batch = requests // 2 if requests % 2 == 0 else requests
+    starts = range(0, requests, batch)
+    pieces = [
+        gather_blocks(lax.slice_in_dim(queries, start, start + batch), "exp") for start in starts
+    ]
     local_lengths = jnp.clip(lengths - exp_at * span, 0, span)
     split_weight = out_weight.reshape(exp_size, share * head_size, -1)
     weight_parts = [take_block(split_weight, targets[0])] + [
         shift(take_block(split_weight, targets[s]), "exp", s) for s in range(1, exp_size)
     ]
-    messages = attend(
-        pieces, sources, new_keys, new_values, key_cache, value_cache, local_lengths,
-        512, 256, exp_size,
-    )
-    received = [take_block(messages, targets[0])] + [
-        shift(take_block(messages, targets[s]), "exp", s) for s in range(1, exp_size)
-    ]
+    received = []
+    for start, gathered in zip(starts, pieces):
+        messages = attend(
+            gathered, sources, new_keys, new_values, key_cache, value_cache, local_lengths,
+            start, 512, 256,
+        )
+        received.append(
+            [messages[0]] + [shift(messages[s], "exp", s) for s in range(1, exp_size)]
+        )
     if dense:
         table = route_table(route_ids, route_weights)
         maps_in = halves(expert_in[0].reshape(model_width, -1), half_width, 0)
         maps_out = halves(expert_out[0], half_width, 1)
         gains = halves(norm_gain, half_width, 0)
-        own_message = received[0]
         own_message, maps_in, maps_out = lax.optimization_barrier(
-            (own_message, maps_in, maps_out)
-        )
-        received = [own_message] + received[1:]
+            (received[-1][0], maps_in, maps_out)
+        )
+        received[-1] = [own_message] + received[-1][1:]
     group_shift = (head_size - (exp_at * share) % group) % head_size
     info = jnp.concatenate([jnp.stack([group_shift, head_at]).astype(jnp.int32), sources])
     kept, sent = merge_project(received, weight_parts, info, share, requests)

time: 186 us -> 195 us (1.048)
  Pallas kernels: 40.9 us -> 50.7 us
  local copies, waits for them, and re-layouts: 17.4 us -> 21.1 us
  waiting for transfers between devices: 50.8 us -> 47.9 us
    pallas_call x2 -> x3, Pallas kernels: 40.9 us -> 50.7 us  [the longest x2 45.2 us: attend(): pl.pallas_call(functools.partial(attend_kernel, pieces, base, listed, sub...]
    ppermute x18, waiting for transfers between devices: 14.5 us -> 21.3 us  [swap(): return lax.ppermute(value, axis, [(i, i ^ bits) for i in range(size)])]
    ppermute x19 -> x25, waiting for transfers between devices: 29.8 us -> 23.7 us  [shift(): lax.ppermute(value, axis, [(i, (i + step) % size) for i in range(size)])]
    all_to_all x1, waiting for transfers between devices: 6.41 us -> 2.84 us  [exchange_table(): lax.all_to_all(table, ('req', 'exp'), split_axis=0, concat_axis=0, tiled=...]
    ppermute x19 -> x25, starting transfers between devices: 35.3 us -> 33.1 us  [shift(): lax.ppermute(value, axis, [(i, (i + step) % size) for i in range(size)])]
    squeeze x3 -> x2, local copies, waits for them, and re-layouts: 4.98 us -> 3.11 us  [take_block(): return lax.dynamic_index_in_dim(value, index, 0, keepdims=False)]
    dynamic_slice x3 -> x2, local copies, waits for them, and re-layouts: 3.38 us -> 4.73 us  [halves(): other = lax.dynamic_slice_in_dim(value, (1 - head_at) * width, width, axis)]
    unnamed x24 -> x39, local copies, waits for them, and re-layouts: 5.77 us -> 6.81 us
  transfers between devices with their start and end apart: 38 -> 44, of which waited for: 15 -> 15; matrix products, arithmetic and copies ran while one was open for 20% -> 20% of each run, Pallas kernels for 19% -> 23%
where the time goes in v2:
time: 195 us; the launch traced here: 198 us
  starting transfers between devices  52.1 us (27%)
  Pallas kernels  50.7 us (26%)
  waiting for transfers between devices  47.9 us (25%)
  local copies, waits for them, and re-layouts  21.1 us (11%)
  other arithmetic  13.5 us (7%)
  matrix products  11.7 us (6%)
    pallas_call x2, Pallas kernels, attend(): pl.pallas_call(functools.partial(attend_kernel, pieces, base, listed, sub...  45.2 us
    ppermute x25, starting transfers between devices, shift(): lax.ppermute(value, axis, [(i, (i + step) % size) for i in range(size)])  33.1 us
    ppermute x25, waiting for transfers between devices, shift(): lax.ppermute(value, axis, [(i, (i + step) % size) for i in range(size)])  23.7 us
    ppermute x18, waiting for transfers between devices, swap(): return lax.ppermute(value, axis, [(i, i ^ bits) for i in range(size)])  21.3 us
    ppermute x18, starting transfers between devices, swap(): return lax.ppermute(value, axis, [(i, i ^ bits) for i in range(size)])  12.7 us
    dot_general x8, matrix products, expert_block(): jnp.dot((x * factor * gain).astype(jnp.bfloat16), maps, preferred_element...  8.19 us
    unnamed x39, local copies, waits for them, and re-layouts  6.81 us
    all_to_all x1, starting transfers between devices, exchange_table(): lax.all_to_all(table, ('req', 'exp'), split_axis=0, concat_axis=0, tiled=...  6.29 us
  transfers between devices with their start and end apart: 44, of which 15 were waited for; matrix products, arithmetic and copies ran while one was open for 20% of the time, Pallas kernels for 23%

profile of v2, /device:TPU:0, one launch (start us, length us, event | category | flops | bytes accessed | tf_op | source)
XLA Modules:
  0.0 197.6 jit_solution(17720364021861993535)
XLA Ops:
  0.0 1.0 fusion.88
  1.0 3.0 %collective-permute-start.6 = (bf16[2,16,16,128]{3,2,1,0:T(8,128)(2,1)S(1)}, bf16[2,16,16,128]{3,2,1,0:T(8,128)(2,1)}, u32[]{:S(2)}, u32[]{:S(2)}) collective-permute-start(bf16[2,16,16,128]{3,2,1,0:T(8,128)(2,1)S(1)} %get-tuple-element.58.refs_0_), channel_id=1, source_target_pairs={{0,1},{1,2},{2,3},{3,0},{4,5},{5,6},{6,7},{7,4},{8,9},{9,10},{10,1... | collective-permute-start | bytes 393224 | tf_op jit(solution)/shard_map/ppermute | solution.py:347
  4.0 1.5 collective-permute-start.7
  5.6 1.4 collective-permute-start.8
  8.1 0.7 subtract_clamp_fusion
  8.7 3.1 %dynamic-slice_bitcast_fusion.2 = (bf16[512,512]{1,0:T(8,128)(2,1)}, bf16[512,512]{1,0:T(8,128)(2,1)}, bf16[512,512]{1,0:T(8,128)(2,1)}, bf16[512,512]{1,0:T(8,128)(2,1)}) fusion(bf16[4,512,512]{2,1,0:T(8,128)(2,1)} %bitcast.76, s32[]{:T(128)S(6)} %select_n.107, s32[]{:T(128)S(6)} %select_n.105, s32[]{:T(128)S(6)} %select_n.103, s32[]{:T(128)S(6)} %select_n.101), kind=kLoop, calls=%fused_computation.97 | loop fusion | bytes 4194320 | tf_op jit(solution)/shard_map/jit(dynamic_index_in_dim)/squeeze | solution.py:351
  11.8 2.0 %collective-permute-start.2 = (bf16[2,16,16,128]{3,2,1,0:T(8,128)(2,1)S(1)}, bf16[2,16,16,128]{3,2,1,0:T(8,128)(2,1)}, u32[]{:S(2)}, u32[]{:S(2)}) collective-permute-start(bf16[2,16,16,128]{3,2,1,0:T(8,128)(2,1)S(1)} %get-tuple-element.59.refs_0_), channel_id=1, source_target_pairs={{0,3},{1,0},{2,1},{3,2},{4,7},{5,4},{6,5},{7,6},{8,11},{9,8},{10,9... | collective-permute-start | bytes 393224 | tf_op jit(solution)/shard_map/ppermute | solution.py:347
  13.9 2.3 %copy.19 = bf16[256,8,2,384]{3,1,2,0:T(8,128)(2,1)} copy(bf16[256,8,2,384]{3,2,1,0:T(2,128)(2,1)S(1)} %bitcast.75) | data formatting | bytes 6291456
  17.2 1.5 collective-permute-start.13
  18.7 20.5 %attend.3 = (bf16[64,1152]{1,0:T(8,128)(2,1)}, bf16[64,1152]{1,0:T(8,128)(2,1)}, bf16[64,1152]{1,0:T(8,128)(2,1)}, bf16[64,1152]{1,0:T(8,128)(2,1)}) custom-call(s32[8]{0:T(128)} %pad_add_fusion.1.info_ref, bf16[2,16,16,128]{3,2,1,0:T(8,128)(2,1)} %copy-done.4, bf16[2,16,16,128]{3,2,1,0:T(8,128)(2,1)} %collective-permute-done.6.refs_1_, ...), custom_call_target="tpu_custom_call" | custom-call | tf_op jit(solution)/shard_map/attend/pallas_call | solution.py:243
  39.4 3.4 %collective-permute-start.11 = (bf16[64,1152]{1,0:T(8,128)(2,1)}, bf16[64,1152]{1,0:T(8,128)(2,1)S(1)}, u32[]{:S(2)}, u32[]{:S(2)}) collective-permute-start(bf16[64,1152]{1,0:T(8,128)(2,1)} %get-tuple-element.30), channel_id=1, source_target_pairs={{0,3},{1,0},{2,1},{3,2},{4,7},{5,4},{6,5},{7,6},{8,11},{9,8},{10,9... | collective-permute-start | bytes 442376 | tf_op jit(solution)/shard_map/ppermute | solution.py:347
  42.8 3.2 %constant_dynamic-slice_fusion = (bf16[1024,768]{1,0:T(8,128)(2,1)}, bf16[1024,768]{1,0:T(8,128)(2,1)S(1)}) fusion(bf16[2048,768]{1,0:T(8,128)(2,1)} %bitcast.72, s32[]{:T(128)S(6)} %select_n.99, s32[]{:T(128)S(6)} %select_n.95), kind=kLoop, calls=%fused_computation.132 | loop fusion | bytes 6291464 | tf_op jit(solution)/shard_map/dynamic_slice | solution.py:387
  46.1 24.7 %attend.2 = (bf16[64,1152]{1,0:T(8,128)(2,1)}, bf16[64,1152]{1,0:T(8,128)(2,1)}, bf16[64,1152]{1,0:T(8,128)(2,1)}, bf16[64,1152]{1,0:T(8,128)(2,1)}) custom-call(s32[8]{0:T(128)} %pad_add_fusion.1.info_ref, bf16[2,16,16,128]{3,2,1,0:T(8,128)(2,1)} %copy-done.3, bf16[2,16,16,128]{3,2,1,0:T(8,128)(2,1)} %copy-done.9, ...), custom_call_target="tpu_custom_call" | custom-call | tf_op jit(solution)/shard_map/attend/pallas_call | solution.py:243
  71.7 5.3 %collective-permute-done.9.refs_5_ = bf16[64,1152]{1,0:T(8,128)(2,1)S(1)} collective-permute-done((bf16[64,1152]{1,0:T(8,128)(2,1)S(1)}, bf16[64,1152]{1,0:T(8,128)(2,1)S(1)}, u32[]{:S(2)}, u32[]{:S(2)}) %collective-permute-start.9) | collective-permute-done | bytes 147488 | tf_op jit(solution)/shard_map/ppermute | solution.py:347
  77.0 2.6 %collective-permute-done.3.refs_1_ = bf16[64,1152]{1,0:T(8,128)(2,1)S(1)} collective-permute-done((bf16[64,1152]{1,0:T(8,128)(2,1)}, bf16[64,1152]{1,0:T(8,128)(2,1)S(1)}, u32[]{:S(2)}, u32[]{:S(2)}) %collective-permute-start.3) | collective-permute-done | bytes 147488 | tf_op jit(solution)/shard_map/ppermute | solution.py:347
  79.6 0.6 copy-done.8
  80.8 1.5 dynamic-slice_bitcast_fusion
  82.4 3.2 %collective-permute-done.5.refs_3_ = bf16[64,1152]{1,0:T(8,128)(2,1)} collective-permute-done((bf16[64,1152]{1,0:T(8,128)(2,1)}, bf16[64,1152]{1,0:T(8,128)(2,1)}, u32[]{:S(2)}, u32[]{:S(2)}) %collective-permute-start.5) | collective-permute-done | bytes 147488 | tf_op jit(solution)/shard_map/ppermute | solution.py:347
  85.7 5.5 %merge_project.1 = (f32[256,1024]{1,0:T(8,128)}, bf16[256,1024]{1,0:T(8,128)(2,1)}) custom-call(s32[6]{0:T(128)} %pad_add_fusion.info_ref, bf16[64,1152]{1,0:T(8,128)(2,1)} %get-tuple-element.22.refs_0_, bf16[64,1152]{1,0:T(8,128)(2,1)} %copy-done.8, bf16[64,1152]{1,0:T(8,128)(2,1)} %collective-permute-done.4.refs_2_, ...), custom_call_target="tpu_custom_call" | custom-call | tf_op jit(solution)/shard_map/merge_project/pallas_call | solution.py:327
  92.0 1.5 collective-permute-done.15
  93.4 1.5 convert_add_fusion.3
  95.2 2.0 %collective-permute-start.17 = (bf16[64,1024]{1,0:T(8,128)(2,1)S(1)}, bf16[64,1024]{1,0:T(8,128)(2,1)S(1)}, u32[]{:S(2)}, u32[]{:S(2)}) collective-permute-start(bf16[64,1024]{1,0:T(8,128)(2,1)S(1)} %get-tuple-element.55), channel_id=1, source_target_pairs={{0,2},{1,3},{2,0},{3,1},{4,6},{5,7},{6,4},{7,5},{8,10},{9,11},{10,... | collective-permute-start | bytes 393224 | tf_op jit(solution)/shard_map/ppermute | solution.py:347
  97.2 0.9 collective-permute-start.18
  98.7 3.7 %collective-permute-done.16 = bf16[64,1024]{1,0:T(8,128)(2,1)S(1)} collective-permute-done((bf16[64,1024]{1,0:T(8,128)(2,1)S(1)}, bf16[64,1024]{1,0:T(8,128)(2,1)S(1)}, u32[]{:S(2)}, u32[]{:S(2)}) %collective-permute-start.16) | collective-permute-done | bytes 131104 | tf_op jit(solution)/shard_map/ppermute | solution.py:347
  102.5 1.1 collective-permute-done.17
  104.3 6.6 %collective-permute-start.20 = (bf16[64,1024]{1,0:T(8,128)(2,1)S(1)}, bf16[64,1024]{1,0:T(8,128)(2,1)}, u32[]{:S(2)}, u32[]{:S(2)}) collective-permute-start(bf16[64,1024]{1,0:T(8,128)(2,1)S(1)} %get-tuple-element.33), channel_id=1, source_target_pairs={{0,16},{8,24},{16,0},{24,8},{1,17},{9,25},{17,1},{25,9},{2,18},{10... | collective-permute-start | bytes 393224 | tf_op jit(solution)/shard_map/ppermute | solution.py:347
  110.9 6.3 %all-to-all-start = ((f32[16,1,64]{2,1,0:T(1,128)}), f32[16,1,64]{2,1,0:T(1,128)S(1)}, u32[]{:S(2)}, u32[]{:S(2)}) async-start(f32[16,1,64]{2,1,0:T(1,128)} %bitcast.82), calls=%async_computation | async-start | bytes 16384 | tf_op jit(solution)/shard_map/all_to_all | solution.py:377
  117.2 0.7 constant_dynamic-update-slice_fusion.3
  117.9 3.7 %collective-permute-start.21 = (bf16[64,1024]{1,0:T(8,128)(2,1)S(1)}, bf16[64,1024]{1,0:T(8,128)(2,1)}, u32[]{:S(2)}, u32[]{:S(2)}) collective-permute-start(bf16[64,1024]{1,0:T(8,128)(2,1)S(1)} %get-tuple-element.33), channel_id=1, source_target_pairs={{0,24},{8,0},{16,8},{24,16},{1,25},{9,1},{17,9},{25,17},{2,26},{10... | collective-permute-start | bytes 393224 | tf_op jit(solution)/shard_map/ppermute | solution.py:347
  121.6 2.8 %all-to-all-done = f32[16,1,64]{2,1,0:T(1,128)S(1)} async-done(((f32[16,1,64]{2,1,0:T(1,128)}), f32[16,1,64]{2,1,0:T(1,128)S(1)}, u32[]{:S(2)}, u32[]{:S(2)}) %all-to-all-start) | async-done | bytes 4128 | tf_op jit(solution)/shard_map/all_to_all | solution.py:377
  124.5 1.3 gather_fusion
  125.8 1.6 constant_dynamic-update-slice_fusion.2
  127.3 1.6 constant_dynamic-update-slice_fusion.1
  128.9 1.6 constant_dynamic-update-slice_fusion
  130.5 0.7 collective-permute-start.28
  131.7 0.8 broadcast_select_fusion
  132.8 1.3 fusion.4
  134.1 8.0 %collective-permute-done.24 = bf16[256,1024]{1,0:T(8,128)(2,1)} collective-permute-done((bf16[256,1024]{1,0:T(8,128)(2,1)}, bf16[256,1024]{1,0:T(8,128)(2,1)}, u32[]{:S(2)}, u32[]{:S(2)}) %collective-permute-start.24) | collective-permute-done | bytes 524320 | tf_op jit(solution)/shard_map/ppermute | solution.py:360
  142.1 1.0 slice.142
  143.1 1.5 collective-permute-start.31
  144.6 1.0 slice.143
  145.6 0.7 collective-permute-start.32
  146.3 1.2 fusion.7
  147.6 1.7 fusion.41
  151.2 1.2 fusion.16
  152.4 1.2 fusion.10
  154.6 1.7 fusion.36
  157.8 1.7 fusion.39
  159.5 0.6 convolution_add_fusion.1
  160.4 0.6 fusion.28
  161.1 0.6 fusion.32
  164.9 1.5 collective-permute-start.35
  166.4 1.5 collective-permute-start.39
  168.4 0.7 collective-permute-start.27
  169.1 5.0 %collective-permute-done.35 = bf16[128,1024]{1,0:T(8,128)(2,1)S(1)} collective-permute-done((bf16[128,1024]{1,0:T(8,128)(2,1)S(1)}, bf16[128,1024]{1,0:T(8,128)(2,1)S(1)}, u32[]{:S(2)}, u32[]{:S(2)}) %collective-permute-start.35) | collective-permute-done | bytes 262176 | tf_op jit(solution)/shard_map/ppermute | solution.py:360
  174.2 1.6 collective-permute-start.36
  175.8 2.9 %collective-permute-done.39 = bf16[128,1024]{1,0:T(8,128)(2,1)S(1)} collective-permute-done((bf16[128,1024]{1,0:T(8,128)(2,1)S(1)}, bf16[128,1024]{1,0:T(8,128)(2,1)S(1)}, u32[]{:S(2)}, u32[]{:S(2)}) %collective-permute-start.39) | collective-permute-done | bytes 262176 | tf_op jit(solution)/shard_map/ppermute | solution.py:360
  178.8 1.4 collective-permute-start.40
  180.7 3.1 %collective-permute-done.36 = bf16[128,1024]{1,0:T(8,128)(2,1)S(1)} collective-permute-done((bf16[128,1024]{1,0:T(8,128)(2,1)S(1)}, bf16[128,1024]{1,0:T(8,128)(2,1)S(1)}, u32[]{:S(2)}, u32[]{:S(2)}) %collective-permute-start.36) | collective-permute-done | bytes 262176 | tf_op jit(solution)/shard_map/ppermute | solution.py:360
  183.8 2.3 %collective-permute-done.40 = bf16[128,1024]{1,0:T(8,128)(2,1)S(1)} collective-permute-done((bf16[128,1024]{1,0:T(8,128)(2,1)S(1)}, bf16[128,1024]{1,0:T(8,128)(2,1)S(1)}, u32[]{:S(2)}, u32[]{:S(2)}) %collective-permute-start.40) | collective-permute-done | bytes 262176 | tf_op jit(solution)/shard_map/ppermute | solution.py:360
  186.8 0.9 collective-permute-start.42
  187.8 3.0 %collective-permute-start.37 = (bf16[64,1024]{1,0:T(8,128)(2,1)S(1)}, bf16[64,1024]{1,0:T(8,128)(2,1)S(1)}, u32[]{:S(2)}, u32[]{:S(2)}) collective-permute-start(bf16[64,1024]{1,0:T(8,128)(2,1)S(1)} %slice.200), channel_id=1, source_target_pairs={{0,24},{8,0},{16,8},{24,16},{1,25},{9,1},{17,9},{25,17},{2,26},{10... | collective-permute-start | bytes 393224 | tf_op jit(solution)/shard_map/ppermute | solution.py:347
  190.7 5.8 %collective-permute-done.41 = bf16[64,1024]{1,0:T(8,128)(2,1)S(1)} collective-permute-done((bf16[64,1024]{1,0:T(8,128)(2,1)S(1)}, bf16[64,1024]{1,0:T(8,128)(2,1)S(1)}, u32[]{:S(2)}, u32[]{:S(2)}) %collective-permute-start.41) | collective-permute-done | bytes 131104 | tf_op jit(solution)/shard_map/ppermute | solution.py:347
  196.8 0.7 fusion.76
  (139 shorter events, 17.0 us)
Async XLA Ops:
  1.0 10.8 %copy-start.4 = (bf16[2,16,16,128]{3,2,1,0:T(8,128)(2,1)}, bf16[2,16,16,128]{3,2,1,0:T(8,128)(2,1)S(1)}, u32[]{:S(2)}) copy-start(bf16[2,16,16,128]{3,2,1,0:T(8,128)(2,1)S(1)} %get-tuple-element.58.refs_0_) | copy-start | bytes 393220
  1.0 10.8 %copy-start.3 = (bf16[2,16,16,128]{3,2,1,0:T(8,128)(2,1)}, bf16[2,16,16,128]{3,2,1,0:T(8,128)(2,1)S(1)}, u32[]{:S(2)}) copy-start(bf16[2,16,16,128]{3,2,1,0:T(8,128)(2,1)S(1)} %get-tuple-element.59.refs_0_) | copy-start | bytes 393220
  1.0 10.8 %collective-permute-start.6 = (bf16[2,16,16,128]{3,2,1,0:T(8,128)(2,1)S(1)}, bf16[2,16,16,128]{3,2,1,0:T(8,128)(2,1)}, u32[]{:S(2)}, u32[]{:S(2)}) collective-permute-start(bf16[2,16,16,128]{3,2,1,0:T(8,128)(2,1)S(1)} %get-tuple-element.58.refs_0_), channel_id=1, source_target_pairs={{0,1},{1,2},{2,3},{3,0},{4,5},{5,6},{6,7},{7,4},{8,9},{9,10},{10,1... | collective-permute-start | bytes 393224 | tf_op jit(solution)/shard_map/ppermute | solution.py:347
  4.0 12.7 %collective-permute-start.7 = (bf16[2,16,16,128]{3,2,1,0:T(8,128)(2,1)S(1)}, bf16[2,16,16,128]{3,2,1,0:T(8,128)(2,1)}, u32[]{:S(2)}, u32[]{:S(2)}) collective-permute-start(bf16[2,16,16,128]{3,2,1,0:T(8,128)(2,1)S(1)} %get-tuple-element.58.refs_0_), channel_id=1, source_target_pairs={{0,2},{1,3},{2,0},{3,1},{4,6},{5,7},{6,4},{7,5},{8,10},{9,11},{10,... | collective-permute-start | bytes 393224 | tf_op jit(solution)/shard_map/ppermute | solution.py:347
  5.6 11.7 %collective-permute-start.8 = (bf16[2,16,16,128]{3,2,1,0:T(8,128)(2,1)S(1)}, bf16[2,16,16,128]{3,2,1,0:T(8,128)(2,1)}, u32[]{:S(2)}, u32[]{:S(2)}) collective-permute-start(bf16[2,16,16,128]{3,2,1,0:T(8,128)(2,1)S(1)} %get-tuple-element.58.refs_0_), channel_id=1, source_target_pairs={{0,3},{1,0},{2,1},{3,2},{4,7},{5,4},{6,5},{7,6},{8,11},{9,8},{10,9... | collective-permute-start | bytes 393224 | tf_op jit(solution)/shard_map/ppermute | solution.py:347
  7.0 32.3 %collective-permute-start = (bf16[2,16,16,128]{3,2,1,0:T(8,128)(2,1)S(1)}, bf16[2,16,16,128]{3,2,1,0:T(8,128)(2,1)S(1)}, u32[]{:S(2)}, u32[]{:S(2)}) collective-permute-start(bf16[2,16,16,128]{3,2,1,0:T(8,128)(2,1)S(1)} %get-tuple-element.59.refs_0_), channel_id=1, source_target_pairs={{0,1},{1,2},{2,3},{3,0},{4,5},{5,6},{6,7},{7,4},{8,9},{9,10},{10,1... | collective-permute-start | bytes 393224 | tf_op jit(solution)/shard_map/ppermute | solution.py:347
  7.6 31.8 %collective-permute-start.1 = (bf16[2,16,16,128]{3,2,1,0:T(8,128)(2,1)S(1)}, bf16[2,16,16,128]{3,2,1,0:T(8,128)(2,1)}, u32[]{:S(2)}, u32[]{:S(2)}) collective-permute-start(bf16[2,16,16,128]{3,2,1,0:T(8,128)(2,1)S(1)} %get-tuple-element.59.refs_0_), channel_id=1, source_target_pairs={{0,2},{1,3},{2,0},{3,1},{4,6},{5,7},{6,4},{7,5},{8,10},{9,11},{10,... | collective-permute-start | bytes 393224 | tf_op jit(solution)/shard_map/ppermute | solution.py:347
  8.7 5.1 %copy-start.1 = (bf16[1,2048,2,384]{3,2,1,0:T(2,128)(2,1)S(1)}, bf16[1,2048,2,384]{3,2,1,0:T(2,128)(2,1)}, u32[]{:S(2)}) copy-start(bf16[1,2048,2,384]{3,2,1,0:T(2,128)(2,1)} %param.24) | copy-start | bytes 9437188
  11.8 27.6 %collective-permute-start.2 = (bf16[2,16,16,128]{3,2,1,0:T(8,128)(2,1)S(1)}, bf16[2,16,16,128]{3,2,1,0:T(8,128)(2,1)}, u32[]{:S(2)}, u32[]{:S(2)}) collective-permute-start(bf16[2,16,16,128]{3,2,1,0:T(8,128)(2,1)S(1)} %get-tuple-element.59.refs_0_), channel_id=1, source_target_pairs={{0,3},{1,0},{2,1},{3,2},{4,7},{5,4},{6,5},{7,6},{8,11},{9,8},{10,9... | collective-permute-start | bytes 393224 | tf_op jit(solution)/shard_map/ppermute | solution.py:347
  13.8 2.3 %copy-start.14 = (s32[4]{0:T(128)}, s32[4]{0:T(128)S(1)}, u32[]{:S(2)}) copy-start(s32[4]{0:T(128)S(1)} %and_select_fusion.1) | copy-start | bytes 52
  16.8 68.9 %collective-permute-start.12 = (bf16[512,512]{1,0:T(8,128)(2,1)}, bf16[512,512]{1,0:T(8,128)(2,1)}, u32[]{:S(2)}, u32[]{:S(2)}) collective-permute-start(bf16[512,512]{1,0:T(8,128)(2,1)} %get-tuple-element.45), channel_id=1, source_target_pairs={{0,1},{1,2},{2,3},{3,0},{4,5},{5,6},{6,7},{7,4},{8,9},{9,10},{10,1... | collective-permute-start | bytes 1572872 | tf_op jit(solution)/shard_map/ppermute | solution.py:347
  17.2 68.4 %collective-permute-start.13 = (bf16[512,512]{1,0:T(8,128)(2,1)}, bf16[512,512]{1,0:T(8,128)(2,1)}, u32[]{:S(2)}, u32[]{:S(2)}) collective-permute-start(bf16[512,512]{1,0:T(8,128)(2,1)} %get-tuple-element.44), channel_id=1, source_target_pairs={{0,2},{1,3},{2,0},{3,1},{4,6},{5,7},{6,4},{7,5},{8,10},{9,11},{10,... | collective-permute-start | bytes 1572872 | tf_op jit(solution)/shard_map/ppermute | solution.py:347
  39.3 6.8 %copy-start.9 = (bf16[2,16,16,128]{3,2,1,0:T(8,128)(2,1)}, bf16[2,16,16,128]{3,2,1,0:T(8,128)(2,1)S(1)}, u32[]{:S(2)}) copy-start(bf16[2,16,16,128]{3,2,1,0:T(8,128)(2,1)S(1)} %collective-permute-done.refs_1_) | copy-start | bytes 393220
  39.3 46.4 %collective-permute-start.14 = (bf16[512,512]{1,0:T(8,128)(2,1)}, bf16[512,512]{1,0:T(8,128)(2,1)}, u32[]{:S(2)}, u32[]{:S(2)}) collective-permute-start(bf16[512,512]{1,0:T(8,128)(2,1)} %get-tuple-element.43), channel_id=1, source_target_pairs={{0,3},{1,0},{2,1},{3,2},{4,7},{5,4},{6,5},{7,6},{8,11},{9,8},{10,9... | collective-permute-start | bytes 1572872 | tf_op jit(solution)/shard_map/ppermute | solution.py:347
  39.4 31.4 %collective-permute-start.10 = (bf16[64,1152]{1,0:T(8,128)(2,1)}, bf16[64,1152]{1,0:T(8,128)(2,1)S(1)}, u32[]{:S(2)}, u32[]{:S(2)}) collective-permute-start(bf16[64,1152]{1,0:T(8,128)(2,1)} %get-tuple-element.29), channel_id=1, source_target_pairs={{0,2},{1,3},{2,0},{3,1},{4,6},{5,7},{6,4},{7,5},{8,10},{9,11},{10,... | collective-permute-start | bytes 442376 | tf_op jit(solution)/shard_map/ppermute | solution.py:347
  39.4 31.4 %collective-permute-start.11 = (bf16[64,1152]{1,0:T(8,128)(2,1)}, bf16[64,1152]{1,0:T(8,128)(2,1)S(1)}, u32[]{:S(2)}, u32[]{:S(2)}) collective-permute-start(bf16[64,1152]{1,0:T(8,128)(2,1)} %get-tuple-element.30), channel_id=1, source_target_pairs={{0,3},{1,0},{2,1},{3,2},{4,7},{5,4},{6,5},{7,6},{8,11},{9,8},{10,9... | collective-permute-start | bytes 442376 | tf_op jit(solution)/shard_map/ppermute | solution.py:347
  46.1 24.7 %copy-start.16 = (bf16[64,1152]{1,0:T(8,128)(2,1)S(1)}, bf16[64,1152]{1,0:T(8,128)(2,1)}, u32[]{:S(2)}) copy-start(bf16[64,1152]{1,0:T(8,128)(2,1)} %get-tuple-element.28) | copy-start | bytes 442372
  46.1 25.0 %copy-start.15 = (s32[4]{0:T(128)S(1)}, s32[4]{0:T(128)}, u32[]{:S(2)}) copy-start(s32[4]{0:T(128)} %copy-done.14) | copy-start | bytes 52
  70.7 11.5 %copy-start.5 = (bf16[64,1152]{1,0:T(8,128)(2,1)}, bf16[64,1152]{1,0:T(8,128)(2,1)S(1)}, u32[]{:S(2)}) copy-start(bf16[64,1152]{1,0:T(8,128)(2,1)S(1)} %collective-permute-done.10.refs_6_) | copy-start | bytes 442372
  70.8 6.2 %collective-permute-start.9 = (bf16[64,1152]{1,0:T(8,128)(2,1)S(1)}, bf16[64,1152]{1,0:T(8,128)(2,1)S(1)}, u32[]{:S(2)}, u32[]{:S(2)}) collective-permute-start(bf16[64,1152]{1,0:T(8,128)(2,1)S(1)} %copy-done.16), channel_id=1, source_target_pairs={{0,1},{1,2},{2,3},{3,0},{4,5},{5,6},{6,7},{7,4},{8,9},{9,10},{10,1... | collective-permute-start | bytes 442376 | tf_op jit(solution)/shard_map/ppermute | solution.py:347
  70.8 8.7 %copy-start.6 = (bf16[64,1152]{1,0:T(8,128)(2,1)}, bf16[64,1152]{1,0:T(8,128)(2,1)S(1)}, u32[]{:S(2)}) copy-start(bf16[64,1152]{1,0:T(8,128)(2,1)S(1)} %collective-permute-done.11.refs_7_) | copy-start | bytes 442372
  70.8 8.7 %collective-permute-start.3 = (bf16[64,1152]{1,0:T(8,128)(2,1)}, bf16[64,1152]{1,0:T(8,128)(2,1)S(1)}, u32[]{:S(2)}, u32[]{:S(2)}) collective-permute-start(bf16[64,1152]{1,0:T(8,128)(2,1)} %get-tuple-element.23), channel_id=1, source_target_pairs={{0,1},{1,2},{2,3},{3,0},{4,5},{5,6},{6,7},{7,4},{8,9},{9,10},{10,1... | collective-permute-start | bytes 442376 | tf_op jit(solution)/shard_map/ppermute | solution.py:347
  77.0 2.6 %copy-start.7 = (bf16[64,1152]{1,0:T(8,128)(2,1)}, bf16[64,1152]{1,0:T(8,128)(2,1)S(1)}, u32[]{:S(2)}) copy-start(bf16[64,1152]{1,0:T(8,128)(2,1)S(1)} %collective-permute-done.9.refs_5_) | copy-start | bytes 442372
  77.0 5.5 %collective-permute-start.4 = (bf16[64,1152]{1,0:T(8,128)(2,1)}, bf16[64,1152]{1,0:T(8,128)(2,1)}, u32[]{:S(2)}, u32[]{:S(2)}) collective-permute-start(bf16[64,1152]{1,0:T(8,128)(2,1)} %get-tuple-element.24), channel_id=1, source_target_pairs={{0,2},{1,3},{2,0},{3,1},{4,6},{5,7},{6,4},{7,5},{8,10},{9,11},{10,... | collective-permute-start | bytes 442376 | tf_op jit(solution)/shard_map/ppermute | solution.py:347
  79.6 0.7 copy-start.8
  80.2 5.5 %collective-permute-start.5 = (bf16[64,1152]{1,0:T(8,128)(2,1)}, bf16[64,1152]{1,0:T(8,128)(2,1)}, u32[]{:S(2)}, u32[]{:S(2)}) collective-permute-start(bf16[64,1152]{1,0:T(8,128)(2,1)} %get-tuple-element.25), channel_id=1, source_target_pairs={{0,3},{1,0},{2,1},{3,2},{4,7},{5,4},{6,5},{7,6},{8,11},{9,8},{10,9... | collective-permute-start | bytes 442376 | tf_op jit(solution)/shard_map/ppermute | solution.py:347
  91.2 2.3 %collective-permute-start.15 = (bf16[256,1024]{1,0:T(8,128)(2,1)}, bf16[256,1024]{1,0:T(8,128)(2,1)}, u32[]{:S(2)}, u32[]{:S(2)}) collective-permute-start(bf16[256,1024]{1,0:T(8,128)(2,1)} %get-tuple-element.32), channel_id=1, source_target_pairs={{0,4},{4,0},{1,5},{5,1},{2,6},{6,2},{3,7},{7,3},{8,12},{12,8},{9,1... | collective-permute-start | bytes 1572872 | tf_op jit(solution)/shard_map/ppermute | solution.py:347
  94.9 3.2 %copy-start.11 = (f32[2048]{0:T(1024)S(1)}, f32[2048]{0:T(1024)}, u32[]{:S(2)}) copy-start(f32[2048]{0:T(1024)} %param.21) | copy-start | bytes 24580
  94.9 3.1 %copy-start.12 = (f32[64,8]{0,1:T(8,128)S(1)}, f32[64,8]{0,1:T(8,128)}, u32[]{:S(2)}) copy-start(f32[64,8]{0,1:T(8,128)} %param.23) | copy-start | bytes 6148
  95.0 3.1 %copy-start.13 = (s32[64,8]{0,1:T(8,128)S(1)}, s32[64,8]{0,1:T(8,128)}, u32[]{:S(2)}) copy-start(s32[64,8]{0,1:T(8,128)} %param.22) | copy-start | bytes 6148
  95.0 8.6 %copy-start.10 = (bf16[64,2048]{1,0:T(8,128)(2,1)S(1)}, bf16[64,2048]{1,0:T(8,128)(2,1)}, u32[]{:S(2)}) copy-start(bf16[64,2048]{1,0:T(8,128)(2,1)} %param.19) | copy-start | bytes 786436
  95.1 7.4 %collective-permute-start.16 = (bf16[64,1024]{1,0:T(8,128)(2,1)S(1)}, bf16[64,1024]{1,0:T(8,128)(2,1)S(1)}, u32[]{:S(2)}, u32[]{:S(2)}) collective-permute-start(bf16[64,1024]{1,0:T(8,128)(2,1)S(1)} %get-tuple-element.53), channel_id=1, source_target_pairs={{0,1},{1,2},{2,3},{3,0},{4,5},{5,6},{6,7},{7,4},{8,9},{9,10},{10,1... | collective-permute-start | bytes 393224 | tf_op jit(solution)/shard_map/ppermute | solution.py:347
  95.2 8.4 %collective-permute-start.17 = (bf16[64,1024]{1,0:T(8,128)(2,1)S(1)}, bf16[64,1024]{1,0:T(8,128)(2,1)S(1)}, u32[]{:S(2)}, u32[]{:S(2)}) collective-permute-start(bf16[64,1024]{1,0:T(8,128)(2,1)S(1)} %get-tuple-element.55), channel_id=1, source_target_pairs={{0,2},{1,3},{2,0},{3,1},{4,6},{5,7},{6,4},{7,5},{8,10},{9,11},{10,... | collective-permute-start | bytes 393224 | tf_op jit(solution)/shard_map/ppermute | solution.py:347
  97.2 6.4 %collective-permute-start.18 = (bf16[64,1024]{1,0:T(8,128)(2,1)S(1)}, bf16[64,1024]{1,0:T(8,128)(2,1)S(1)}, u32[]{:S(2)}, u32[]{:S(2)}) collective-permute-start(bf16[64,1024]{1,0:T(8,128)(2,1)S(1)} %get-tuple-element.54), channel_id=1, source_target_pairs={{0,3},{1,0},{2,1},{3,2},{4,7},{5,4},{6,5},{7,6},{8,11},{9,8},{10,9... | collective-permute-start | bytes 393224 | tf_op jit(solution)/shard_map/ppermute | solution.py:347
  103.7 22.1 %collective-permute-start.19 = (bf16[64,1024]{1,0:T(8,128)(2,1)S(1)}, bf16[64,1024]{1,0:T(8,128)(2,1)}, u32[]{:S(2)}, u32[]{:S(2)}) collective-permute-start(bf16[64,1024]{1,0:T(8,128)(2,1)S(1)} %get-tuple-element.33), channel_id=1, source_target_pairs={{0,8},{8,16},{16,24},{24,0},{1,9},{9,17},{17,25},{25,1},{2,10},{10... | collective-permute-start | bytes 393224 | tf_op jit(solution)/shard_map/ppermute | solution.py:347
  104.3 23.0 %collective-permute-start.20 = (bf16[64,1024]{1,0:T(8,128)(2,1)S(1)}, bf16[64,1024]{1,0:T(8,128)(2,1)}, u32[]{:S(2)}, u32[]{:S(2)}) collective-permute-start(bf16[64,1024]{1,0:T(8,128)(2,1)S(1)} %get-tuple-element.33), channel_id=1, source_target_pairs={{0,16},{8,24},{16,0},{24,8},{1,17},{9,25},{17,1},{25,9},{2,18},{10... | collective-permute-start | bytes 393224 | tf_op jit(solution)/shard_map/ppermute | solution.py:347
  110.9 13.5 %all-to-all-start = ((f32[16,1,64]{2,1,0:T(1,128)}), f32[16,1,64]{2,1,0:T(1,128)S(1)}, u32[]{:S(2)}, u32[]{:S(2)}) async-start(f32[16,1,64]{2,1,0:T(1,128)} %bitcast.82), calls=%async_computation | async-start | bytes 16384 | tf_op jit(solution)/shard_map/all_to_all | solution.py:377
  117.9 11.0 %collective-permute-start.21 = (bf16[64,1024]{1,0:T(8,128)(2,1)S(1)}, bf16[64,1024]{1,0:T(8,128)(2,1)}, u32[]{:S(2)}, u32[]{:S(2)}) collective-permute-start(bf16[64,1024]{1,0:T(8,128)(2,1)S(1)} %get-tuple-element.33), channel_id=1, source_target_pairs={{0,24},{8,0},{16,8},{24,16},{1,25},{9,1},{17,9},{25,17},{2,26},{10... | collective-permute-start | bytes 393224 | tf_op jit(solution)/shard_map/ppermute | solution.py:347
  130.5 14.1 %collective-permute-start.28 = (bf16[256,1024]{1,0:T(8,128)(2,1)}, bf16[256,1024]{1,0:T(8,128)(2,1)}, u32[]{:S(2)}, u32[]{:S(2)}) collective-permute-start(bf16[256,1024]{1,0:T(8,128)(2,1)} %constant_dynamic-update-slice_fusion), channel_id=1, source_target_pairs={{0,2},{1,3},{2,0},{3,1},{4,6},{5,7},{6,4},{7,5},{8,10},{9,11},{10,... | collective-permute-start | bytes 1572872 | tf_op jit(solution)/shard_map/ppermute | solution.py:360
  131.1 11.0 %collective-permute-start.24 = (bf16[256,1024]{1,0:T(8,128)(2,1)}, bf16[256,1024]{1,0:T(8,128)(2,1)}, u32[]{:S(2)}, u32[]{:S(2)}) collective-permute-start(bf16[256,1024]{1,0:T(8,128)(2,1)} %constant_dynamic-update-slice_fusion), channel_id=1, source_target_pairs={{0,1},{1,0},{2,3},{3,2},{4,5},{5,4},{6,7},{7,6},{8,9},{9,8},{10,11... | collective-permute-start | bytes 1572872 | tf_op jit(solution)/shard_map/ppermute | solution.py:360
  131.7 14.6 %collective-permute-start.22 = (bf16[256,1024]{1,0:T(8,128)(2,1)}, bf16[256,1024]{1,0:T(8,128)(2,1)}, u32[]{:S(2)}, u32[]{:S(2)}) collective-permute-start(bf16[256,1024]{1,0:T(8,128)(2,1)} %constant_dynamic-update-slice_fusion), channel_id=1, source_target_pairs={{0,4},{4,0},{1,5},{5,1},{2,6},{6,2},{3,7},{7,3},{8,12},{12,8},{9,1... | collective-permute-start | bytes 1572872 | tf_op jit(solution)/shard_map/ppermute | solution.py:360
  132.8 14.8 %copy-start = (bf16[1024,768]{1,0:T(8,128)(2,1)S(1)}, bf16[1024,768]{1,0:T(8,128)(2,1)}, u32[]{:S(2)}) copy-start(bf16[1024,768]{1,0:T(8,128)(2,1)} %get-tuple-element.35) | copy-start | bytes 4718596
  143.1 10.5 %collective-permute-start.31 = (bf16[128,1024]{1,0:T(8,128)(2,1)S(1)}, bf16[128,1024]{1,0:T(8,128)(2,1)S(1)}, u32[]{:S(2)}, u32[]{:S(2)}) collective-permute-start(bf16[128,1024]{1,0:T(8,128)(2,1)S(1)} %slice.142), channel_id=1, source_target_pairs={{0,2},{1,3},{2,0},{3,1},{4,6},{5,7},{6,4},{7,5},{8,10},{9,11},{10,... | collective-permute-start | bytes 786440 | tf_op jit(solution)/shard_map/ppermute | solution.py:360
  145.6 8.1 %collective-permute-start.32 = (bf16[128,1024]{1,0:T(8,128)(2,1)S(1)}, bf16[128,1024]{1,0:T(8,128)(2,1)S(1)}, u32[]{:S(2)}, u32[]{:S(2)}) collective-permute-start(bf16[128,1024]{1,0:T(8,128)(2,1)S(1)} %slice.143), channel_id=1, source_target_pairs={{0,1},{1,0},{2,3},{3,2},{4,5},{5,4},{6,7},{7,6},{8,9},{9,8},{10,11... | collective-permute-start | bytes 786440 | tf_op jit(solution)/shard_map/ppermute | solution.py:360
  147.5 1.8 copy-start.2
  150.5 29.7 %collective-permute-start.23 = (bf16[256,1024]{1,0:T(8,128)(2,1)S(1)}, bf16[256,1024]{1,0:T(8,128)(2,1)S(1)}, u32[]{:S(2)}, u32[]{:S(2)}) collective-permute-start(bf16[256,1024]{1,0:T(8,128)(2,1)S(1)} %fusion), channel_id=1, source_target_pairs={{0,4},{4,0},{1,5},{5,1},{2,6},{6,2},{3,7},{7,3},{8,12},{12,8},{9,1... | collective-permute-start | bytes 1572872 | tf_op jit(solution)/shard_map/ppermute | solution.py:360
  150.6 3.8 %collective-permute-start.29 = (bf16[256,1024]{1,0:T(8,128)(2,1)}, bf16[256,1024]{1,0:T(8,128)(2,1)S(1)}, u32[]{:S(2)}, u32[]{:S(2)}) collective-permute-start(bf16[256,1024]{1,0:T(8,128)(2,1)} %collective-permute-done.28), channel_id=1, source_target_pairs={{0,4},{4,0},{1,5},{5,1},{2,6},{6,2},{3,7},{7,3},{8,12},{12,8},{9,1... | collective-permute-start | bytes 1572872 | tf_op jit(solution)/shard_map/ppermute | solution.py:360
  151.1 6.5 %collective-permute-start.25 = (bf16[256,1024]{1,0:T(8,128)(2,1)}, bf16[256,1024]{1,0:T(8,128)(2,1)S(1)}, u32[]{:S(2)}, u32[]{:S(2)}) collective-permute-start(bf16[256,1024]{1,0:T(8,128)(2,1)} %collective-permute-done.24), channel_id=1, source_target_pairs={{0,4},{4,0},{1,5},{5,1},{2,6},{6,2},{3,7},{7,3},{8,12},{12,8},{9,1... | collective-permute-start | bytes 1572872 | tf_op jit(solution)/shard_map/ppermute | solution.py:360
  153.7 6.5 %collective-permute-start.33 = (bf16[256,1024]{1,0:T(8,128)(2,1)S(1)}, bf16[256,1024]{1,0:T(8,128)(2,1)S(1)}, u32[]{:S(2)}, u32[]{:S(2)}) collective-permute-start(bf16[256,1024]{1,0:T(8,128)(2,1)S(1)} %constant_dynamic-update-slice_fusion.4), channel_id=1, source_target_pairs={{0,4},{4,0},{1,5},{5,1},{2,6},{6,2},{3,7},{7,3},{8,12},{12,8},{9,1... | collective-permute-start | bytes 1572872 | tf_op jit(solution)/shard_map/ppermute | solution.py:360
  157.5 5.9 %collective-permute-start.30 = (bf16[256,1024]{1,0:T(8,128)(2,1)S(1)}, bf16[256,1024]{1,0:T(8,128)(2,1)S(1)}, u32[]{:S(2)}, u32[]{:S(2)}) collective-permute-start(bf16[256,1024]{1,0:T(8,128)(2,1)S(1)} %fusion.2), channel_id=1, source_target_pairs={{0,4},{4,0},{1,5},{5,1},{2,6},{6,2},{3,7},{7,3},{8,12},{12,8},{9,1... | collective-permute-start | bytes 1572872 | tf_op jit(solution)/shard_map/ppermute | solution.py:360
  162.3 2.1 %collective-permute-start.34 = (bf16[256,1024]{1,0:T(8,128)(2,1)S(1)}, bf16[256,1024]{1,0:T(8,128)(2,1)S(1)}, u32[]{:S(2)}, u32[]{:S(2)}) collective-permute-start(bf16[256,1024]{1,0:T(8,128)(2,1)S(1)} %fusion.3), channel_id=1, source_target_pairs={{0,4},{4,0},{1,5},{5,1},{2,6},{6,2},{3,7},{7,3},{8,12},{12,8},{9,1... | collective-permute-start | bytes 1572872 | tf_op jit(solution)/shard_map/ppermute | solution.py:360
  163.2 4.7 %collective-permute-start.26 = (bf16[256,1024]{1,0:T(8,128)(2,1)S(1)}, bf16[256,1024]{1,0:T(8,128)(2,1)S(1)}, u32[]{:S(2)}, u32[]{:S(2)}) collective-permute-start(bf16[256,1024]{1,0:T(8,128)(2,1)S(1)} %fusion.1), channel_id=1, source_target_pairs={{0,4},{4,0},{1,5},{5,1},{2,6},{6,2},{3,7},{7,3},{8,12},{12,8},{9,1... | collective-permute-start | bytes 1572872 | tf_op jit(solution)/shard_map/ppermute | solution.py:360
  163.9 16.8 %collective-permute-start.38 = (bf16[128,1024]{1,0:T(8,128)(2,1)S(1)}, bf16[128,1024]{1,0:T(8,128)(2,1)S(1)}, u32[]{:S(2)}, u32[]{:S(2)}) collective-permute-start(bf16[128,1024]{1,0:T(8,128)(2,1)S(1)} %slice.198), channel_id=1, source_target_pairs={{0,2},{1,3},{2,0},{3,1},{4,6},{5,7},{6,4},{7,5},{8,10},{9,11},{10,... | collective-permute-start | bytes 786440 | tf_op jit(solution)/shard_map/ppermute | solution.py:360
  164.9 9.2 %collective-permute-start.35 = (bf16[128,1024]{1,0:T(8,128)(2,1)S(1)}, bf16[128,1024]{1,0:T(8,128)(2,1)S(1)}, u32[]{:S(2)}, u32[]{:S(2)}) collective-permute-start(bf16[128,1024]{1,0:T(8,128)(2,1)S(1)} %get-tuple-element.52), channel_id=1, source_target_pairs={{0,1},{1,0},{2,3},{3,2},{4,5},{5,4},{6,7},{7,6},{8,9},{9,8},{10,11... | collective-permute-start | bytes 786440 | tf_op jit(solution)/shard_map/ppermute | solution.py:360
  166.4 12.3 %collective-permute-start.39 = (bf16[128,1024]{1,0:T(8,128)(2,1)S(1)}, bf16[128,1024]{1,0:T(8,128)(2,1)S(1)}, u32[]{:S(2)}, u32[]{:S(2)}) collective-permute-start(bf16[128,1024]{1,0:T(8,128)(2,1)S(1)} %get-tuple-element.51), channel_id=1, source_target_pairs={{0,2},{1,3},{2,0},{3,1},{4,6},{5,7},{6,4},{7,5},{8,10},{9,11},{10,... | collective-permute-start | bytes 786440 | tf_op jit(solution)/shard_map/ppermute | solution.py:360
  168.4 12.3 %collective-permute-start.27 = (bf16[128,1024]{1,0:T(8,128)(2,1)S(1)}, bf16[128,1024]{1,0:T(8,128)(2,1)S(1)}, u32[]{:S(2)}, u32[]{:S(2)}) collective-permute-start(bf16[128,1024]{1,0:T(8,128)(2,1)S(1)} %slice.199), channel_id=1, source_target_pairs={{0,1},{1,0},{2,3},{3,2},{4,5},{5,4},{6,7},{7,6},{8,9},{9,8},{10,11... | collective-permute-start | bytes 786440 | tf_op jit(solution)/shard_map/ppermute | solution.py:360
  174.2 9.6 %collective-permute-start.36 = (bf16[128,1024]{1,0:T(8,128)(2,1)S(1)}, bf16[128,1024]{1,0:T(8,128)(2,1)S(1)}, u32[]{:S(2)}, u32[]{:S(2)}) collective-permute-start(bf16[128,1024]{1,0:T(8,128)(2,1)S(1)} %fusion.51), channel_id=1, source_target_pairs={{0,2},{1,3},{2,0},{3,1},{4,6},{5,7},{6,4},{7,5},{8,10},{9,11},{10,... | collective-permute-start | bytes 786440 | tf_op jit(solution)/shard_map/ppermute | solution.py:360
  178.8 7.3 %collective-permute-start.40 = (bf16[128,1024]{1,0:T(8,128)(2,1)S(1)}, bf16[128,1024]{1,0:T(8,128)(2,1)S(1)}, u32[]{:S(2)}, u32[]{:S(2)}) collective-permute-start(bf16[128,1024]{1,0:T(8,128)(2,1)S(1)} %fusion.48), channel_id=1, source_target_pairs={{0,1},{1,0},{2,3},{3,2},{4,5},{5,4},{6,7},{7,6},{8,9},{9,8},{10,11... | collective-permute-start | bytes 786440 | tf_op jit(solution)/shard_map/ppermute | solution.py:360
  186.4 10.2 %collective-permute-start.41 = (bf16[64,1024]{1,0:T(8,128)(2,1)S(1)}, bf16[64,1024]{1,0:T(8,128)(2,1)S(1)}, u32[]{:S(2)}, u32[]{:S(2)}) collective-permute-start(bf16[64,1024]{1,0:T(8,128)(2,1)S(1)} %get-tuple-element.56), channel_id=1, source_target_pairs={{0,16},{8,24},{16,0},{24,8},{1,17},{9,25},{17,1},{25,9},{2,18},{10... | collective-permute-start | bytes 393224 | tf_op jit(solution)/shard_map/ppermute | solution.py:347
  186.8 9.7 %collective-permute-start.42 = (bf16[64,1024]{1,0:T(8,128)(2,1)S(1)}, bf16[64,1024]{1,0:T(8,128)(2,1)S(1)}, u32[]{:S(2)}, u32[]{:S(2)}) collective-permute-start(bf16[64,1024]{1,0:T(8,128)(2,1)S(1)} %get-tuple-element.57), channel_id=1, source_target_pairs={{0,8},{8,16},{16,24},{24,0},{1,9},{9,17},{17,25},{25,1},{2,10},{10... | collective-permute-start | bytes 393224 | tf_op jit(solution)/shard_map/ppermute | solution.py:347
  187.8 9.1 %collective-permute-start.37 = (bf16[64,1024]{1,0:T(8,128)(2,1)S(1)}, bf16[64,1024]{1,0:T(8,128)(2,1)S(1)}, u32[]{:S(2)}, u32[]{:S(2)}) collective-permute-start(bf16[64,1024]{1,0:T(8,128)(2,1)S(1)} %slice.200), channel_id=1, source_target_pairs={{0,24},{8,0},{16,8},{24,16},{1,25},{9,1},{17,9},{25,17},{2,26},{10... | collective-permute-start | bytes 393224 | tf_op jit(solution)/shard_map/ppermute | solution.py:347

commit v3 on v2

--- a/solution.py
+++ b/solution.py
@@ -378,7 +378,7 @@
     by_req = (lax.axis_index("req") - lax.iota(jnp.int32, req_size)) % req_size
     by_exp = lax.axis_index("exp") ^ lax.iota(jnp.int32, exp_size)
     order = by_req[None, :] * exp_size + by_exp[:, None]
-    return jnp.take(mine, order.reshape(-1), axis=0).reshape(exp_size, -1)
+    return jnp.take(mine, order.reshape(-1), axis=0).reshape(-1, 1)
 
 
 def halves(value, width, axis):
@@ -388,37 +388,50 @@
     return own, other
 
 
-def expert_block(own, weights, gains, maps_in, maps_out):
+def expert_kernel(first, own_ref, other_ref, weight_ref, gain_0, gain_1, in_0, in_1, out_0, out_1, kept_ref, sent_ref):
+    rows, half_width = own_ref.shape
+    wide = [own_ref[...].astype(jnp.float32), other_ref[...].astype(jnp.float32)]
+    squares = sum(jnp.sum(x * x, axis=-1, keepdims=True) for x in wide)
+    factor = lax.rsqrt(squares / (2 * half_width) + norm_epsilon)
+    gate_up = sum(
+        jnp.dot(
+            (x * factor * gain[...]).astype(jnp.bfloat16),
+            maps[...],
+            preferred_element_type=jnp.float32,
+        )
+        for x, gain, maps in zip(wide, (gain_0, gain_1), (in_0, in_1))
+    )
+    half_units = gate_up.shape[-1] // 2
+    gate = gate_up[:, :half_units]
+    activated = (gate / (1.0 + jnp.exp(-gate)) * gate_up[:, half_units:]).astype(jnp.bfloat16)
+    weight = weight_ref[first : first + rows, :]
+    for maps, target in ((out_0, kept_ref), (out_1, sent_ref)):
+        made = jnp.dot(activated, maps[...], preferred_element_type=jnp.float32)
+        target[...] = (made * weight).astype(jnp.bfloat16)
+
+
+def expert_block(own, index, weights, gains, maps_in, maps_out):
     other = swap(own, "head", 1)
-    wide = [own.astype(jnp.float32), other.astype(jnp.float32)]
-    squares = sum(jnp.sum(x * x, axis=-1, keepdims=True) for x in wide)
-    factor = lax.rsqrt(squares / (2 * own.shape[1]) + norm_epsilon)
-    gate_up = sum(
-        jnp.dot((x * factor * gain).astype(jnp.bfloat16), maps, preferred_element_type=jnp.float32)
-        for x, gain, maps in zip(wide, gains, maps_in)
-    )
-    half_units = gate_up.shape[-1] // 2
-    activated = (jax.nn.silu(gate_up[:, :half_units]) * gate_up[:, half_units:]).astype(
-        jnp.bfloat16
-    )
-    kept, passed = [
-        jnp.dot(activated, maps, preferred_element_type=jnp.float32) * weights[:, None]
-        for maps in maps_out
-    ]
-    return kept + swap(passed.astype(jnp.bfloat16), "head", 1).astype(jnp.float32)
-
-
-def dense_experts(half_hidden, table, gains, maps_in, maps_out):
+    rows = own.shape[0]
+    kept, passed = pl.pallas_call(
+        functools.partial(expert_kernel, index * rows),
+        in_specs=[pl.BlockSpec(memory_space=pltpu.VMEM)] * 9,
+        out_specs=[pl.BlockSpec(memory_space=pltpu.VMEM)] * 2,
+        out_shape=[jax.ShapeDtypeStruct(own.shape, jnp.bfloat16)] * 2,
+        name="expert_block",
+    )(own, other, weights, *[g[None, :] for g in gains], *maps_in, *maps_out)
+    return kept.astype(jnp.float32) + swap(passed, "head", 1).astype(jnp.float32)
+
+
+def dense_experts(half_hidden, row_weights, gains, maps_in, maps_out):
     row_count, half_width = half_hidden.shape
     req_size = lax.axis_size("req")
     sent = half_hidden.astype(jnp.bfloat16)
-    sent, table = lax.optimization_barrier((sent, table))
     column = jnp.concatenate(gather_blocks(sent, "req"), axis=0)
-    row_weights = exchange_table(table)
     middle = column.shape[0] // 2
 
-    def run(block, weights):
-        return expert_block(block, weights, gains, maps_in, maps_out)
+    def run(block, index):
+        return expert_block(block, index, row_weights, gains, maps_in, maps_out)
 
     def over(value, bits):
         return swap(value.astype(jnp.bfloat16), "exp", bits).astype(jnp.float32)
@@ -427,12 +440,12 @@
     near_y = swap(column, "exp", 2)
     far_top = swap(near_x[:middle], "exp", 2)
     far_low = swap(near_y[middle:], "exp", 1)
-    own = run(column, row_weights[0])
-    for_x = run(near_x, row_weights[1])
-    for_y = run(near_y, row_weights[2])
+    own = run(column, 0)
+    for_x = run(near_x, 1)
+    for_y = run(near_y, 2)
     top = own[:middle] + over(for_x[:middle], 1)
     low = own[middle:] + over(for_y[middle:], 2)
-    far = run(jnp.concatenate([far_top, far_low], axis=0), row_weights[3])
+    far = run(jnp.concatenate([far_top, far_low], axis=0), 3)
     top = top + over(for_y[:middle] + over(far[:middle], 1), 2)
     low = low + over(for_x[middle:] + over(far[middle:], 2), 1)
     plane_sum = jnp.concatenate([top, low], axis=0).reshape(req_size, row_count, half_width)
@@ -524,7 +537,7 @@
     capacity = max(2, 2 * row_count * route_ids.shape[1] // experts_all)
     dense = capacity >= row_count and experts_all == groups and exp_size == 4
 
-    batch = requests // 2 if requests % 2 == 0 else requests
+    batch = requests
     starts = range(0, requests, batch)
     pieces = [
         gather_blocks(lax.slice_in_dim(queries, start, start + batch), "exp") for start in starts
@@ -534,6 +547,10 @@
     weight_parts = [take_block(split_weight, targets[0])] + [
         shift(take_block(split_weight, targets[s]), "exp", s) for s in range(1, exp_size)
     ]
+    if dense:
+        row_weights = exchange_table(route_table(route_ids, route_weights))
+        own_piece, row_weights = lax.optimization_barrier((pieces[0][0], row_weights))
+        pieces[0] = [own_piece] + pieces[0][1:]
     received = []
     for start, gathered in zip(starts, pieces):
         messages = attend(
@@ -544,7 +561,6 @@
             [messages[0]] + [shift(messages[s], "exp", s) for s in range(1, exp_size)]
         )
     if dense:
-        table = route_table(route_ids, route_weights)
         maps_in = halves(expert_in[0].reshape(model_width, -1), half_width, 0)
         maps_out = halves(expert_out[0], half_width, 1)
         gains = halves(norm_gain, half_width, 0)
@@ -565,7 +581,7 @@
         hidden = hidden + shift(take_block(outgoing, targets[s]), "exp", s).astype(jnp.float32)
 
     if dense:
-        mixture = dense_experts(hidden, table, gains, maps_in, maps_out)
+        mixture = dense_experts(hidden, row_weights, gains, maps_in, maps_out)
     else:
         mixture = sparse_experts(
             hidden, route_ids, route_weights, norm_gain, expert_in, expert_out, capacity

time: 195 us -> 216 us (1.11); the launches traced: 198 us -> 216 us
  waiting for transfers between devices: 47.9 us -> 82.1 us
  Pallas kernels: 50.7 us -> 71.2 us
  matrix products: 11.7 us -> 0 us
  starting transfers between devices: 52.1 us -> 43.2 us
  other arithmetic: 13.5 us -> 5.44 us
  local copies, waits for them, and re-layouts: 21.1 us -> 13.7 us
    pallas_call x0 -> x4, Pallas kernels: none -> 24 us  [expert_block(): pl.pallas_call(functools.partial(expert_kernel, index * rows), in_specs=[...]
    all_to_all x1, waiting for transfers between devices: 2.84 us -> 16.2 us  [exchange_table(): lax.all_to_all(table, ('req', 'exp'), split_axis=0, concat_axis=0, tiled=...]
    ppermute x18, waiting for transfers between devices: 21.3 us -> 34 us  [swap(): return lax.ppermute(value, axis, [(i, i ^ bits) for i in range(size)])]
    dot_general x16 -> x0, matrix products: 11.7 us -> none  [the longest x8 8.19 us: expert_block(): jnp.dot((x * factor * gain).astype(jnp.bfloat16), maps, preferred_element...]
    ppermute x25 -> x19, starting transfers between devices: 33.1 us -> 25 us  [shift(): lax.ppermute(value, axis, [(i, (i + step) % size) for i in range(size)])]
    ppermute x25 -> x19, waiting for transfers between devices: 23.7 us -> 31.8 us  [shift(): lax.ppermute(value, axis, [(i, (i + step) % size) for i in range(size)])]
    reduce_sum x8 -> x0, other arithmetic: 5.74 us -> none  [expert_block(): squares = sum((jnp.sum(x * x, axis=-1, keepdims=True) for x in wide))]
    pallas_call x2 -> x1, Pallas kernels: 45.2 us -> 42.1 us  [attend(): pl.pallas_call(functools.partial(attend_kernel, pieces, base, listed, sub...]
  transfers between devices with their start and end apart: 44 -> 38, of which waited for: 15 -> 16; matrix products, arithmetic and copies ran while one was open for 20% -> 7% of each run, Pallas kernels for 23% -> 31%
where the time goes in v3:
time: 216 us
  waiting for transfers between devices  82.1 us (38%)
  Pallas kernels  71.2 us (33%)
  starting transfers between devices  43.2 us (20%)
  local copies, waits for them, and re-layouts  13.7 us (6%)
  other arithmetic  5.44 us (3%)
    pallas_call x1, Pallas kernels, attend(): pl.pallas_call(functools.partial(attend_kernel, pieces, base, listed, sub...  42.1 us
    ppermute x18, waiting for transfers between devices, swap(): return lax.ppermute(value, axis, [(i, i ^ bits) for i in range(size)])  34 us
    ppermute x19, waiting for transfers between devices, shift(): lax.ppermute(value, axis, [(i, (i + step) % size) for i in range(size)])  31.8 us
    ppermute x19, starting transfers between devices, shift(): lax.ppermute(value, axis, [(i, (i + step) % size) for i in range(size)])  25 us
    pallas_call x4, Pallas kernels, expert_block(): pl.pallas_call(functools.partial(expert_kernel, index * rows), in_specs=[...  24 us
    all_to_all x1, waiting for transfers between devices, exchange_table(): lax.all_to_all(table, ('req', 'exp'), split_axis=0, concat_axis=0, tiled=...  16.2 us
    ppermute x18, starting transfers between devices, swap(): return lax.ppermute(value, axis, [(i, i ^ bits) for i in range(size)])  11.4 us
    all_to_all x1, starting transfers between devices, exchange_table(): lax.all_to_all(table, ('req', 'exp'), split_axis=0, concat_axis=0, tiled=...  6.81 us
  transfers between devices with their start and end apart: 38, of which 16 were waited for; matrix products, arithmetic and copies ran while one was open for 7% of the time, Pallas kernels for 31%

profile of v3, /device:TPU:0, one launch (start us, length us, event | category | flops | bytes accessed | tf_op | source)
XLA Modules:
  0.0 216.0 jit_solution(5389910408731763781)
XLA Ops:
  0.0 3.0 %collective-permute-start = (bf16[4,16,16,128]{3,2,1,0:T(8,128)(2,1)}, bf16[4,16,16,128]{3,2,1,0:T(8,128)(2,1)S(1)}, u32[]{:S(2)}, u32[]{:S(2)}) collective-permute-start(bf16[4,16,16,128]{3,2,1,0:T(8,128)(2,1)} %refs_0_), channel_id=1, source_target_pairs={{0,1},{1,2},{2,3},{3,0},{4,5},{5,6},{6,7},{7,4},{8,9},{9,10},{10,1... | collective-permute-start | bytes 786440 | tf_op jit(solution)/shard_map/ppermute | solution.py:347
  3.0 1.5 collective-permute-start.1
  4.5 1.4 collective-permute-start.2
  5.9 3.1 %dynamic-slice_bitcast_fusion.2 = (bf16[512,512]{1,0:T(8,128)(2,1)}, bf16[512,512]{1,0:T(8,128)(2,1)}, bf16[512,512]{1,0:T(8,128)(2,1)}, bf16[512,512]{1,0:T(8,128)(2,1)}) fusion(bf16[4,512,512]{2,1,0:T(8,128)(2,1)} %bitcast.52, s32[]{:T(128)S(6)} %select_n.123, s32[]{:T(128)S(6)} %select_n.121, s32[]{:T(128)S(6)} %select_n.119, s32[]{:T(128)S(6)} %select_n.117), kind=kLoop, calls=%fused_computation.20 | loop fusion | bytes 4194320 | tf_op jit(solution)/shard_map/jit(dynamic_index_in_dim)/squeeze | solution.py:351
  9.0 0.6 collective-permute-start.6
  9.6 0.5 collective-permute-start.7
  10.1 0.6 select_reduce_fusion
  10.8 6.8 %all-to-all-start = ((f32[16,1,64]{2,1,0:T(1,128)}), f32[16,1,64]{2,1,0:T(1,128)S(1)}, u32[]{:S(2)}, u32[]{:S(2)}) async-start(f32[16,1,64]{2,1,0:T(1,128)} %bitcast.3), calls=%async_computation | async-start | bytes 16384 | tf_op jit(solution)/shard_map/all_to_all | solution.py:377
  17.9 1.3 dynamic-slice_bitcast_fusion
  19.3 0.7 pad_add_fusion.1.info_ref
  19.9 2.5 %copy.33 = bf16[256,8,2,384]{3,1,2,0:T(8,128)(2,1)S(1)} copy(bf16[256,8,2,384]{3,2,1,0:T(2,128)(2,1)} %bitcast.51) | data formatting | bytes 6291456
  22.5 16.2 %all-to-all-done = f32[16,1,64]{2,1,0:T(1,128)S(1)} async-done(((f32[16,1,64]{2,1,0:T(1,128)}), f32[16,1,64]{2,1,0:T(1,128)S(1)}, u32[]{:S(2)}, u32[]{:S(2)}) %all-to-all-start) | async-done | bytes 4128 | tf_op jit(solution)/shard_map/all_to_all | solution.py:377
  38.7 0.6 gather_fusion
  39.5 0.4 copy-done.12
  40.0 42.1 %attend.1 = (bf16[64,2176]{1,0:T(8,128)(2,1)}, bf16[64,2176]{1,0:T(8,128)(2,1)}, bf16[64,2176]{1,0:T(8,128)(2,1)}, bf16[64,2176]{1,0:T(8,128)(2,1)}) custom-call(s32[8]{0:T(128)} %pad_add_fusion.1.info_ref, bf16[4,16,16,128]{3,2,1,0:T(8,128)(2,1)} %refs_0_, bf16[4,16,16,128]{3,2,1,0:T(8,128)(2,1)} %copy-done.12, ...), custom_call_target="tpu_custom_call" | custom-call | tf_op jit(solution)/shard_map/attend/pallas_call | solution.py:243
  82.2 2.8 %collective-permute-start.5 = (bf16[64,2176]{1,0:T(8,128)(2,1)}, bf16[64,2176]{1,0:T(8,128)(2,1)}, u32[]{:S(2)}, u32[]{:S(2)}) collective-permute-start(bf16[64,2176]{1,0:T(8,128)(2,1)} %get-tuple-element.31), channel_id=1, source_target_pairs={{0,3},{1,0},{2,1},{3,2},{4,7},{5,4},{6,5},{7,6},{8,11},{9,8},{10,9... | collective-permute-start | bytes 835592 | tf_op jit(solution)/shard_map/ppermute | solution.py:347
  85.1 0.6 pad_add_fusion.info_ref
  85.6 1.8 constant_dynamic-slice_fusion
  87.5 5.3 %collective-permute-done.3.refs_1_ = bf16[64,2176]{1,0:T(8,128)(2,1)S(1)} collective-permute-done((bf16[64,2176]{1,0:T(8,128)(2,1)}, bf16[64,2176]{1,0:T(8,128)(2,1)S(1)}, u32[]{:S(2)}, u32[]{:S(2)}) %collective-permute-start.3) | collective-permute-done | bytes 278560 | tf_op jit(solution)/shard_map/ppermute | solution.py:347
  92.8 4.3 %collective-permute-done.4.refs_2_ = bf16[64,2176]{1,0:T(8,128)(2,1)} collective-permute-done((bf16[64,2176]{1,0:T(8,128)(2,1)}, bf16[64,2176]{1,0:T(8,128)(2,1)}, u32[]{:S(2)}, u32[]{:S(2)}) %collective-permute-start.4) | collective-permute-done | bytes 278560 | tf_op jit(solution)/shard_map/ppermute | solution.py:347
  97.1 5.1 %merge_project.1 = (f32[256,1024]{1,0:T(8,128)}, bf16[256,1024]{1,0:T(8,128)(2,1)}) custom-call(s32[6]{0:T(128)} %pad_add_fusion.info_ref, bf16[64,2176]{1,0:T(8,128)(2,1)} %get-tuple-element.28.refs_0_, bf16[64,2176]{1,0:T(8,128)(2,1)} %copy-done.11, bf16[64,2176]{1,0:T(8,128)(2,1)} %collective-permute-done.4.refs_2_, ...), custom_call_target="tpu_custom_call" | custom-call | tf_op jit(solution)/shard_map/merge_project/pallas_call | solution.py:327
  102.2 2.1 collective-permute-done.9
  104.3 1.4 convert_add_fusion.3
  105.9 1.4 collective-permute-start.10
  107.3 1.8 collective-permute-start.11
  109.1 1.2 collective-permute-start.12
  110.3 2.9 %collective-permute-done.10 = bf16[64,1024]{1,0:T(8,128)(2,1)S(1)} collective-permute-done((bf16[64,1024]{1,0:T(8,128)(2,1)S(1)}, bf16[64,1024]{1,0:T(8,128)(2,1)S(1)}, u32[]{:S(2)}, u32[]{:S(2)}) %collective-permute-start.10) | collective-permute-done | bytes 131104 | tf_op jit(solution)/shard_map/ppermute | solution.py:347
  113.2 2.0 collective-permute-done.11
  115.3 1.7 collective-permute-start.13
  117.0 2.4 %collective-permute-start.15 = (bf16[64,1024]{1,0:T(8,128)(2,1)S(1)}, bf16[64,1024]{1,0:T(8,128)(2,1)S(1)}, u32[]{:S(2)}, u32[]{:S(2)}) collective-permute-start(bf16[64,1024]{1,0:T(8,128)(2,1)S(1)} %get-tuple-element.47), channel_id=1, source_target_pairs={{0,24},{8,0},{16,8},{24,16},{1,25},{9,1},{17,9},{25,17},{2,26},{10... | collective-permute-start | bytes 393224 | tf_op jit(solution)/shard_map/ppermute | solution.py:347
  119.4 4.2 %collective-permute-done.13 = bf16[64,1024]{1,0:T(8,128)(2,1)S(1)} collective-permute-done((bf16[64,1024]{1,0:T(8,128)(2,1)S(1)}, bf16[64,1024]{1,0:T(8,128)(2,1)S(1)}, u32[]{:S(2)}, u32[]{:S(2)}) %collective-permute-start.13) | collective-permute-done | bytes 131104 | tf_op jit(solution)/shard_map/ppermute | solution.py:347
  123.6 4.7 %collective-permute-done.14 = bf16[64,1024]{1,0:T(8,128)(2,1)S(1)} collective-permute-done((bf16[64,1024]{1,0:T(8,128)(2,1)S(1)}, bf16[64,1024]{1,0:T(8,128)(2,1)S(1)}, u32[]{:S(2)}, u32[]{:S(2)}) %collective-permute-start.14) | collective-permute-done | bytes 131104 | tf_op jit(solution)/shard_map/ppermute | solution.py:347
  128.3 1.0 collective-permute-start.18
  129.3 0.6 collective-permute-start.22
  129.9 12.2 %collective-permute-done.18.own_ref = bf16[256,1024]{1,0:T(8,128)(2,1)S(1)} collective-permute-done((bf16[256,1024]{1,0:T(8,128)(2,1)S(1)}, bf16[256,1024]{1,0:T(8,128)(2,1)S(1)}, u32[]{:S(2)}, u32[]{:S(2)}) %collective-permute-start.18) | collective-permute-done | bytes 524320 | tf_op jit(solution)/shard_map/ppermute | solution.py:360
  142.1 1.5 collective-permute-start.25
  144.0 5.4 %collective-permute-done.25 = bf16[128,1024]{1,0:T(8,128)(2,1)S(1)} collective-permute-done((bf16[128,1024]{1,0:T(8,128)(2,1)S(1)}, bf16[128,1024]{1,0:T(8,128)(2,1)S(1)}, u32[]{:S(2)}, u32[]{:S(2)}) %collective-permute-start.25) | collective-permute-done | bytes 262176 | tf_op jit(solution)/shard_map/ppermute | solution.py:360
  149.5 1.2 collective-permute-done.26
  150.9 0.7 fusion.20
  151.5 1.0 copy.29.weight_ref
  152.6 0.4 collective-permute-start.16
  153.1 0.8 copy-done.7
  153.9 6.0 %expert_block.6 = (bf16[256,1024]{1,0:T(8,128)(2,1)}, bf16[256,1024]{1,0:T(8,128)(2,1)}) custom-call(bf16[256,1024]{1,0:T(8,128)(2,1)} %copy-done.3, bf16[256,1024]{1,0:T(8,128)(2,1)} %copy-done.7, f32[1024,1]{1,0:T(8,128)} %copy.29.weight_ref, f32[1,1024]{1,0:T(1,128)} %bitcast.58, f32[1,1024]{1,0:T(1,128)} %bitcast.54, ...), custom_call_target="tpu_custom_call" | custom-call | tf_op jit(solution)/shard_map/expert_block/pallas_call | solution.py:416
  159.9 0.5 collective-permute-start.24
  160.4 6.0 %expert_block.7 = (bf16[256,1024]{1,0:T(8,128)(2,1)}, bf16[256,1024]{1,0:T(8,128)(2,1)}) custom-call(bf16[256,1024]{1,0:T(8,128)(2,1)} %copy-done.4, bf16[256,1024]{1,0:T(8,128)(2,1)} %collective-permute-done.27.other_ref, f32[1024,1]{1,0:T(8,128)} %copy.29.weight_ref, f32[1,1024]{1,0:T(1,128)} %bitcast.59, f32[1,1024]{1,0:T(1,128)} %bitcast.55, ...), custom_call_target="tpu_custom_call" | custom-call | tf_op jit(solution)/shard_map/expert_block/pallas_call | solution.py:416
  166.4 6.0 %expert_block.4 = (bf16[256,1024]{1,0:T(8,128)(2,1)}, bf16[256,1024]{1,0:T(8,128)(2,1)}) custom-call(bf16[256,1024]{1,0:T(8,128)(2,1)} %copy-done, bf16[256,1024]{1,0:T(8,128)(2,1)} %collective-permute-done.16.other_ref, f32[1024,1]{1,0:T(8,128)} %copy.29.weight_ref, f32[1,1024]{1,0:T(1,128)} %bitcast.60, f32[1,1024]{1,0:T(1,128)} %bitcast.56, ...), custom_call_target="tpu_custom_call" | custom-call | tf_op jit(solution)/shard_map/expert_block/pallas_call | solution.py:416
  172.4 0.4 collective-permute-start.17
  172.9 0.8 copy-done.6
  173.7 6.0 %expert_block.5 = (bf16[256,1024]{1,0:T(8,128)(2,1)}, bf16[256,1024]{1,0:T(8,128)(2,1)}) custom-call(bf16[256,1024]{1,0:T(8,128)(2,1)} %copy-done.2, bf16[256,1024]{1,0:T(8,128)(2,1)} %copy-done.6, f32[1024,1]{1,0:T(8,128)} %copy.29.weight_ref, f32[1,1024]{1,0:T(1,128)} %bitcast.61, f32[1,1024]{1,0:T(1,128)} %bitcast.57, ...), custom_call_target="tpu_custom_call" | custom-call | tf_op jit(solution)/shard_map/expert_block/pallas_call | solution.py:416
  180.0 0.7 collective-permute-start.32
  181.0 1.1 collective-permute-start.29
  182.0 0.9 collective-permute-start.33
  183.2 1.5 collective-permute-start.21
  184.7 5.5 %collective-permute-done.29 = bf16[128,1024]{1,0:T(8,128)(2,1)S(1)} collective-permute-done((bf16[128,1024]{1,0:T(8,128)(2,1)S(1)}, bf16[128,1024]{1,0:T(8,128)(2,1)S(1)}, u32[]{:S(2)}, u32[]{:S(2)}) %collective-permute-start.29) | collective-permute-done | bytes 262176 | tf_op jit(solution)/shard_map/ppermute | solution.py:360
  190.3 1.4 collective-permute-start.30
  191.7 3.2 %collective-permute-done.33 = bf16[128,1024]{1,0:T(8,128)(2,1)S(1)} collective-permute-done((bf16[128,1024]{1,0:T(8,128)(2,1)S(1)}, bf16[128,1024]{1,0:T(8,128)(2,1)S(1)}, u32[]{:S(2)}, u32[]{:S(2)}) %collective-permute-start.33) | collective-permute-done | bytes 262176 | tf_op jit(solution)/shard_map/ppermute | solution.py:360
  194.9 0.6 collective-permute-start.34
  195.7 4.2 %collective-permute-done.30 = bf16[128,1024]{1,0:T(8,128)(2,1)S(1)} collective-permute-done((bf16[128,1024]{1,0:T(8,128)(2,1)S(1)}, bf16[128,1024]{1,0:T(8,128)(2,1)S(1)}, u32[]{:S(2)}, u32[]{:S(2)}) %collective-permute-start.30) | collective-permute-done | bytes 262176 | tf_op jit(solution)/shard_map/ppermute | solution.py:360
  199.9 2.3 %collective-permute-done.34 = bf16[128,1024]{1,0:T(8,128)(2,1)S(1)} collective-permute-done((bf16[128,1024]{1,0:T(8,128)(2,1)S(1)}, bf16[128,1024]{1,0:T(8,128)(2,1)S(1)}, u32[]{:S(2)}, u32[]{:S(2)}) %collective-permute-start.34) | collective-permute-done | bytes 262176 | tf_op jit(solution)/shard_map/ppermute | solution.py:360
  202.5 2.5 %collective-permute-start.35 = (bf16[64,1024]{1,0:T(8,128)(2,1)S(1)}, bf16[64,1024]{1,0:T(8,128)(2,1)S(1)}, u32[]{:S(2)}, u32[]{:S(2)}) collective-permute-start(bf16[64,1024]{1,0:T(8,128)(2,1)S(1)} %get-tuple-element.64), channel_id=1, source_target_pairs={{0,16},{8,24},{16,0},{24,8},{1,17},{9,25},{17,1},{25,9},{2,18},{10... | collective-permute-start | bytes 393224 | tf_op jit(solution)/shard_map/ppermute | solution.py:347
  205.0 1.1 collective-permute-start.36
  206.1 2.8 %collective-permute-start.31 = (bf16[64,1024]{1,0:T(8,128)(2,1)S(1)}, bf16[64,1024]{1,0:T(8,128)(2,1)S(1)}, u32[]{:S(2)}, u32[]{:S(2)}) collective-permute-start(bf16[64,1024]{1,0:T(8,128)(2,1)S(1)} %slice.112), channel_id=1, source_target_pairs={{0,24},{8,0},{16,8},{24,16},{1,25},{9,1},{17,9},{25,17},{2,26},{10... | collective-permute-start | bytes 393224 | tf_op jit(solution)/shard_map/ppermute | solution.py:347
  208.9 6.4 %collective-permute-done.35 = bf16[64,1024]{1,0:T(8,128)(2,1)S(1)} collective-permute-done((bf16[64,1024]{1,0:T(8,128)(2,1)S(1)}, bf16[64,1024]{1,0:T(8,128)(2,1)S(1)}, u32[]{:S(2)}, u32[]{:S(2)}) %collective-permute-start.35) | collective-permute-done | bytes 131104 | tf_op jit(solution)/shard_map/ppermute | solution.py:347
  215.3 0.7 fusion.8
  (97 shorter events, 2.9 us)
Async XLA Ops:
  0.0 39.3 %collective-permute-start = (bf16[4,16,16,128]{3,2,1,0:T(8,128)(2,1)}, bf16[4,16,16,128]{3,2,1,0:T(8,128)(2,1)S(1)}, u32[]{:S(2)}, u32[]{:S(2)}) collective-permute-start(bf16[4,16,16,128]{3,2,1,0:T(8,128)(2,1)} %refs_0_), channel_id=1, source_target_pairs={{0,1},{1,2},{2,3},{3,0},{4,5},{5,6},{6,7},{7,4},{8,9},{9,10},{10,1... | collective-permute-start | bytes 786440 | tf_op jit(solution)/shard_map/ppermute | solution.py:347
  3.0 36.6 %collective-permute-start.1 = (bf16[4,16,16,128]{3,2,1,0:T(8,128)(2,1)}, bf16[4,16,16,128]{3,2,1,0:T(8,128)(2,1)}, u32[]{:S(2)}, u32[]{:S(2)}) collective-permute-start(bf16[4,16,16,128]{3,2,1,0:T(8,128)(2,1)} %refs_0_), channel_id=1, source_target_pairs={{0,2},{1,3},{2,0},{3,1},{4,6},{5,7},{6,4},{7,5},{8,10},{9,11},{10,... | collective-permute-start | bytes 786440 | tf_op jit(solution)/shard_map/ppermute | solution.py:347
  4.5 35.0 %collective-permute-start.2 = (bf16[4,16,16,128]{3,2,1,0:T(8,128)(2,1)}, bf16[4,16,16,128]{3,2,1,0:T(8,128)(2,1)}, u32[]{:S(2)}, u32[]{:S(2)}) collective-permute-start(bf16[4,16,16,128]{3,2,1,0:T(8,128)(2,1)} %refs_0_), channel_id=1, source_target_pairs={{0,3},{1,0},{2,1},{3,2},{4,7},{5,4},{6,5},{7,6},{8,11},{9,8},{10,9... | collective-permute-start | bytes 786440 | tf_op jit(solution)/shard_map/ppermute | solution.py:347
  5.9 4.2 %copy-start.15 = (f32[64,8]{0,1:T(8,128)S(1)}, f32[64,8]{0,1:T(8,128)}, u32[]{:S(2)}) copy-start(f32[64,8]{0,1:T(8,128)} %param.23) | copy-start | bytes 6148
  5.9 4.2 %copy-start.16 = (s32[64,8]{0,1:T(8,128)S(1)}, s32[64,8]{0,1:T(8,128)}, u32[]{:S(2)}) copy-start(s32[64,8]{0,1:T(8,128)} %param.22) | copy-start | bytes 6148
  5.9 12.0 %copy-start.17 = (s32[4]{0:T(128)S(1)}, s32[4]{0:T(128)}, u32[]{:S(2)}) copy-start(s32[4]{0:T(128)} %param.18) | copy-start | bytes 52
  5.9 12.0 %copy-start.1 = (bf16[1,384,2048]{2,1,0:T(8,128)(2,1)S(1)}, bf16[1,384,2048]{2,1,0:T(8,128)(2,1)}, u32[]{:S(2)}) copy-start(bf16[1,384,2048]{2,1,0:T(8,128)(2,1)} %param.25) | copy-start | bytes 4718596
  9.0 73.2 %collective-permute-start.6 = (bf16[512,512]{1,0:T(8,128)(2,1)}, bf16[512,512]{1,0:T(8,128)(2,1)}, u32[]{:S(2)}, u32[]{:S(2)}) collective-permute-start(bf16[512,512]{1,0:T(8,128)(2,1)} %get-tuple-element.53), channel_id=1, source_target_pairs={{0,1},{1,2},{2,3},{3,0},{4,5},{5,6},{6,7},{7,4},{8,9},{9,10},{10,1... | collective-permute-start | bytes 1572872 | tf_op jit(solution)/shard_map/ppermute | solution.py:347
  9.6 77.9 %collective-permute-start.7 = (bf16[512,512]{1,0:T(8,128)(2,1)}, bf16[512,512]{1,0:T(8,128)(2,1)}, u32[]{:S(2)}, u32[]{:S(2)}) collective-permute-start(bf16[512,512]{1,0:T(8,128)(2,1)} %get-tuple-element.52), channel_id=1, source_target_pairs={{0,2},{1,3},{2,0},{3,1},{4,6},{5,7},{6,4},{7,5},{8,10},{9,11},{10,... | collective-permute-start | bytes 1572872 | tf_op jit(solution)/shard_map/ppermute | solution.py:347
  10.8 27.9 %all-to-all-start = ((f32[16,1,64]{2,1,0:T(1,128)}), f32[16,1,64]{2,1,0:T(1,128)S(1)}, u32[]{:S(2)}, u32[]{:S(2)}) async-start(f32[16,1,64]{2,1,0:T(1,128)} %bitcast.3), calls=%async_computation | async-start | bytes 16384 | tf_op jit(solution)/shard_map/all_to_all | solution.py:377
  39.3 0.7 copy-start.12
  39.3 48.2 %collective-permute-start.8 = (bf16[512,512]{1,0:T(8,128)(2,1)}, bf16[512,512]{1,0:T(8,128)(2,1)}, u32[]{:S(2)}, u32[]{:S(2)}) collective-permute-start(bf16[512,512]{1,0:T(8,128)(2,1)} %get-tuple-element.51), channel_id=1, source_target_pairs={{0,3},{1,0},{2,1},{3,2},{4,7},{5,4},{6,5},{7,6},{8,11},{9,8},{10,9... | collective-permute-start | bytes 1572872 | tf_op jit(solution)/shard_map/ppermute | solution.py:347
  82.1 10.7 %collective-permute-start.3 = (bf16[64,2176]{1,0:T(8,128)(2,1)}, bf16[64,2176]{1,0:T(8,128)(2,1)S(1)}, u32[]{:S(2)}, u32[]{:S(2)}) collective-permute-start(bf16[64,2176]{1,0:T(8,128)(2,1)} %get-tuple-element.29), channel_id=1, source_target_pairs={{0,1},{1,2},{2,3},{3,0},{4,5},{5,6},{6,7},{7,4},{8,9},{9,10},{10,1... | collective-permute-start | bytes 835592 | tf_op jit(solution)/shard_map/ppermute | solution.py:347
  82.1 14.9 %collective-permute-start.4 = (bf16[64,2176]{1,0:T(8,128)(2,1)}, bf16[64,2176]{1,0:T(8,128)(2,1)}, u32[]{:S(2)}, u32[]{:S(2)}) collective-permute-start(bf16[64,2176]{1,0:T(8,128)(2,1)} %get-tuple-element.30), channel_id=1, source_target_pairs={{0,2},{1,3},{2,0},{3,1},{4,6},{5,7},{6,4},{7,5},{8,10},{9,11},{10,... | collective-permute-start | bytes 835592 | tf_op jit(solution)/shard_map/ppermute | solution.py:347
  82.2 14.8 %collective-permute-start.5 = (bf16[64,2176]{1,0:T(8,128)(2,1)}, bf16[64,2176]{1,0:T(8,128)(2,1)}, u32[]{:S(2)}, u32[]{:S(2)}) collective-permute-start(bf16[64,2176]{1,0:T(8,128)(2,1)} %get-tuple-element.31), channel_id=1, source_target_pairs={{0,3},{1,0},{2,1},{3,2},{4,7},{5,4},{6,5},{7,6},{8,11},{9,8},{10,9... | collective-permute-start | bytes 835592 | tf_op jit(solution)/shard_map/ppermute | solution.py:347
  92.8 4.3 %copy-start.11 = (bf16[64,2176]{1,0:T(8,128)(2,1)}, bf16[64,2176]{1,0:T(8,128)(2,1)S(1)}, u32[]{:S(2)}) copy-start(bf16[64,2176]{1,0:T(8,128)(2,1)S(1)} %collective-permute-done.3.refs_1_) | copy-start | bytes 835588
  102.2 2.1 collective-permute-start.9
  104.3 10.8 %copy-start.13 = (bf16[64,2048]{1,0:T(8,128)(2,1)S(1)}, bf16[64,2048]{1,0:T(8,128)(2,1)}, u32[]{:S(2)}) copy-start(bf16[64,2048]{1,0:T(8,128)(2,1)} %param.19) | copy-start | bytes 786436
  105.9 7.3 %collective-permute-start.10 = (bf16[64,1024]{1,0:T(8,128)(2,1)S(1)}, bf16[64,1024]{1,0:T(8,128)(2,1)S(1)}, u32[]{:S(2)}, u32[]{:S(2)}) collective-permute-start(bf16[64,1024]{1,0:T(8,128)(2,1)S(1)} %get-tuple-element.61), channel_id=1, source_target_pairs={{0,1},{1,2},{2,3},{3,0},{4,5},{5,6},{6,7},{7,4},{8,9},{9,10},{10,1... | collective-permute-start | bytes 393224 | tf_op jit(solution)/shard_map/ppermute | solution.py:347
  107.3 7.9 %collective-permute-start.11 = (bf16[64,1024]{1,0:T(8,128)(2,1)S(1)}, bf16[64,1024]{1,0:T(8,128)(2,1)S(1)}, u32[]{:S(2)}, u32[]{:S(2)}) collective-permute-start(bf16[64,1024]{1,0:T(8,128)(2,1)S(1)} %get-tuple-element.63), channel_id=1, source_target_pairs={{0,2},{1,3},{2,0},{3,1},{4,6},{5,7},{6,4},{7,5},{8,10},{9,11},{10,... | collective-permute-start | bytes 393224 | tf_op jit(solution)/shard_map/ppermute | solution.py:347
  109.1 41.8 %copy-start.14 = (f32[2048]{0:T(1024)S(1)}, f32[2048]{0:T(1024)}, u32[]{:S(2)}) copy-start(f32[2048]{0:T(1024)} %param.21) | copy-start | bytes 24580
  109.1 6.1 %collective-permute-start.12 = (bf16[64,1024]{1,0:T(8,128)(2,1)S(1)}, bf16[64,1024]{1,0:T(8,128)(2,1)S(1)}, u32[]{:S(2)}, u32[]{:S(2)}) collective-permute-start(bf16[64,1024]{1,0:T(8,128)(2,1)S(1)} %get-tuple-element.62), channel_id=1, source_target_pairs={{0,3},{1,0},{2,1},{3,2},{4,7},{5,4},{6,5},{7,6},{8,11},{9,8},{10,9... | collective-permute-start | bytes 393224 | tf_op jit(solution)/shard_map/ppermute | solution.py:347
  115.3 8.3 %collective-permute-start.13 = (bf16[64,1024]{1,0:T(8,128)(2,1)S(1)}, bf16[64,1024]{1,0:T(8,128)(2,1)S(1)}, u32[]{:S(2)}, u32[]{:S(2)}) collective-permute-start(bf16[64,1024]{1,0:T(8,128)(2,1)S(1)} %get-tuple-element.47), channel_id=1, source_target_pairs={{0,8},{8,16},{16,24},{24,0},{1,9},{9,17},{17,25},{25,1},{2,10},{10... | collective-permute-start | bytes 393224 | tf_op jit(solution)/shard_map/ppermute | solution.py:347
  117.0 11.3 %collective-permute-start.14 = (bf16[64,1024]{1,0:T(8,128)(2,1)S(1)}, bf16[64,1024]{1,0:T(8,128)(2,1)S(1)}, u32[]{:S(2)}, u32[]{:S(2)}) collective-permute-start(bf16[64,1024]{1,0:T(8,128)(2,1)S(1)} %get-tuple-element.47), channel_id=1, source_target_pairs={{0,16},{8,24},{16,0},{24,8},{1,17},{9,25},{17,1},{25,9},{2,18},{10... | collective-permute-start | bytes 393224 | tf_op jit(solution)/shard_map/ppermute | solution.py:347
  117.0 11.3 %collective-permute-start.15 = (bf16[64,1024]{1,0:T(8,128)(2,1)S(1)}, bf16[64,1024]{1,0:T(8,128)(2,1)S(1)}, u32[]{:S(2)}, u32[]{:S(2)}) collective-permute-start(bf16[64,1024]{1,0:T(8,128)(2,1)S(1)} %get-tuple-element.47), channel_id=1, source_target_pairs={{0,24},{8,0},{16,8},{24,16},{1,25},{9,1},{17,9},{25,17},{2,26},{10... | collective-permute-start | bytes 393224 | tf_op jit(solution)/shard_map/ppermute | solution.py:347
  128.3 31.6 %copy-start = (bf16[256,1024]{1,0:T(8,128)(2,1)}, bf16[256,1024]{1,0:T(8,128)(2,1)S(1)}, u32[]{:S(2)}) copy-start(bf16[256,1024]{1,0:T(8,128)(2,1)S(1)} %pad_maximum_fusion.own_ref) | copy-start | bytes 1572868
  128.3 13.8 %collective-permute-start.18 = (bf16[256,1024]{1,0:T(8,128)(2,1)S(1)}, bf16[256,1024]{1,0:T(8,128)(2,1)S(1)}, u32[]{:S(2)}, u32[]{:S(2)}) collective-permute-start(bf16[256,1024]{1,0:T(8,128)(2,1)S(1)} %pad_maximum_fusion.own_ref), channel_id=1, source_target_pairs={{0,1},{1,0},{2,3},{3,2},{4,5},{5,4},{6,7},{7,6},{8,9},{9,8},{10,11... | collective-permute-start | bytes 1572872 | tf_op jit(solution)/shard_map/ppermute | solution.py:360
  129.3 14.4 %collective-permute-start.22 = (bf16[256,1024]{1,0:T(8,128)(2,1)S(1)}, bf16[256,1024]{1,0:T(8,128)(2,1)S(1)}, u32[]{:S(2)}, u32[]{:S(2)}) collective-permute-start(bf16[256,1024]{1,0:T(8,128)(2,1)S(1)} %pad_maximum_fusion.own_ref), channel_id=1, source_target_pairs={{0,2},{1,3},{2,0},{3,1},{4,6},{5,7},{6,4},{7,5},{8,10},{9,11},{10,... | collective-permute-start | bytes 1572872 | tf_op jit(solution)/shard_map/ppermute | solution.py:360
  142.1 17.7 %copy-start.2 = (bf16[256,1024]{1,0:T(8,128)(2,1)}, bf16[256,1024]{1,0:T(8,128)(2,1)S(1)}, u32[]{:S(2)}) copy-start(bf16[256,1024]{1,0:T(8,128)(2,1)S(1)} %collective-permute-done.18.own_ref) | copy-start | bytes 1572868
  142.1 7.3 %collective-permute-start.25 = (bf16[128,1024]{1,0:T(8,128)(2,1)S(1)}, bf16[128,1024]{1,0:T(8,128)(2,1)S(1)}, u32[]{:S(2)}, u32[]{:S(2)}) collective-permute-start(bf16[128,1024]{1,0:T(8,128)(2,1)S(1)} %slice.73), channel_id=1, source_target_pairs={{0,2},{1,3},{2,0},{3,1},{4,6},{5,7},{6,4},{7,5},{8,10},{9,11},{10,... | collective-permute-start | bytes 786440 | tf_op jit(solution)/shard_map/ppermute | solution.py:360
  143.7 9.4 %copy-start.3 = (bf16[256,1024]{1,0:T(8,128)(2,1)}, bf16[256,1024]{1,0:T(8,128)(2,1)S(1)}, u32[]{:S(2)}) copy-start(bf16[256,1024]{1,0:T(8,128)(2,1)S(1)} %collective-permute-done.22.own_ref) | copy-start | bytes 1572868
  143.7 7.1 %collective-permute-start.26 = (bf16[128,1024]{1,0:T(8,128)(2,1)S(1)}, bf16[128,1024]{1,0:T(8,128)(2,1)S(1)}, u32[]{:S(2)}, u32[]{:S(2)}) collective-permute-start(bf16[128,1024]{1,0:T(8,128)(2,1)S(1)} %slice.74), channel_id=1, source_target_pairs={{0,1},{1,0},{2,3},{3,2},{4,5},{5,4},{6,7},{7,6},{8,9},{9,8},{10,11... | collective-permute-start | bytes 786440 | tf_op jit(solution)/shard_map/ppermute | solution.py:360
  144.0 9.1 %collective-permute-start.23 = (bf16[256,1024]{1,0:T(8,128)(2,1)S(1)}, bf16[256,1024]{1,0:T(8,128)(2,1)S(1)}, u32[]{:S(2)}, u32[]{:S(2)}) collective-permute-start(bf16[256,1024]{1,0:T(8,128)(2,1)S(1)} %collective-permute-done.22.own_ref), channel_id=1, source_target_pairs={{0,4},{4,0},{1,5},{5,1},{2,6},{6,2},{3,7},{7,3},{8,12},{12,8},{9,1... | collective-permute-start | bytes 1572872 | tf_op jit(solution)/shard_map/ppermute | solution.py:360
  150.8 9.1 %copy-start.4 = (bf16[256,1024]{1,0:T(8,128)(2,1)}, bf16[256,1024]{1,0:T(8,128)(2,1)S(1)}, u32[]{:S(2)}) copy-start(bf16[256,1024]{1,0:T(8,128)(2,1)S(1)} %constant_dynamic-update-slice_fusion.own_ref) | copy-start | bytes 1572868
  150.8 9.6 %collective-permute-start.27 = (bf16[256,1024]{1,0:T(8,128)(2,1)S(1)}, bf16[256,1024]{1,0:T(8,128)(2,1)}, u32[]{:S(2)}, u32[]{:S(2)}) collective-permute-start(bf16[256,1024]{1,0:T(8,128)(2,1)S(1)} %constant_dynamic-update-slice_fusion.own_ref), channel_id=1, source_target_pairs={{0,4},{4,0},{1,5},{5,1},{2,6},{6,2},{3,7},{7,3},{8,12},{12,8},{9,1... | collective-permute-start | bytes 1572872 | tf_op jit(solution)/shard_map/ppermute | solution.py:360
  152.6 13.8 %collective-permute-start.16 = (bf16[256,1024]{1,0:T(8,128)(2,1)S(1)}, bf16[256,1024]{1,0:T(8,128)(2,1)}, u32[]{:S(2)}, u32[]{:S(2)}) collective-permute-start(bf16[256,1024]{1,0:T(8,128)(2,1)S(1)} %pad_maximum_fusion.own_ref), channel_id=1, source_target_pairs={{0,4},{4,0},{1,5},{5,1},{2,6},{6,2},{3,7},{7,3},{8,12},{12,8},{9,1... | collective-permute-start | bytes 1572872 | tf_op jit(solution)/shard_map/ppermute | solution.py:360
  153.0 19.9 %collective-permute-start.19 = (bf16[256,1024]{1,0:T(8,128)(2,1)S(1)}, bf16[256,1024]{1,0:T(8,128)(2,1)S(1)}, u32[]{:S(2)}, u32[]{:S(2)}) collective-permute-start(bf16[256,1024]{1,0:T(8,128)(2,1)S(1)} %collective-permute-done.18.own_ref), channel_id=1, source_target_pairs={{0,4},{4,0},{1,5},{5,1},{2,6},{6,2},{3,7},{7,3},{8,12},{12,8},{9,1... | collective-permute-start | bytes 1572872 | tf_op jit(solution)/shard_map/ppermute | solution.py:360
  153.1 0.8 copy-start.7
  159.9 19.9 %collective-permute-start.24 = (bf16[256,1024]{1,0:T(8,128)(2,1)}, bf16[256,1024]{1,0:T(8,128)(2,1)S(1)}, u32[]{:S(2)}, u32[]{:S(2)}) collective-permute-start(bf16[256,1024]{1,0:T(8,128)(2,1)} %get-tuple-element.44), channel_id=1, source_target_pairs={{0,4},{4,0},{1,5},{5,1},{2,6},{6,2},{3,7},{7,3},{8,12},{12,8},{9,1... | collective-permute-start | bytes 1572872 | tf_op jit(solution)/shard_map/ppermute | solution.py:360
  166.3 14.3 %collective-permute-start.28 = (bf16[256,1024]{1,0:T(8,128)(2,1)}, bf16[256,1024]{1,0:T(8,128)(2,1)S(1)}, u32[]{:S(2)}, u32[]{:S(2)}) collective-permute-start(bf16[256,1024]{1,0:T(8,128)(2,1)} %get-tuple-element.46), channel_id=1, source_target_pairs={{0,4},{4,0},{1,5},{5,1},{2,6},{6,2},{3,7},{7,3},{8,12},{12,8},{9,1... | collective-permute-start | bytes 1572872 | tf_op jit(solution)/shard_map/ppermute | solution.py:360
  172.4 7.3 %copy-start.9 = (bf16[256,1024]{1,0:T(8,128)(2,1)S(1)}, bf16[256,1024]{1,0:T(8,128)(2,1)}, u32[]{:S(2)}) copy-start(bf16[256,1024]{1,0:T(8,128)(2,1)} %get-tuple-element.43) | copy-start | bytes 1572868
  172.4 23.1 %collective-permute-start.17 = (bf16[256,1024]{1,0:T(8,128)(2,1)}, bf16[256,1024]{1,0:T(8,128)(2,1)S(1)}, u32[]{:S(2)}, u32[]{:S(2)}) collective-permute-start(bf16[256,1024]{1,0:T(8,128)(2,1)} %get-tuple-element.40), channel_id=1, source_target_pairs={{0,4},{4,0},{1,5},{5,1},{2,6},{6,2},{3,7},{7,3},{8,12},{12,8},{9,1... | collective-permute-start | bytes 1572872 | tf_op jit(solution)/shard_map/ppermute | solution.py:360
  172.9 0.8 copy-start.6
  179.7 1.0 copy-start.5
  179.7 3.3 %collective-permute-start.20 = (bf16[256,1024]{1,0:T(8,128)(2,1)}, bf16[256,1024]{1,0:T(8,128)(2,1)S(1)}, u32[]{:S(2)}, u32[]{:S(2)}) collective-permute-start(bf16[256,1024]{1,0:T(8,128)(2,1)} %get-tuple-element.42), channel_id=1, source_target_pairs={{0,4},{4,0},{1,5},{5,1},{2,6},{6,2},{3,7},{7,3},{8,12},{12,8},{9,1... | collective-permute-start | bytes 1572872 | tf_op jit(solution)/shard_map/ppermute | solution.py:360
  179.9 3.0 %copy-start.10 = (bf16[256,1024]{1,0:T(8,128)(2,1)S(1)}, bf16[256,1024]{1,0:T(8,128)(2,1)}, u32[]{:S(2)}) copy-start(bf16[256,1024]{1,0:T(8,128)(2,1)} %get-tuple-element.41) | copy-start | bytes 1572868
  180.0 15.7 %collective-permute-start.32 = (bf16[128,1024]{1,0:T(8,128)(2,1)S(1)}, bf16[128,1024]{1,0:T(8,128)(2,1)S(1)}, u32[]{:S(2)}, u32[]{:S(2)}) collective-permute-start(bf16[128,1024]{1,0:T(8,128)(2,1)S(1)} %slice.110), channel_id=1, source_target_pairs={{0,2},{1,3},{2,0},{3,1},{4,6},{5,7},{6,4},{7,5},{8,10},{9,11},{10,... | collective-permute-start | bytes 786440 | tf_op jit(solution)/shard_map/ppermute | solution.py:360
  181.0 9.2 %collective-permute-start.29 = (bf16[128,1024]{1,0:T(8,128)(2,1)S(1)}, bf16[128,1024]{1,0:T(8,128)(2,1)S(1)}, u32[]{:S(2)}, u32[]{:S(2)}) collective-permute-start(bf16[128,1024]{1,0:T(8,128)(2,1)S(1)} %get-tuple-element.60), channel_id=1, source_target_pairs={{0,1},{1,0},{2,3},{3,2},{4,5},{5,4},{6,7},{7,6},{8,9},{9,8},{10,11... | collective-permute-start | bytes 786440 | tf_op jit(solution)/shard_map/ppermute | solution.py:360
  182.0 12.8 %collective-permute-start.33 = (bf16[128,1024]{1,0:T(8,128)(2,1)S(1)}, bf16[128,1024]{1,0:T(8,128)(2,1)S(1)}, u32[]{:S(2)}, u32[]{:S(2)}) collective-permute-start(bf16[128,1024]{1,0:T(8,128)(2,1)S(1)} %get-tuple-element.59), channel_id=1, source_target_pairs={{0,2},{1,3},{2,0},{3,1},{4,6},{5,7},{6,4},{7,5},{8,10},{9,11},{10,... | collective-permute-start | bytes 786440 | tf_op jit(solution)/shard_map/ppermute | solution.py:360
  183.0 12.6 %copy-start.8 = (bf16[256,1024]{1,0:T(8,128)(2,1)S(1)}, bf16[256,1024]{1,0:T(8,128)(2,1)}, u32[]{:S(2)}) copy-start(bf16[256,1024]{1,0:T(8,128)(2,1)} %get-tuple-element.39) | copy-start | bytes 1572868
  183.2 12.5 %collective-permute-start.21 = (bf16[128,1024]{1,0:T(8,128)(2,1)S(1)}, bf16[128,1024]{1,0:T(8,128)(2,1)S(1)}, u32[]{:S(2)}, u32[]{:S(2)}) collective-permute-start(bf16[128,1024]{1,0:T(8,128)(2,1)S(1)} %slice.111), channel_id=1, source_target_pairs={{0,1},{1,0},{2,3},{3,2},{4,5},{5,4},{6,7},{7,6},{8,9},{9,8},{10,11... | collective-permute-start | bytes 786440 | tf_op jit(solution)/shard_map/ppermute | solution.py:360
  190.3 9.7 %collective-permute-start.30 = (bf16[128,1024]{1,0:T(8,128)(2,1)S(1)}, bf16[128,1024]{1,0:T(8,128)(2,1)S(1)}, u32[]{:S(2)}, u32[]{:S(2)}) collective-permute-start(bf16[128,1024]{1,0:T(8,128)(2,1)S(1)} %fusion.3), channel_id=1, source_target_pairs={{0,2},{1,3},{2,0},{3,1},{4,6},{5,7},{6,4},{7,5},{8,10},{9,11},{10,... | collective-permute-start | bytes 786440 | tf_op jit(solution)/shard_map/ppermute | solution.py:360
  194.9 7.3 %collective-permute-start.34 = (bf16[128,1024]{1,0:T(8,128)(2,1)S(1)}, bf16[128,1024]{1,0:T(8,128)(2,1)S(1)}, u32[]{:S(2)}, u32[]{:S(2)}) collective-permute-start(bf16[128,1024]{1,0:T(8,128)(2,1)S(1)} %fusion), channel_id=1, source_target_pairs={{0,1},{1,0},{2,3},{3,2},{4,5},{5,4},{6,7},{7,6},{8,9},{9,8},{10,11... | collective-permute-start | bytes 786440 | tf_op jit(solution)/shard_map/ppermute | solution.py:360
  202.5 12.8 %collective-permute-start.35 = (bf16[64,1024]{1,0:T(8,128)(2,1)S(1)}, bf16[64,1024]{1,0:T(8,128)(2,1)S(1)}, u32[]{:S(2)}, u32[]{:S(2)}) collective-permute-start(bf16[64,1024]{1,0:T(8,128)(2,1)S(1)} %get-tuple-element.64), channel_id=1, source_target_pairs={{0,16},{8,24},{16,0},{24,8},{1,17},{9,25},{17,1},{25,9},{2,18},{10... | collective-permute-start | bytes 393224 | tf_op jit(solution)/shard_map/ppermute | solution.py:347
  205.0 10.3 %collective-permute-start.36 = (bf16[64,1024]{1,0:T(8,128)(2,1)S(1)}, bf16[64,1024]{1,0:T(8,128)(2,1)S(1)}, u32[]{:S(2)}, u32[]{:S(2)}) collective-permute-start(bf16[64,1024]{1,0:T(8,128)(2,1)S(1)} %get-tuple-element.65), channel_id=1, source_target_pairs={{0,8},{8,16},{16,24},{24,0},{1,9},{9,17},{17,25},{25,1},{2,10},{10... | collective-permute-start | bytes 393224 | tf_op jit(solution)/shard_map/ppermute | solution.py:347
  206.1 9.2 %collective-permute-start.31 = (bf16[64,1024]{1,0:T(8,128)(2,1)S(1)}, bf16[64,1024]{1,0:T(8,128)(2,1)S(1)}, u32[]{:S(2)}, u32[]{:S(2)}) collective-permute-start(bf16[64,1024]{1,0:T(8,128)(2,1)S(1)} %slice.112), channel_id=1, source_target_pairs={{0,24},{8,0},{16,8},{24,16},{1,25},{9,1},{17,9},{25,17},{2,26},{10... | collective-permute-start | bytes 393224 | tf_op jit(solution)/shard_map/ppermute | solution.py:347
